TPU v7x, 128 devices: a whole 4x4x4 slice. The times are simulated.
128 devices in a mesh: gz: 16 (over y, z), gy: 8 (over x, core).
Axes of the slice: x: 4, y: 4, z: 4, core: 2. Of those that a mesh axis runs over, the one named last changes fastest.
Arguments:
- patch_force: float32 [16384, 24, 128], P(('gz', 'gy')), may hold values from -36 to 36
- patch_owner: int32 [16384], P(('gz', 'gy')), may hold values from 0 to 127, as said below
- patch_voxel: int32 [16384, 128], P(('gz', 'gy')), may hold values from 0 to 16383
- patch_live: int32 [16384, 8], P(('gz', 'gy')), may hold values from 64 to 128
- voxel_mask: int32 [128, 64, 256], P('gz', 'gy'), may hold values 0 or 1
- element_matrix: float32 [24, 24], replicated, may hold values from -0.2 to 6.5, as said below
Outputs:
- displacement: float32 [24, 128, 64, 256], P(None, 'gz', 'gy')
- residual: float32 [24, 128, 64, 256], P(None, 'gz', 'gy')
Inputs may be any that keep to these rules, and one draw needn't show every extreme that they name: `patch_owner`: within the 128 patch blocks of one device no owner appears more than 2 times, and in every device's blocks some owner appears exactly 2 times. `element_matrix`: symmetric positive definite.
All inputs are finite; a program needn't handle non-finite values. No bound on the sum of `voxel_mask` on one device may be relied on, other than what follows from the above.
Results may differ from a plain program's by a relative error of at most 0.00029.
Values sent between devices are 32-bit elements; how exact they have to be, the bound alone decides.
No kernel may reach another device: no remote copies, remote signals or barrier semaphores. Data moves between devices by JAX's collectives and lax.ppermute only.
A program may use at most 128 MiB of HBM per device.

v0:
```python
import jax
import jax.numpy as jnp
from jax import lax
from jax.sharding import PartitionSpec as P

LOADS = 8
ITERS = 2


spring = 0.5
highest = lax.Precision.HIGHEST


def padded_2(block, sides, width):
    for axis, dim in sides:
        count = lax.axis_size(axis)
        forward = [(i, i + 1) for i in range(count - 1)]
        backward = [(target, source) for source, target in forward]
        low = lax.ppermute(
            lax.slice_in_dim(block, block.shape[dim] - width, None, axis=dim), axis, forward
        )
        high = lax.ppermute(lax.slice_in_dim(block, 0, width, axis=dim), axis, backward)
        block = jnp.concatenate([low, block, high], axis=dim)
    return block


def shifted(value, axis, steps):
    count = lax.axis_size(axis)
    leading, last = (max(0, -steps), min(count, count - steps))
    return lax.ppermute(value, axis, [(source, source + steps) for source in range(leading, last)])


def shift_left(values):
    filler = jnp.zeros(values.shape[:-1] + (1,), values.dtype)
    return jnp.concatenate([values[..., 1:], filler], axis=-1)


def shift_right(values):
    filler = jnp.zeros(values.shape[:-1] + (1,), values.dtype)
    return jnp.concatenate([filler, values[..., :-1]], axis=-1)


def plane_terms(padded, modulus, element_matrix, plane_index):
    channels = padded.shape[0]
    load_count = channels // 3
    width_rows = padded.shape[2] - 2
    width_cols = padded.shape[3]
    layer = lax.dynamic_slice_in_dim(padded, plane_index, 2, 1)
    corners = []
    for corner_z in (0, 1):
        for corner_y in (0, 1):
            sliced = layer[:, corner_z, corner_y : corner_y + width_rows + 1, :]
            corners.append(sliced)
            corners.append(shift_left(sliced))
    stacked = jnp.stack(corners, 0).reshape(24, load_count, -1)
    weights = lax.dynamic_index_in_dim(modulus, plane_index, 0, False).reshape(1, 1, -1)
    forces = jnp.einsum("ij,jlq->ilq", element_matrix, stacked, precision=highest) * weights
    forces = forces.reshape(8, channels, width_rows + 1, width_cols)
    lower_part = jnp.zeros((channels, width_rows, width_cols), forces.dtype)
    upper_part = jnp.zeros((channels, width_rows, width_cols), forces.dtype)
    for corner_y in (0, 1):
        start_y = 1 - corner_y
        lower_part = lower_part + forces[corner_y * 2][:, start_y : start_y + width_rows, :]
        lower_part = lower_part + shift_right(
            forces[corner_y * 2 + 1][:, start_y : start_y + width_rows, :]
        )
        upper_part = upper_part + forces[4 + corner_y * 2][:, start_y : start_y + width_rows, :]
        upper_part = upper_part + shift_right(
            forces[5 + corner_y * 2][:, start_y : start_y + width_rows, :]
        )
    return (lower_part, upper_part)


def assemble(padded, modulus, element_matrix):
    plane_count = modulus.shape[0]
    channels = padded.shape[0]
    width_rows = padded.shape[2] - 2
    width_cols = padded.shape[3]
    empty = jnp.zeros((channels, plane_count, width_rows, width_cols), jnp.float32)

    def one_plane(plane_index, buffers):
        lower_buf, upper_buf = buffers
        lower_part, upper_part = plane_terms(padded, modulus, element_matrix, plane_index)
        lower_buf = lax.dynamic_update_slice_in_dim(lower_buf, lower_part[:, None], plane_index, 1)
        upper_buf = lax.dynamic_update_slice_in_dim(upper_buf, upper_part[:, None], plane_index, 1)
        return (lower_buf, upper_buf)

    lower_buf, upper_buf = lax.fori_loop(0, plane_count, one_plane, (empty, empty))
    return lower_buf[:, 1:] + upper_buf[:, :-1]


def apply_operator(vector_field, modulus, element_matrix):
    padded = padded_2(vector_field, (("gz", 1), ("gy", 2)), 1)
    return assemble(padded, modulus, element_matrix) + spring * vector_field


def gram_local(first, second):
    return jnp.einsum(
        "clq,cmq->lm", first.reshape(3, LOADS, -1), second.reshape(3, LOADS, -1), precision=highest
    )


def combine(vector_field, matrix):
    mixed = jnp.einsum("clq,lm->cmq", vector_field.reshape(3, LOADS, -1), matrix, precision=highest)
    return mixed.reshape(vector_field.shape)


def solve_small(matrix, target):
    factor = jnp.linalg.cholesky(matrix)
    halfway = lax.linalg.triangular_solve(factor, target, left_side=True, lower=True)
    return lax.linalg.triangular_solve(
        factor, halfway, left_side=True, lower=True, transpose_a=True
    )


def norm_sum(residual):
    return lax.psum(gram_local(residual, residual), ("gz", "gy"))


def curvature_sum(direction, applied):
    return lax.psum(gram_local(direction, applied), ("gz", "gy"))


def body(patch_force, patch_owner, patch_voxel, patch_live, voxel_mask, element_matrix):
    patch_total = patch_force.shape[0]
    channels = patch_force.shape[1]
    slot_width = patch_force.shape[2]
    slab_depth, slab_rows, slab_cols = voxel_mask.shape
    groups_z = lax.axis_size("gz")
    groups_y = lax.axis_size("gy")
    device_count = groups_z * groups_y
    capacity = max(2, (2 * patch_total + device_count - 1) // device_count)
    load_of = jnp.arange(channels, dtype=jnp.int32) % LOADS
    live_count = patch_live[:, load_of]
    keep = jnp.arange(slot_width, dtype=jnp.int32)[None, None, :] < live_count[:, :, None]
    loaded = jnp.where(keep, patch_force, jnp.zeros_like(patch_force))
    owner_hits = (
        patch_owner[:, None] == jnp.arange(device_count, dtype=jnp.int32)[None, :]
    ).astype(jnp.int32)
    earlier = jnp.cumsum(owner_hits, axis=0) - owner_hits
    rank_within = jnp.sum(earlier * owner_hits, axis=1)
    target_slot = patch_owner * capacity + rank_within
    send_force = (
        jnp.zeros((device_count * capacity, channels, slot_width), jnp.float32)
        .at[target_slot]
        .set(loaded)
    )
    send_ids = (
        jnp.zeros((device_count * capacity, slot_width), jnp.int32).at[target_slot].set(patch_voxel)
    )
    send_force = send_force.reshape(device_count, capacity, channels, slot_width)
    send_ids = send_ids.reshape(device_count, capacity, slot_width)
    got_force, got_ids = (
        lax.all_to_all(send_force, ("gz", "gy"), split_axis=0, concat_axis=0, tiled=True),
        lax.all_to_all(send_ids, ("gz", "gy"), split_axis=0, concat_axis=0, tiled=True),
    )
    got_force = got_force.reshape(-1, channels, slot_width)
    flat_ids = got_ids.reshape(-1)
    contrib = jnp.transpose(got_force, (1, 0, 2)).reshape(channels, -1)
    volume = slab_depth * slab_rows * slab_cols
    nodal_force = jnp.zeros((channels, volume), jnp.float32).at[:, flat_ids].add(contrib)
    nodal_force = nodal_force.reshape(channels, slab_depth, slab_rows, slab_cols)
    top_plane = voxel_mask[-1]
    below_plane = shifted(top_plane, "gz", 1)
    mask_z = jnp.concatenate([below_plane[None], voxel_mask], axis=0)
    last_row = mask_z[:, -1, :]
    beside_row = shifted(last_row, "gy", 1)
    mask_full = jnp.concatenate([beside_row[:, None, :], mask_z], axis=1)
    modulus = mask_full.astype(jnp.float32).reshape(slab_depth + 1, (slab_rows + 1) * slab_cols)
    displacement = jnp.zeros_like(nodal_force)
    residual = nodal_force
    direction = nodal_force
    norm_gram = norm_sum(residual)
    for iteration in range(ITERS):
        applied = apply_operator(direction, modulus, element_matrix)
        curvature = curvature_sum(direction, applied)
        curvature = 0.5 * (curvature + curvature.T)
        step_alpha = solve_small(curvature, norm_gram)
        displacement = displacement + combine(direction, step_alpha)
        residual = residual - combine(applied, step_alpha)
        if iteration + 1 < ITERS:
            norm_next = norm_sum(residual)
            step_beta = solve_small(norm_gram, norm_next)
            direction = residual + combine(direction, step_beta)
            norm_gram = norm_next
    return (displacement, residual)


def solution(mesh):
    placed = (
        P(("gz", "gy"), None, None),
        P(("gz", "gy")),
        P(("gz", "gy"), None),
        P(("gz", "gy"), None),
        P("gz", "gy", None),
        P(),
    )
    return jax.shard_map(
        body,
        mesh=mesh,
        in_specs=placed,
        out_specs=(P(None, "gz", "gy", None), P(None, "gz", "gy", None)),
        check_vma=False,
    )
```

profile of v0, /device:TPU:1, one launch (start us, length us, event | category | flops | bytes accessed | tf_op | source)
XLA Modules:
  0.0 1267.3 jit_solution(8029878859421293857)
XLA Ops:
  4.9 11.5 all-to-all-start
  20.6 15.6 %scatter_fusion = f32[256,24,128]{2,1,0:T(8,128)} fusion(f32[256,24,128]{2,1,0:T(8,128)} %broadcast_in_dim.60, s32[128]{0:T(128)S(1)} %compare_select_fusion.2, f32[128,24,128]{2,1,0:T(8,128)S(1)} %fusion.28), kind=kCustom, calls=%fused_computation.2 | custom fusion | bytes 4719104 | tf_op jit(solution)/shard_map/scatter | solution.py:146
  36.2 10.2 all-to-all-start.1
  46.6 41.2 %all-to-all-done.1 = f32[128,2,24,128]{3,2,1,0:T(8,128)} async-done(((f32[128,2,24,128]{3,2,1,0:T(8,128)}), f32[128,2,24,128]{3,2,1,0:T(8,128)}, u32[]{:S(2)}, u32[]{:S(2)}) %all-to-all-start.1) | async-done | bytes 3145760 | tf_op jit(solution)/shard_map/all_to_all | solution.py:154
  87.7 10.0 copy.209
  97.7 208.5 %scatter_custom_fusion.2 = f32[24,16384]{0,1:T(8,128)} fusion(s32[32768]{0:T(1024)S(1)} %bitcast.314, f32[32768,24]{1,0:T(8,128)} %bitcast.303, f32[]{:T(128)} %constant.138.clone.1), kind=kCustom, calls=%fused_computation.67 | custom fusion | flops 786432 | bytes 1573376 | tf_op jit(solution)/shard_map/scatter-add | solution.py:161
  306.2 5.2 copy.211
  314.1 4.0 collective-permute-start.4
  318.9 5.2 collective-permute-start.5
  327.1 3.6 collective-permute-start.3
  331.6 6.1 copy.218
  337.7 5.1 copy.210
  342.8 4.1 fusion.29
  346.9 3.7 pad_maximum_fusion
  353.5 333.7 %while.30 = (s32[]{:T(128)}, f32[24,9,8,256]{3,0,2,1:T(8,128)}, f32[24,9,8,256]{3,0,2,1:T(8,128)}, f32[24,10,10,256]{3,2,0,1:T(8,128)}, f32[24,24]{1,0:T(8,128)S...) while((s32[]{:T(128)}, f32[24,9,8,256]{3,0,2,1:T(8,128)}, f32[24,9,8,256]{3,0,2,1:T(8,128)}, ...), condition=%wide.region_6.7_spmd, body=%wide.region_5.6_spmd.sunk | while | flops 128139264 | bytes 31001880 | solution.py:88
  693.3 3.7 fusion.32
  697.0 66.4 %all-reduce.16 = (f32[8,8]{0,1:T(8,128)S(1)}, f32[8,8]{1,0:T(8,128)S(1)}) all-reduce(f32[8,8]{0,1:T(8,128)S(1)} %copy-done.17, f32[8,8]{1,0:T(8,128)S(1)} %fusion.32), channel_id=1, replica_groups=mesh['gz'=16,'gy'=8] {'gz','gy'}, use_global_device_ids=true, to_apply=%region_10.12 | all-reduce | flops 128 | bytes 1024 | tf_op jit(solution)/shard_map/psum | solution.py:117
  772.4 3.5 convolution_bitcast_fusion.3
  775.9 64.0 %psum.30 = f32[8,8]{1,0:T(8,128)S(1)} all-reduce(f32[8,8]{1,0:T(8,128)S(1)} %convolution_bitcast_fusion.3), channel_id=1, replica_groups=mesh['gz'=16,'gy'=8] {'gz','gy'}, use_global_device_ids=true, to_apply=%region_11.15 | all-reduce | flops 64 | bytes 512 | tf_op jit(solution)/shard_map/psum | solution.py:117
  851.7 3.9 collective-permute-done.7
  855.7 4.2 collective-permute-start.8
  872.0 300.9 %while.31 = (s32[]{:T(128)}, f32[24,9,8,256]{3,0,2,1:T(8,128)}, f32[24,9,8,256]{3,0,2,1:T(8,128)}, f32[24,10,10,256]{3,0,2,1:T(8,128)}, f32[24,24]{1,0:T(8,128)S...) while((s32[]{:T(128)}, f32[24,9,8,256]{3,0,2,1:T(8,128)}, f32[24,9,8,256]{3,0,2,1:T(8,128)}, ...), condition=%wide.region_13.17_spmd, body=%wide.region_12.16_spmd.sunk | while | flops 128139264 | bytes 32254724 | solution.py:88
  1179.9 5.4 convolution_bitcast_fusion.1
  1185.3 66.3 %psum.31 = f32[8,8]{1,0:T(8,128)S(1)} all-reduce(f32[8,8]{1,0:T(8,128)S(1)} %convolution_bitcast_fusion.1), channel_id=1, replica_groups=mesh['gz'=16,'gy'=8] {'gz','gy'}, use_global_device_ids=true, to_apply=%region_14.18 | all-reduce | flops 64 | bytes 512 | tf_op jit(solution)/shard_map/psum | solution.py:121
  (886 shorter events, 711.5 us)
Async XLA Ops:
  0.6 15.8 %copy-start = (s32[128,8]{0,1:T(8,128)S(1)}, s32[128,8]{0,1:T(8,128)}, u32[]{:S(2)}) copy-start(s32[128,8]{0,1:T(8,128)} %param.18) | copy-start | bytes 12292
  4.9 31.4 %all-to-all-start = ((s32[128,2,128]{2,1,0:T(2,128)}), s32[128,2,128]{2,1,0:T(2,128)S(1)}, u32[]{:S(2)}, u32[]{:S(2)}) async-start(s32[128,2,128]{2,1,0:T(2,128)} %bitcast.32), calls=%async_computation | async-start | bytes 262144 | tf_op jit(solution)/shard_map/all_to_all | solution.py:155
  36.2 51.5 %all-to-all-start.1 = ((f32[128,2,24,128]{3,2,1,0:T(8,128)}), f32[128,2,24,128]{3,2,1,0:T(8,128)}, u32[]{:S(2)}, u32[]{:S(2)}) async-start(f32[128,2,24,128]{3,2,1,0:T(8,128)} %bitcast.302), calls=%async_computation.1 | async-start | bytes 6291456 | tf_op jit(solution)/shard_map/all_to_all | solution.py:154
  306.2 7.9 copy-start.14
  311.5 12.6 collective-permute-start
  312.8 11.3 collective-permute-start.1
  314.1 4.8 collective-permute-start.4
  318.9 11.8 collective-permute-start.5
  325.2 21.7 %collective-permute-start.2 = (f32[24,10,1,256]{3,2,0,1:T(1,128)}, f32[24,10,1,256]{3,2,0,1:T(1,128)}, u32[]{:S(2)}, u32[]{:S(2)}) collective-permute-start(f32[24,10,1,256]{3,2,0,1:T(1,128)} %get-tuple-element.313), channel_id=1, source_target_pairs={{0,1},{1,2},{2,3},{3,4},{4,5},{5,6},{6,7},{8,9},{9,10},{10,11},{11... | collective-permute-start | bytes 737288 | tf_op jit(solution)/shard_map/ppermute | solution.py:19
  327.1 19.8 %collective-permute-start.3 = (f32[24,10,1,256]{3,2,0,1:T(1,128)}, f32[24,10,1,256]{3,2,0,1:T(1,128)}, u32[]{:S(2)}, u32[]{:S(2)}) collective-permute-start(f32[24,10,1,256]{3,2,0,1:T(1,128)} %get-tuple-element.314), channel_id=1, source_target_pairs={{1,0},{2,1},{3,2},{4,3},{5,4},{6,5},{7,6},{9,8},{10,9},{11,10},{12... | collective-permute-start | bytes 737288 | tf_op jit(solution)/shard_map/ppermute | solution.py:22
  350.6 2.9 copy-start.13
  693.3 76.1 %copy-start.9 = (f32[3,8,16384]{2,1,0:T(8,128)}, f32[3,8,16384]{2,1,0:T(8,128)S(1)}, u32[]{:S(2)}) copy-start(f32[3,8,16384]{2,1,0:T(8,128)S(1)} %reshape.197) | copy-start | bytes 4718596
  693.3 3.7 copy-start.17
  772.4 70.0 %copy-start.2 = (f32[8,3,16384]{2,0,1:T(8,128)}, f32[8,3,16384]{2,0,1:T(8,128)S(1)}, u32[]{:S(2)}) copy-start(f32[8,3,16384]{2,0,1:T(8,128)S(1)} %fusion.61) | copy-start | bytes 4718596
  843.0 2.6 copy-start.10
  845.6 21.8 %copy-start.4 = (f32[24,8,8,256]{3,0,2,1:T(8,128)}, f32[24,8,8,256]{3,0,2,1:T(8,128)S(1)}, u32[]{:S(2)}) copy-start(f32[24,8,8,256]{3,0,2,1:T(8,128)S(1)} %copy_add_fusion) | copy-start | bytes 4718596
  846.4 5.2 collective-permute-start.6
  847.7 7.9 collective-permute-start.7
  855.7 8.7 collective-permute-start.8
  859.9 7.5 collective-permute-start.9
  1177.2 2.7 copy-start.3
  1179.9 74.5 %copy-start.16 = (f32[8,8]{1,0:T(8,128)S(1)}, f32[8,8]{1,0:T(8,128)}, u32[]{:S(2)}) copy-start(f32[8,8]{1,0:T(8,128)} %copy-done.15) | copy-start | bytes 772
  1261.3 2.4 copy-start.12
  1263.7 3.1 copy-start.1
  (6 other events, 9.9 us)
where the time goes:
time: 1280 us; the launch traced here: 1270 us
  local copies, waits for them, and re-layouts  608 us (48%)
  other arithmetic  292 us (23%)
  blocking collectives  197 us (15%)
  matrix products  66.9 us (5%)
  waiting for transfers between devices  51.5 us (4%)
  starting transfers between devices  47.7 us (4%)
    scatter-add x1, other arithmetic, body(): jnp.zeros((channels, volume), jnp.float32).at[:, flat_ids].add(contrib)  209 us
    while x162, local copies, waits for them, and re-layouts  140 us
    psum x2, blocking collectives, norm_sum(): return lax.psum(gram_local(residual, residual), ('gz', 'gy'))  130 us
    psum x1, blocking collectives, curvature_sum(): return lax.psum(gram_local(direction, applied), ('gz', 'gy'))  66.3 us
    squeeze x36, local copies, waits for them, and re-layouts, plane_terms(): forces[corner_y * 2 + 1][:, start_y:start_y + width_rows, :]  61.9 us
    slice x72, local copies, waits for them, and re-layouts, shift_right(): return jnp.concatenate([filler, values[..., :-1]], axis=-1)  60.2 us
    reshape x18, local copies, waits for them, and re-layouts, plane_terms(): stacked = jnp.stack(corners, 0).reshape(24, load_count, -1)  46.7 us
    squeeze x36, local copies, waits for them, and re-layouts, plane_terms(): forces[corner_y * 2][:, start_y:start_y + width_rows, :]  45.2 us
  transfers between devices with their start and end apart: 12, of which 5 were waited for; matrix products, arithmetic and copies ran while one was open for 3% of the time, Pallas kernels for 0%

commit v1 on v0

v1 whole, which is shorter than its diff:
```python
import functools
import jax
import jax.numpy as jnp
from jax import lax
from jax.experimental import pallas as pl
from jax.experimental.pallas import tpu as pltpu
from jax.sharding import PartitionSpec as P

LOADS = 8
CH = 24
ROWS = 56
GROUP = 4
AXES = ("gz", "gy")
SPRING = 0.5
F32 = jnp.float32
BF16 = jnp.bfloat16
VMEM_LIMIT = 60 * 1024 * 1024


def vmem():
    return pl.BlockSpec(memory_space=pltpu.VMEM)


def smem():
    return pl.BlockSpec(memory_space=pltpu.SMEM)


def pack_kernel(owner_ref, live_ref, voxel_ref, force_ref, out_ref, count_ref):
    devices = out_ref.shape[0]
    blocks = force_ref.shape[0]
    lane = lax.broadcasted_iota(jnp.int32, (8, 128), 1)

    def clear(i, carry):
        count_ref[i] = 0
        out_ref[i, 48:56, :] = jnp.full((8, 128), -1.0, F32)
        return carry

    lax.fori_loop(0, devices, clear, 0)
    live = live_ref[...]

    def one(p, carry):
        owner = owner_ref[p]
        rank = count_ref[owner]
        count_ref[owner] = rank + 1
        limit = jnp.sum(jnp.where(lane == p, live, 0.0), axis=1, keepdims=True)
        keep = lane.astype(F32) < limit
        for k in range(3):
            base = pl.multiple_of(rank * CH + k * 8, 8)
            out_ref[owner, pl.ds(base, 8), :] = jnp.where(
                keep, force_ref[p, k * 8 : (k + 1) * 8, :], 0.0
            )
        out_ref[owner, pl.ds(48 + rank, 1), :] = voxel_ref[pl.ds(p, 1), :].astype(F32)
        return carry

    lax.fori_loop(0, blocks, one, 0, unroll=4)


def pack(owner, live_t, voxel, force, devices):
    return pl.pallas_call(
        pack_kernel,
        out_shape=jax.ShapeDtypeStruct((devices, ROWS, 128), F32),
        in_specs=[smem(), vmem(), vmem(), vmem()],
        out_specs=vmem(),
        scratch_shapes=[pltpu.SMEM((devices,), jnp.int32)],
        compiler_params=pltpu.CompilerParams(vmem_limit_bytes=VMEM_LIMIT),
        name="pack",
    )(owner, live_t, voxel, force)


def scatter_kernel(valid_ref, recv_ref, *refs):
    outs = refs[:9]
    list_ref, left_ref, right_ref, acc_ref = refs[9:]
    total = valid_ref.shape[0]

    def collect(i, n):
        list_ref[n] = i
        return n + valid_ref[i]

    count = lax.fori_loop(0, total, collect, jnp.int32(0), unroll=8)
    acc_ref[...] = jnp.zeros_like(acc_ref)
    row_x = lax.broadcasted_iota(jnp.int32, (256, 128), 0)
    row_zy = lax.broadcasted_iota(jnp.int32, (64, 128), 0)

    def group(g, carry):
        for j in range(GROUP):
            place = g * GROUP + j
            index = list_ref[jnp.minimum(place, count - 1)]
            source = index // 2
            rank = index % 2
            ids = recv_ref[source, pl.ds(48 + rank, 1), :].astype(jnp.int32)
            zy = jnp.where(place < count, ids // 256, -1)
            x = ids & 255
            hot_x = jnp.where(row_x == x, 1.0, 0.0).astype(BF16)
            right_ref[:, j * 256 : j * 256 + 128] = hot_x
            right_ref[:, j * 256 + 128 : (j + 1) * 256] = hot_x
            hot_zy = jnp.where(row_zy == zy, 1.0, 0.0).astype(BF16)
            value = recv_ref[source, pl.ds(pl.multiple_of(rank * CH, 8), CH), :]
            high = value.astype(BF16).astype(F32)
            low = value - high
            for c in range(CH):
                for half, part in enumerate((high, low)):
                    line = jnp.broadcast_to(part[c : c + 1, :], (16, 128)).astype(BF16)
                    tile = jnp.concatenate([line] * 4, axis=0) * hot_zy
                    at = j * 256 + half * 128
                    left_ref[c * 64 : (c + 1) * 64, at : at + 128] = tile
        for m in range(3):
            part = lax.dot_general(
                left_ref[m * 512 : (m + 1) * 512, :],
                right_ref[...],
                (((1,), (1,)), ((), ())),
                preferred_element_type=F32,
            )
            for h in range(2):
                acc_ref[h, m * 512 : (m + 1) * 512, :] += part[:, h * 128 : (h + 1) * 128]
        return carry

    lax.fori_loop(0, (count + GROUP - 1) // GROUP, group, 0)

    field, z_low, z_high, y_low, y_high, c_ll, c_lh, c_hl, c_hh = outs
    for z in range(8):
        for y in range(8):
            node = jnp.concatenate(
                [
                    jnp.concatenate(
                        [
                            acc_ref[h, pl.ds(k * 512 + z * 8 + y, 8, stride=64), :]
                            for k in range(3)
                        ],
                        axis=0,
                    )
                    for h in range(2)
                ],
                axis=1,
            )
            field[z, y] = node
            if z < 2:
                z_low[z, y] = node
            if z > 5:
                z_high[z - 6, y] = node
            if y < 2:
                y_low[z, y] = node
            if y > 5:
                y_high[z, y - 6] = node
            if z < 2 and y < 2:
                c_ll[z, y] = node
            if z < 2 and y > 5:
                c_lh[z, y - 6] = node
            if z > 5 and y < 2:
                c_hl[z - 6, y] = node
            if z > 5 and y > 5:
                c_hh[z - 6, y - 6] = node


def scatter(valid, recv):
    def shape(a, b):
        return jax.ShapeDtypeStruct((a, b, CH, 256), F32)

    return pl.pallas_call(
        scatter_kernel,
        out_shape=[shape(8, 8), shape(2, 8), shape(2, 8), shape(8, 2), shape(8, 2)]
        + [shape(2, 2)] * 4,
        in_specs=[smem(), vmem()],
        out_specs=[vmem()] * 9,
        scratch_shapes=[
            pltpu.SMEM((valid.shape[0] + 8,), jnp.int32),
            pltpu.VMEM((CH * 64, GROUP * 256), BF16),
            pltpu.VMEM((256, GROUP * 256), BF16),
            pltpu.VMEM((2, CH * 64, 128), F32),
        ],
        compiler_params=pltpu.CompilerParams(vmem_limit_bytes=VMEM_LIMIT),
        name="scatter",
    )(valid, recv)


def shift_down(v, lane):
    return jnp.where(lane == 255, 0.0, pltpu.roll(v, 255, axis=1))


def shift_up(v, lane):
    return jnp.where(lane == 0, 0.0, pltpu.roll(v, 1, axis=1))


def operator_kernel(
    flag_ref, field, z_low, z_high, y_low, y_high, c_ll, c_lh, c_hl, c_hh, mask_ref, k_both, k_high,
    s_out, q_out, gram_out,
    v32, vh, vl, s32, sh, sl, carry_ref, gram_ref,
):
    lane = lax.broadcasted_iota(jnp.int32, (CH, 256), 1)

    def put(full, high, low, z, y, v):
        full[z, y * CH : (y + 1) * CH, :] = v
        both = jnp.concatenate([v, shift_down(v, lane)], axis=0)
        top = both.astype(BF16)
        high[z, y * 48 : (y + 1) * 48, :] = top
        low[z, y * 48 : (y + 1) * 48, :] = (both - top.astype(F32)).astype(BF16)

    def rows(source, z_count, y_count, z_at, y_at):
        def one(z, carry):
            for y in range(y_count):
                put(v32, vh, vl, z + z_at, y + y_at, source[z, y])
            return carry

        lax.fori_loop(0, z_count, one, 0)

    rows(c_ll, 2, 2, 0, 0)
    rows(z_low, 2, 8, 0, 2)
    rows(c_lh, 2, 2, 0, 10)
    rows(y_low, 8, 2, 2, 0)
    rows(field, 8, 8, 2, 2)
    rows(y_high, 8, 2, 2, 10)
    rows(c_hl, 2, 2, 10, 0)
    rows(z_high, 2, 8, 10, 2)
    rows(c_hh, 2, 2, 10, 10)

    def element(high, low, ez, ey):
        def gather(ref):
            return jnp.concatenate(
                [ref[ez, ey * 48 : (ey + 2) * 48, :], ref[ez + 1, ey * 48 : (ey + 2) * 48, :]], axis=0
            )

        first = jnp.dot(k_both[...], gather(high), preferred_element_type=F32)
        second = jnp.dot(k_high[...], gather(low), preferred_element_type=F32)
        force = first[:192] + first[192:] + second
        return force * mask_ref[ez, ey : ey + 1, :]

    def layer(high, low, full, ez, start, stop, finish):
        before = None
        for ey in range(start, stop):
            force = element(high, low, ez, ey)
            if ey > start:
                lower = before[0] + force[0:48] + carry_ref[ey]
                carry_ref[ey] = before[1] + force[96:144]
                value = lower[:CH] + shift_up(lower[CH:], lane)
                finish(ey, value + SPRING * full[ez, ey * CH : (ey + 1) * CH, :])
            before = (force[48:96], force[144:192])

    carry_ref[...] = jnp.zeros_like(carry_ref)

    def first_pass(ez, carry):
        inside = jnp.where(ez == 10, flag_ref[0], 1.0)

        def finish(n, value):
            keep = inside * flag_ref[1] if n == 10 else inside
            put(s32, sh, sl, ez, n, value * keep)

        layer(vh, vl, v32, ez, 0, 11, finish)
        return carry

    lax.fori_loop(0, 11, first_pass, 0)
    carry_ref[...] = jnp.zeros_like(carry_ref)

    def second_pass(ez, carry):
        def finish(n, value):
            q_out[jnp.maximum(ez - 2, 0), n - 2] = value

        layer(sh, sl, s32, ez, 1, 10, finish)
        return carry

    lax.fori_loop(1, 10, second_pass, 0)

    gram_ref[...] = jnp.zeros_like(gram_ref)

    def products(z, carry):
        sums = [None] * 20
        for y in range(8):
            r_row = field[z, y]
            s_row = s32[z + 2, (y + 2) * CH : (y + 3) * CH, :]
            q_row = q_out[z, y]
            s_out[z, y] = s_row
            for k in range(3):
                for h in range(2):
                    r, s, q = (t[k * 8 : (k + 1) * 8, h * 128 : (h + 1) * 128] for t in (r_row, s_row, q_row))
                    for j in range(5):
                        if j == 0:
                            rj, sj, qj = r, s, q
                        else:
                            rj, sj, qj = (pltpu.roll(t, 8 - j, axis=0) for t in (r, s, q))
                        for n, term in enumerate((r * rj, r * sj, s * sj, s * qj)):
                            at = n * 5 + j
                            sums[at] = term if sums[at] is None else sums[at] + term
        for at in range(20):
            gram_ref[at] += sums[at]
        return carry

    lax.fori_loop(0, 8, products, 0)
    spot = lax.broadcasted_iota(jnp.int32, (8, 128), 1)
    packed = jnp.zeros((8, 128), F32)
    for at in range(20):
        packed = packed + jnp.where(spot == at, jnp.sum(gram_ref[at], axis=1, keepdims=True), 0.0)

    def send(i, carry):
        gram_out[i] = packed
        return carry

    lax.fori_loop(0, gram_out.shape[0], send, 0, unroll=8)


def operator(flags, fields, mask, k_both, k_high, devices):
    node = jax.ShapeDtypeStruct((8, 8, CH, 256), F32)
    return pl.pallas_call(
        operator_kernel,
        out_shape=[node, node, jax.ShapeDtypeStruct((devices, 8, 128), F32)],
        in_specs=[smem()] + [vmem()] * 12,
        out_specs=[vmem()] * 3,
        scratch_shapes=[
            pltpu.VMEM((12, 12 * CH, 256), F32),
            pltpu.VMEM((12, 12 * 48, 256), BF16),
            pltpu.VMEM((12, 12 * 48, 256), BF16),
            pltpu.VMEM((11, 11 * CH, 256), F32),
            pltpu.VMEM((11, 11 * 48, 256), BF16),
            pltpu.VMEM((11, 11 * 48, 256), BF16),
            pltpu.VMEM((11, 48, 256), F32),
            pltpu.VMEM((20, 8, 128), F32),
        ],
        compiler_params=pltpu.CompilerParams(vmem_limit_bytes=VMEM_LIMIT),
        name="operator",
    )(flags, *fields, mask, k_both, k_high)


def final_kernel(gram_ref, field, s_ref, q_ref, u_out, r_out, u_half, r_half):
    sub = lax.broadcasted_iota(jnp.int32, (8, 128), 0)
    lane = lax.broadcasted_iota(jnp.int32, (8, 128), 1)
    inside = lane < 8

    total = gram_ref[0]
    for i in range(1, gram_ref.shape[0]):
        total = total + gram_ref[i]

    def column(m, j):
        return jnp.sum(jnp.where(lane == j, m, 0.0), axis=1, keepdims=True)

    def row(m, i):
        return jnp.sum(jnp.where(sub == i, m, 0.0), axis=0, keepdims=True)

    def unpack(base):
        out = jnp.zeros((8, 128), F32)
        for j in range(5):
            out = jnp.where(inside & (((lane - sub) & 7) == j), column(total, base + j), out)
            if 0 < j < 4:
                turned = pltpu.roll(total, j, axis=0)
                out = jnp.where(inside & (((sub - lane) & 7) == j), column(turned, base + j), out)
        return out

    def mul(a, b):
        out = jnp.zeros((8, 128), F32)
        for i in range(8):
            out = out + column(a, i) * row(b, i)
        return out

    def flip(a):
        out = jnp.zeros((8, 128), F32)
        for i in range(8):
            out = jnp.where(lane == i, jnp.sum(jnp.where(lane == sub, row(a, i), 0.0), axis=1, keepdims=True), out)
        return out

    def solve(m, b):
        for i in range(8):
            pivot_row = row(m, i)
            scale = 1.0 / column(pivot_row, i)
            pivot_b = row(b, i) * scale
            pivot_row = pivot_row * scale
            factor = jnp.where(sub == i, 0.0, column(m, i))
            m = jnp.where(sub == i, pivot_row, m - factor * pivot_row)
            b = jnp.where(sub == i, pivot_b, b - factor * pivot_b)
        return b

    rr, w, ss, tt = (unpack(5 * n) for n in range(4))
    alpha = solve(w, rr)
    alpha_t = flip(alpha)
    w_alpha = mul(w, alpha)
    s_alpha = mul(ss, alpha)
    new = rr - w_alpha - flip(w_alpha) + mul(alpha_t, s_alpha)
    beta = solve(rr, new)
    one_beta = beta + jnp.where(lane == sub, 1.0, 0.0)
    turn = flip(one_beta)
    cross = mul(turn, s_alpha)
    w2 = mul(turn, mul(w, one_beta)) - cross - flip(cross) + mul(alpha_t, mul(tt, alpha))
    alpha2 = solve(0.5 * (w2 + flip(w2)), new)
    p_mat = alpha + mul(one_beta, alpha2)
    q_mat = mul(alpha, alpha2)

    def coefficients(mat):
        turned = flip(mat)
        return [
            jnp.broadcast_to(
                jnp.sum(jnp.where(inside & (((lane - sub) & 7) == j), turned, 0.0), axis=1, keepdims=True),
                (8, 128),
            )
            for j in range(8)
        ]

    p_co = coefficients(p_mat)
    q_co = coefficients(q_mat)

    def plane(z, carry):
        for y in range(8):
            for k in range(3):
                for h in range(2):
                    part = (slice(k * 8, (k + 1) * 8), slice(h * 128, (h + 1) * 128))
                    r = field[z, y, part[0], part[1]]
                    s = s_ref[z, y, part[0], part[1]]
                    q = q_ref[z, y, part[0], part[1]]
                    u = None
                    e = r
                    for j in range(8):
                        rj, sj, qj = (t if j == 0 else pltpu.roll(t, 8 - j, axis=0) for t in (r, s, q))
                        term = p_co[j] * rj - q_co[j] * sj
                        u = term if u is None else u + term
                        e = e - p_co[j] * sj + q_co[j] * qj
                    at = pl.ds(k * 512 + z * 8 + y, 8, stride=64)
                    u_half[h, at, :] = u
                    r_half[h, at, :] = e
        return carry

    lax.fori_loop(0, 8, plane, 0)

    def join(i, carry):
        at = pl.ds(pl.multiple_of(i * 64, 64), 64)
        for h in range(2):
            u_out[at, h * 128 : (h + 1) * 128] = u_half[h, at, :]
            r_out[at, h * 128 : (h + 1) * 128] = r_half[h, at, :]
        return carry

    lax.fori_loop(0, CH, join, 0)


def final(gram, field, s, q):
    out = jax.ShapeDtypeStruct((CH * 64, 256), F32)
    return pl.pallas_call(
        final_kernel,
        out_shape=[out, out],
        in_specs=[vmem()] * 4,
        out_specs=[vmem()] * 2,
        scratch_shapes=[pltpu.VMEM((2, CH * 64, 128), F32)] * 2,
        compiler_params=pltpu.CompilerParams(vmem_limit_bytes=VMEM_LIMIT),
        name="final",
    )(gram, field, s, q)


def moved(value, dz, dy):
    nz, ny = lax.axis_size("gz"), lax.axis_size("gy")
    pairs = []
    for z in range(nz):
        for y in range(ny):
            if 0 <= z + dz < nz and 0 <= y + dy < ny:
                pairs.append((z * ny + y, (z + dz) * ny + y + dy))
    return lax.ppermute(value, AXES, pairs)


def body(patch_force, patch_owner, patch_voxel, patch_live, voxel_mask, element_matrix):
    nz, ny = lax.axis_size("gz"), lax.axis_size("gy")
    devices = nz * ny

    send = pack(patch_owner, patch_live.astype(F32).T, patch_voxel, patch_force, devices)
    recv = lax.all_to_all(send, AXES, split_axis=0, concat_axis=0, tiled=True)

    mask = voxel_mask
    mask = jnp.concatenate([moved(mask[6:8], 1, 0), mask, moved(mask[0:1], -1, 0)], axis=0)
    mask = jnp.concatenate([moved(mask[:, 6:8], 0, 1), mask, moved(mask[:, 0:1], 0, -1)], axis=1)
    mask = mask.astype(F32)

    big = jnp.einsum("ij,lm->iljm", element_matrix, jnp.eye(LOADS, dtype=F32)).reshape(192, 192)
    rounded = lax.reduce_precision(big, 8, 7)
    k_high = rounded.astype(BF16)
    k_both = jnp.concatenate([k_high, (big - rounded).astype(BF16)], axis=0)

    valid = (recv[:, 48:50, 0] >= 0).astype(jnp.int32).reshape(-1)
    field, z_low, z_high, y_low, y_high, c_ll, c_lh, c_hl, c_hh = scatter(valid, recv)
    around = (
        field,
        moved(z_high, 1, 0),
        moved(z_low, -1, 0),
        moved(y_high, 0, 1),
        moved(y_low, 0, -1),
        moved(c_hh, 1, 1),
        moved(c_hl, 1, -1),
        moved(c_lh, -1, 1),
        moved(c_ll, -1, -1),
    )
    flags = jnp.stack([lax.axis_index("gz") + 1 < nz, lax.axis_index("gy") + 1 < ny]).astype(F32)
    s, q, gram = operator(flags, around, mask, k_both, k_high, devices)
    gram = lax.all_to_all(gram, AXES, split_axis=0, concat_axis=0, tiled=True)
    u, r = final(gram, field, s, q)
    return u.reshape(CH, 8, 8, 256), r.reshape(CH, 8, 8, 256)


def solution(mesh):
    placed = (
        P(AXES, None, None),
        P(AXES),
        P(AXES, None),
        P(AXES, None),
        P("gz", "gy", None),
        P(),
    )
    return jax.shard_map(
        body,
        mesh=mesh,
        in_specs=placed,
        out_specs=(P(None, "gz", "gy", None), P(None, "gz", "gy", None)),
        check_vma=False,
    )
```

time: 1280 us -> 231 us (0.18)
  local copies, waits for them, and re-layouts: 608 us -> 2.54 us
  other arithmetic: 292 us -> 6.84 us
  blocking collectives: 197 us -> 38.6 us
  Pallas kernels: 0 us -> 83.6 us
  matrix products: 66.9 us -> 0 us
  waiting for transfers between devices: 51.5 us -> 37.4 us
    scatter-add x1 -> x0, other arithmetic: 209 us -> none  [body(): jnp.zeros((channels, volume), jnp.float32).at[:, flat_ids].add(contrib)]
    psum x3 -> x0, blocking collectives: 197 us -> none  [the longest x2 130 us: norm_sum(): return lax.psum(gram_local(residual, residual), ('gz', 'gy'))]
    slice x317 -> x4, local copies, waits for them, and re-layouts: 165 us -> 0.03 us  [the longest x1 0.01 us: body(): mask[:, 6:8]]
    while x162 -> x0, local copies, waits for them, and re-layouts: 140 us -> none
    squeeze x154 -> x0, local copies, waits for them, and re-layouts: 124 us -> none  [the longest x36 61.9 us: plane_terms(): forces[corner_y * 2 + 1][:, start_y:start_y + width_rows, :]]
    pallas_call x0 -> x4, Pallas kernels: none -> 83.6 us  [the longest x1 32.4 us: scatter(): pl.pallas_call(scatter_kernel, out_shape=[shape(8, 8), shape(2, 8), shape...]
    reshape x23 -> x1, local copies, waits for them, and re-layouts: 72.4 us -> 0.67 us  [body(): jnp.einsum('ij,lm->iljm', element_matrix, jnp.eye(LOADS, dtype=F32))]
    dot_general x27 -> x0, matrix products: 65.7 us -> none  [the longest x18 37.9 us: plane_terms(): jnp.einsum('ij,jlq->ilq', element_matrix, stacked, precision=highest)]
  transfers between devices with their start and end apart: 12 -> 13, of which waited for: 5 -> 4; matrix products, arithmetic and copies ran while one was open for 3% -> 3% of each run, Pallas kernels for 0% -> 14%
where the time goes in v1:
time: 231 us; the launch traced here: 229 us
  Pallas kernels  83.6 us (36%)
  starting transfers between devices  59.5 us (26%)
  blocking collectives  38.6 us (17%)
  waiting for transfers between devices  37.4 us (16%)
  other arithmetic  6.84 us (3%)
  local copies, waits for them, and re-layouts  2.54 us (1%)
    ppermute x12, starting transfers between devices, moved(): return lax.ppermute(value, AXES, pairs)  47.6 us
    all_to_all x1, blocking collectives, body(): gram = lax.all_to_all(gram, AXES, split_axis=0, concat_axis=0, tiled=True)  38.6 us
    pallas_call x1, Pallas kernels, scatter(): pl.pallas_call(scatter_kernel, out_shape=[shape(8, 8), shape(2, 8), shape...  32.4 us
    pallas_call x1, Pallas kernels, operator(): pl.pallas_call(operator_kernel, out_shape=[node, node, jax.ShapeDtypeStru...  31.5 us
    all_to_all x1, waiting for transfers between devices, body(): recv = lax.all_to_all(send, AXES, split_axis=0, concat_axis=0, tiled=True)  19.9 us
    ppermute x12, waiting for transfers between devices, moved(): return lax.ppermute(value, AXES, pairs)  17.5 us
    pallas_call x1, Pallas kernels, final(): pl.pallas_call(final_kernel, out_shape=[out, out], in_specs=[vmem()] * 4,...  12.7 us
    all_to_all x1, starting transfers between devices, body(): recv = lax.all_to_all(send, AXES, split_axis=0, concat_axis=0, tiled=True)  11.9 us
  transfers between devices with their start and end apart: 13, of which 4 were waited for; matrix products, arithmetic and copies ran while one was open for 3% of the time, Pallas kernels for 14%

profile of v1, /device:TPU:1, one launch (start us, length us, event | category | flops | bytes accessed | tf_op | source)
XLA Modules:
  0.0 229.4 jit_solution(4564427363013107518)
XLA Ops:
  0.6 1.3 convert_bitcast_fusion.live_ref
  1.9 6.9 %pack.1 = f32[128,56,128]{2,1,0:T(8,128)} custom-call(s32[128]{0:T(128)} %owner_ref.1, f32[8,128]{1,0:T(8,128)} %convert_bitcast_fusion.live_ref, s32[128,128]{1,0:T(8,128)} %voxel_ref.1, f32[128,24,128]{2,1,0:T(8,128)} %force_ref.1), custom_call_target="tpu_custom_call" | custom-call | tf_op jit(solution)/shard_map/pack/pallas_call | solution.py:59
  8.8 11.9 %all-to-all-start = ((f32[128,56,128]{2,1,0:T(8,128)}), f32[128,56,128]{2,1,0:T(8,128)}, u32[]{:S(2)}, u32[]{:S(2)}) async-start(f32[128,56,128]{2,1,0:T(8,128)} %pack.1), calls=%async_computation | async-start | bytes 7340032 | tf_op jit(solution)/shard_map/all_to_all | solution.py:455
  20.7 1.3 collective-permute-start.9
  22.0 4.0 %collective-permute-start.8 = (s32[2,8,256]{2,1,0:T(8,128)S(1)}, s32[2,8,256]{2,1,0:T(8,128)S(1)}, u32[]{:S(2)}, u32[]{:S(2)}) collective-permute-start(s32[2,8,256]{2,1,0:T(8,128)S(1)} %slice.16), channel_id=1, source_target_pairs={{0,8},{1,9},{2,10},{3,11},{4,12},{5,13},{6,14},{7,15},{8,16},{9,17... | collective-permute-start | bytes 49160 | tf_op jit(solution)/shard_map/ppermute | solution.py:447
  27.0 18.9 %collective-permute-start.11 = (s32[11,1,256]{2,1,0:T(1,128)S(1)}, s32[11,1,256]{2,1,0:T(1,128)S(1)}, u32[]{:S(2)}, u32[]{:S(2)}) collective-permute-start(s32[11,1,256]{2,1,0:T(1,128)S(1)} %slice.22), channel_id=1, source_target_pairs={{1,0},{2,1},{3,2},{4,3},{5,4},{6,5},{7,6},{9,8},{10,9},{11,10},{12... | collective-permute-start | bytes 33800 | tf_op jit(solution)/shard_map/ppermute | solution.py:447
  45.9 1.9 collective-permute-start.10
  47.8 19.9 %all-to-all-done.recv_ref = f32[128,56,128]{2,1,0:T(8,128)} async-done(((f32[128,56,128]{2,1,0:T(8,128)}), f32[128,56,128]{2,1,0:T(8,128)}, u32[]{:S(2)}, u32[]{:S(2)}) %all-to-all-start) | async-done | bytes 3670048 | tf_op jit(solution)/shard_map/all_to_all | solution.py:455
  67.7 3.3 %fusion.1 = s32[128,2]{1,0:T(8,128)S(1)} fusion(f32[128,56,128]{2,1,0:T(8,128)} %all-to-all-done.recv_ref), kind=kLoop, calls=%fused_computation.7 | loop fusion | flops 512 | bytes 2048 | tf_op jit(solution)/shard_map/convert_element_type | solution.py:467
  71.7 32.4 %scatter.1 = (f32[8,8,24,256]{3,2,1,0:T(8,128)}, f32[2,8,24,256]{3,2,1,0:T(8,128)}, f32[2,8,24,256]{3,2,1,0:T(8,128)}, f32[8,2,24,256]{3,2,1,0:T(8,128)}, f32[8,...) custom-call(s32[256]{0:T(256)} %reshape.22.valid_ref, ...), custom_call_target="tpu_custom_call" | custom-call | tf_op jit(solution)/shard_map/scatter/pallas_call | solution.py:158
  104.1 1.3 collective-permute-start.4
  105.4 3.8 %collective-permute-start = (f32[2,8,24,256]{3,2,1,0:T(8,128)}, f32[2,8,24,256]{3,2,1,0:T(8,128)S(1)}, u32[]{:S(2)}, u32[]{:S(2)}) collective-permute-start(f32[2,8,24,256]{3,2,1,0:T(8,128)} %get-tuple-element.17), channel_id=1, source_target_pairs={{0,8},{1,9},{2,10},{3,11},{4,12},{5,13},{6,14},{7,15},{8,16},{9,17... | collective-permute-start | bytes 1179656 | tf_op jit(solution)/shard_map/ppermute | solution.py:447
  109.2 1.3 collective-permute-start.1
  110.5 1.9 collective-permute-start.2
  112.5 2.4 %collective-permute-start.3 = (f32[8,2,24,256]{3,2,1,0:T(8,128)}, f32[8,2,24,256]{3,2,1,0:T(8,128)S(1)}, u32[]{:S(2)}, u32[]{:S(2)}) collective-permute-start(f32[8,2,24,256]{3,2,1,0:T(8,128)} %get-tuple-element.20), channel_id=1, source_target_pairs={{1,0},{2,1},{3,2},{4,3},{5,4},{6,5},{7,6},{9,8},{10,9},{11,10},{12... | collective-permute-start | bytes 1179656 | tf_op jit(solution)/shard_map/ppermute | solution.py:447
  115.0 8.2 %collective-permute-start.5 = (f32[2,2,24,256]{3,2,1,0:T(8,128)}, f32[2,2,24,256]{3,2,1,0:T(8,128)S(1)}, u32[]{:S(2)}, u32[]{:S(2)}) collective-permute-start(f32[2,2,24,256]{3,2,1,0:T(8,128)} %get-tuple-element.22), channel_id=1, source_target_pairs={{1,8},{2,9},{3,10},{4,11},{5,12},{6,13},{7,14},{9,16},{10,17},{11,... | collective-permute-start | bytes 294920 | tf_op jit(solution)/shard_map/ppermute | solution.py:447
  123.9 1.2 collective-permute-done.5.c_lh
  125.2 1.3 collective-permute-start.6
  127.1 4.2 %collective-permute-done.6.c_hl = f32[2,2,24,256]{3,2,1,0:T(8,128)S(1)} collective-permute-done((f32[2,2,24,256]{3,2,1,0:T(8,128)}, f32[2,2,24,256]{3,2,1,0:T(8,128)S(1)}, u32[]{:S(2)}, u32[]{:S(2)}) %collective-permute-start.6) | collective-permute-done | bytes 98336 | tf_op jit(solution)/shard_map/ppermute | solution.py:447
  131.3 1.3 collective-permute-start.7
  133.3 12.1 %collective-permute-done.7.c_hh = f32[2,2,24,256]{3,2,1,0:T(8,128)S(1)} collective-permute-done((f32[2,2,24,256]{3,2,1,0:T(8,128)}, f32[2,2,24,256]{3,2,1,0:T(8,128)S(1)}, u32[]{:S(2)}, u32[]{:S(2)}) %collective-permute-start.7) | collective-permute-done | bytes 98336 | tf_op jit(solution)/shard_map/ppermute | solution.py:447
  146.5 31.5 %operator.1 = (f32[8,8,24,256]{3,2,1,0:T(8,128)}, f32[8,8,24,256]{3,2,1,0:T(8,128)}, f32[128,8,128]{2,1,0:T(8,128)}) custom-call(f32[2]{0:T(128)} %add_convert_fusion.1.flag_ref, f32[8,8,24,256]{3,2,1,0:T(8,128)} %get-tuple-element.16.field, f32[2,8,24,256]{3,2,1,0:T(8,128)} %copy-done.1, f32[2,8,24,256]{3,2,1,0:T(8,128)} %copy-done.2, ...), custom_call_target="tpu_custom_call" | custom-call | tf_op jit(solution)/shard_map/operator/pallas_call | solution.py:300
  178.1 38.6 %all_to_all.10.gram_ref = f32[128,8,128]{2,1,0:T(8,128)} all-to-all(f32[128,8,128]{2,1,0:T(8,128)} %get-tuple-element.25), channel_id=1, replica_groups=mesh['gz'=16,'gy'=8] {'gz','gy'}, dimensions={0} | all-to-all | bytes 1048576 | tf_op jit(solution)/shard_map/all_to_all | solution.py:482
  216.7 12.7 %final.1 = (f32[1536,256]{1,0:T(8,128)}, f32[1536,256]{1,0:T(8,128)}) custom-call(f32[128,8,128]{2,1,0:T(8,128)} %all_to_all.10.gram_ref, f32[8,8,24,256]{3,2,1,0:T(8,128)} %get-tuple-element.16.field, f32[8,8,24,256]{3,2,1,0:T(8,128)} %get-tuple-element.26.s_ref, f32[8,8,24,256]{3,2,1,0:T(8,128)} %get-tuple-element.27.q_ref), custom_call_target="tpu_custom_call" | custom-call | tf_op jit(solution)/shard_map/final/pallas_call | solution.py:429
  (46 shorter events, 4.8 us)
Async XLA Ops:
  8.8 11.9 %copy-start.5 = (s32[8,8,256]{2,1,0:T(8,128)S(1)}, s32[8,8,256]{2,1,0:T(8,128)}, u32[]{:S(2)}) copy-start(s32[8,8,256]{2,1,0:T(8,128)} %param.10) | copy-start | bytes 196612
  8.8 17.3 %copy-start.10 = (f32[24,24]{1,0:T(8,128)S(1)}, f32[24,24]{1,0:T(8,128)}, u32[]{:S(2)}) copy-start(f32[24,24]{1,0:T(8,128)} %param.11) | copy-start | bytes 6916
  8.8 58.9 %all-to-all-start = ((f32[128,56,128]{2,1,0:T(8,128)}), f32[128,56,128]{2,1,0:T(8,128)}, u32[]{:S(2)}, u32[]{:S(2)}) async-start(f32[128,56,128]{2,1,0:T(8,128)} %pack.1), calls=%async_computation | async-start | bytes 7340032 | tf_op jit(solution)/shard_map/all_to_all | solution.py:455
  20.7 6.3 %collective-permute-start.9 = (s32[1,8,256]{2,1,0:T(8,128)S(1)}, s32[1,8,256]{2,1,0:T(8,128)S(1)}, u32[]{:S(2)}, u32[]{:S(2)}) collective-permute-start(s32[1,8,256]{2,1,0:T(8,128)S(1)} %slice.17), channel_id=1, source_target_pairs={{8,0},{9,1},{10,2},{11,3},{12,4},{13,5},{14,6},{15,7},{16,8},{17,9... | collective-permute-start | bytes 24584 | tf_op jit(solution)/shard_map/ppermute | solution.py:447
  22.0 4.9 %collective-permute-start.8 = (s32[2,8,256]{2,1,0:T(8,128)S(1)}, s32[2,8,256]{2,1,0:T(8,128)S(1)}, u32[]{:S(2)}, u32[]{:S(2)}) collective-permute-start(s32[2,8,256]{2,1,0:T(8,128)S(1)} %slice.16), channel_id=1, source_target_pairs={{0,8},{1,9},{2,10},{3,11},{4,12},{5,13},{6,14},{7,15},{8,16},{9,17... | collective-permute-start | bytes 49160 | tf_op jit(solution)/shard_map/ppermute | solution.py:447
  27.0 83.5 %collective-permute-start.11 = (s32[11,1,256]{2,1,0:T(1,128)S(1)}, s32[11,1,256]{2,1,0:T(1,128)S(1)}, u32[]{:S(2)}, u32[]{:S(2)}) collective-permute-start(s32[11,1,256]{2,1,0:T(1,128)S(1)} %slice.22), channel_id=1, source_target_pairs={{1,0},{2,1},{3,2},{4,3},{5,4},{6,5},{7,6},{9,8},{10,9},{11,10},{12... | collective-permute-start | bytes 33800 | tf_op jit(solution)/shard_map/ppermute | solution.py:447
  45.9 66.6 %collective-permute-start.10 = (s32[11,2,256]{2,1,0:T(2,128)S(1)}, s32[11,2,256]{2,1,0:T(2,128)S(1)}, u32[]{:S(2)}, u32[]{:S(2)}) collective-permute-start(s32[11,2,256]{2,1,0:T(2,128)S(1)} %slice.21), channel_id=1, source_target_pairs={{0,1},{1,2},{2,3},{3,4},{4,5},{5,6},{6,7},{8,9},{9,10},{10,11},{11... | collective-permute-start | bytes 67592 | tf_op jit(solution)/shard_map/ppermute | solution.py:447
  104.1 10.9 %collective-permute-start.4 = (f32[2,2,24,256]{3,2,1,0:T(8,128)}, f32[2,2,24,256]{3,2,1,0:T(8,128)S(1)}, u32[]{:S(2)}, u32[]{:S(2)}) collective-permute-start(f32[2,2,24,256]{3,2,1,0:T(8,128)} %get-tuple-element.21), channel_id=1, source_target_pairs={{0,9},{1,10},{2,11},{3,12},{4,13},{5,14},{6,15},{8,17},{9,18},{10,... | collective-permute-start | bytes 294920 | tf_op jit(solution)/shard_map/ppermute | solution.py:447
  105.4 40.0 %collective-permute-start = (f32[2,8,24,256]{3,2,1,0:T(8,128)}, f32[2,8,24,256]{3,2,1,0:T(8,128)S(1)}, u32[]{:S(2)}, u32[]{:S(2)}) collective-permute-start(f32[2,8,24,256]{3,2,1,0:T(8,128)} %get-tuple-element.17), channel_id=1, source_target_pairs={{0,8},{1,9},{2,10},{3,11},{4,12},{5,13},{6,14},{7,15},{8,16},{9,17... | collective-permute-start | bytes 1179656 | tf_op jit(solution)/shard_map/ppermute | solution.py:447
  109.2 36.1 %collective-permute-start.1 = (f32[2,8,24,256]{3,2,1,0:T(8,128)}, f32[2,8,24,256]{3,2,1,0:T(8,128)S(1)}, u32[]{:S(2)}, u32[]{:S(2)}) collective-permute-start(f32[2,8,24,256]{3,2,1,0:T(8,128)} %get-tuple-element.18), channel_id=1, source_target_pairs={{8,0},{9,1},{10,2},{11,3},{12,4},{13,5},{14,6},{15,7},{16,8},{17,9... | collective-permute-start | bytes 1179656 | tf_op jit(solution)/shard_map/ppermute | solution.py:447
  110.5 34.9 %collective-permute-start.2 = (f32[8,2,24,256]{3,2,1,0:T(8,128)}, f32[8,2,24,256]{3,2,1,0:T(8,128)S(1)}, u32[]{:S(2)}, u32[]{:S(2)}) collective-permute-start(f32[8,2,24,256]{3,2,1,0:T(8,128)} %get-tuple-element.19), channel_id=1, source_target_pairs={{0,1},{1,2},{2,3},{3,4},{4,5},{5,6},{6,7},{8,9},{9,10},{10,11},{11... | collective-permute-start | bytes 1179656 | tf_op jit(solution)/shard_map/ppermute | solution.py:447
  112.5 32.9 %collective-permute-start.3 = (f32[8,2,24,256]{3,2,1,0:T(8,128)}, f32[8,2,24,256]{3,2,1,0:T(8,128)S(1)}, u32[]{:S(2)}, u32[]{:S(2)}) collective-permute-start(f32[8,2,24,256]{3,2,1,0:T(8,128)} %get-tuple-element.20), channel_id=1, source_target_pairs={{1,0},{2,1},{3,2},{4,3},{5,4},{6,5},{7,6},{9,8},{10,9},{11,10},{12... | collective-permute-start | bytes 1179656 | tf_op jit(solution)/shard_map/ppermute | solution.py:447
  115.0 30.5 %copy-start = (bf16[192,192]{1,0:T(8,128)(2,1)}, bf16[192,192]{1,0:T(8,128)(2,1)S(1)}, u32[]{:S(2)}) copy-start(bf16[192,192]{1,0:T(8,128)(2,1)S(1)} %get-tuple-element.30.k_high) | copy-start | bytes 221188
  115.0 30.5 %copy-start.6 = (f32[2,2,24,256]{3,2,1,0:T(8,128)}, f32[2,2,24,256]{3,2,1,0:T(8,128)S(1)}, u32[]{:S(2)}) copy-start(f32[2,2,24,256]{3,2,1,0:T(8,128)S(1)} %collective-permute-done.4.c_ll) | copy-start | bytes 294916
  115.0 10.2 %collective-permute-start.5 = (f32[2,2,24,256]{3,2,1,0:T(8,128)}, f32[2,2,24,256]{3,2,1,0:T(8,128)S(1)}, u32[]{:S(2)}, u32[]{:S(2)}) collective-permute-start(f32[2,2,24,256]{3,2,1,0:T(8,128)} %get-tuple-element.22), channel_id=1, source_target_pairs={{1,8},{2,9},{3,10},{4,11},{5,12},{6,13},{7,14},{9,16},{10,17},{11,... | collective-permute-start | bytes 294920 | tf_op jit(solution)/shard_map/ppermute | solution.py:447
  125.2 20.3 %copy-start.7 = (f32[2,2,24,256]{3,2,1,0:T(8,128)}, f32[2,2,24,256]{3,2,1,0:T(8,128)S(1)}, u32[]{:S(2)}) copy-start(f32[2,2,24,256]{3,2,1,0:T(8,128)S(1)} %collective-permute-done.5.c_lh) | copy-start | bytes 294916
  125.2 6.1 %collective-permute-start.6 = (f32[2,2,24,256]{3,2,1,0:T(8,128)}, f32[2,2,24,256]{3,2,1,0:T(8,128)S(1)}, u32[]{:S(2)}, u32[]{:S(2)}) collective-permute-start(f32[2,2,24,256]{3,2,1,0:T(8,128)} %get-tuple-element.23), channel_id=1, source_target_pairs={{8,1},{9,2},{10,3},{11,4},{12,5},{13,6},{14,7},{16,9},{17,10},{18,... | collective-permute-start | bytes 294920 | tf_op jit(solution)/shard_map/ppermute | solution.py:447
  131.3 14.2 %copy-start.8 = (f32[2,2,24,256]{3,2,1,0:T(8,128)}, f32[2,2,24,256]{3,2,1,0:T(8,128)S(1)}, u32[]{:S(2)}) copy-start(f32[2,2,24,256]{3,2,1,0:T(8,128)S(1)} %collective-permute-done.6.c_hl) | copy-start | bytes 294916
  131.3 14.1 %collective-permute-start.7 = (f32[2,2,24,256]{3,2,1,0:T(8,128)}, f32[2,2,24,256]{3,2,1,0:T(8,128)S(1)}, u32[]{:S(2)}, u32[]{:S(2)}) collective-permute-start(f32[2,2,24,256]{3,2,1,0:T(8,128)} %get-tuple-element.24), channel_id=1, source_target_pairs={{9,0},{10,1},{11,2},{12,3},{13,4},{14,5},{15,6},{17,8},{18,9},{19,... | collective-permute-start | bytes 294920 | tf_op jit(solution)/shard_map/ppermute | solution.py:447
  145.4 0.6 copy-start.9
  145.4 0.8 copy-start.1
  145.4 0.9 copy-start.2
  145.4 1.0 copy-start.3
  145.4 1.1 copy-start.4

commit v2 on v1

v2 whole, which is shorter than its diff:
```python
import functools
import jax
import jax.numpy as jnp
from jax import lax
from jax.experimental import pallas as pl
from jax.experimental.pallas import tpu as pltpu
from jax.sharding import PartitionSpec as P

LOADS = 8
CH = 24
GROUP = 4
AXES = ("gz", "gy")
SPRING = 0.5
F32 = jnp.float32
BF16 = jnp.bfloat16
VMEM_LIMIT = 60 * 1024 * 1024


def vmem():
    return pl.BlockSpec(memory_space=pltpu.VMEM)


def smem():
    return pl.BlockSpec(memory_space=pltpu.SMEM)


def pack_kernel(with_ids, owner_ref, live_ref, voxel_ref, force_ref, out_ref, count_ref):
    devices = out_ref.shape[0]
    blocks, width = force_ref.shape[0], force_ref.shape[1]
    lane = lax.broadcasted_iota(jnp.int32, (8, 128), 1)

    def clear(i, carry):
        count_ref[i] = 0
        if with_ids:
            out_ref[i, 2 * width : 2 * width + 8, :] = jnp.full((8, 128), -1.0, F32)
        return carry

    lax.fori_loop(0, devices, clear, 0, unroll=8)
    live = live_ref[...]

    def one(p, carry):
        owner = owner_ref[p]
        rank = count_ref[owner]
        count_ref[owner] = rank + 1
        limit = jnp.sum(jnp.where(lane == p, live, 0.0), axis=1, keepdims=True)
        keep = lane.astype(F32) < limit
        for k in range(0, width, 8):
            base = pl.multiple_of(rank * width + k, 8)
            out_ref[owner, pl.ds(base, 8), :] = jnp.where(keep, force_ref[p, k : k + 8, :], 0.0)
        if with_ids:
            out_ref[owner, pl.ds(2 * width + rank, 1), :] = voxel_ref[pl.ds(p, 1), :].astype(F32)
        return carry

    lax.fori_loop(0, blocks, one, 0, unroll=8)


def pack(owner, live_t, voxel, force, devices, width, place, with_ids):
    blocks = force.shape[0]
    rows = 2 * width + (8 if with_ids else 0)
    return pl.pallas_call(
        functools.partial(pack_kernel, with_ids),
        out_shape=jax.ShapeDtypeStruct((devices, rows, 128), F32),
        grid=(1,),
        in_specs=[
            smem(),
            pl.BlockSpec(live_t.shape, lambda i: (0, 0)),
            pl.BlockSpec(voxel.shape, lambda i: (0, 0)),
            pl.BlockSpec((blocks, width, 128), lambda i: (0, place, 0)),
        ],
        out_specs=pl.BlockSpec((devices, rows, 128), lambda i: (0, 0, 0)),
        scratch_shapes=[pltpu.SMEM((devices,), jnp.int32)],
        compiler_params=pltpu.CompilerParams(vmem_limit_bytes=VMEM_LIMIT),
        name="pack",
    )(owner, live_t, voxel, force)


def add_blocks(count, list_ref, ids_ref, value_of, width, left_ref, right_ref, acc_ref):
    acc_ref[...] = jnp.zeros_like(acc_ref)
    row_x = lax.broadcasted_iota(jnp.int32, (256, 128), 0)
    row_zy = lax.broadcasted_iota(jnp.int32, (64, 128), 0)

    def group(g, carry):
        for j in range(GROUP):
            place = g * GROUP + j
            index = list_ref[jnp.minimum(place, count - 1)]
            source = index & 127
            rank = index >> 7
            ids = ids_ref[rank, pl.ds(source, 1), :]
            zy = jnp.where(place < count, ids >> 8, -1)
            x = ids & 255
            hot_x = jnp.where(row_x == x, 1.0, 0.0).astype(BF16)
            right_ref[:, j * 256 : j * 256 + 128] = hot_x
            right_ref[:, j * 256 + 128 : (j + 1) * 256] = hot_x
            hot_zy = jnp.where(row_zy == zy, 1.0, 0.0).astype(BF16)
            value = value_of(source, rank)
            high = value.astype(BF16).astype(F32)
            low = value - high
            for c in range(width):
                for half, part in enumerate((high, low)):
                    line = jnp.broadcast_to(part[c : c + 1, :], (16, 128)).astype(BF16)
                    tile = jnp.concatenate([line] * 4, axis=0) * hot_zy
                    at = j * 256 + half * 128
                    left_ref[c * 64 : (c + 1) * 64, at : at + 128] = tile
        for m in range(width // 8):
            part = lax.dot_general(
                left_ref[m * 512 : (m + 1) * 512, :],
                right_ref[...],
                (((1,), (1,)), ((), ())),
                preferred_element_type=F32,
            )
            for h in range(2):
                acc_ref[h, m * 512 : (m + 1) * 512, :] += part[:, h * 128 : (h + 1) * 128]
        return carry

    lax.fori_loop(0, (count + GROUP - 1) // GROUP, group, 0)


def node_of(acc_ref, width, z, y):
    return jnp.concatenate(
        [
            jnp.concatenate(
                [acc_ref[h, pl.ds(k * 64 + z * 8 + y, 8, stride=64), :] for k in range(0, width, 8)], axis=0
            )
            for h in range(2)
        ],
        axis=1,
    )


def scatter_first_kernel(
    recv_ref, field, list_out, ids_out, flag_v, flag_s, left_ref, right_ref, acc_ref, sem
):
    width = 8
    rows = 2 * width + 8
    lane = lax.broadcasted_iota(jnp.int32, (8, 128), 1)
    for rank in range(2):
        flags = jnp.zeros((8, 128), jnp.int32)
        for t in range(16):
            ids = recv_ref[pl.ds(t * 8 * rows + 2 * width + rank, 8, stride=rows), :].astype(jnp.int32)
            ids_out[rank, t * 8 : (t + 1) * 8, :] = ids
            flags = jnp.where(lane == t, jnp.where(ids[:, 0:1] >= 0, 1, 0), flags)
        flag_v[rank * 8 : (rank + 1) * 8, :] = flags
    copy = pltpu.make_async_copy(flag_v, flag_s, sem)
    copy.start()
    copy.wait()

    count = jnp.int32(0)
    for rank in range(2):

        def collect(t, n):
            for s in range(8):
                list_out[n] = rank * 128 + t * 8 + s
                n = n + flag_s[rank * 8 + s, t]
            return n

        count = lax.fori_loop(0, 16, collect, count)
    list_out[list_out.shape[0] - 1] = count

    def value_of(source, rank):
        return recv_ref[pl.ds(pl.multiple_of(source * rows + rank * width, 8), width), :]

    add_blocks(count, list_out, ids_out, value_of, width, left_ref, right_ref, acc_ref)
    for z in range(8):
        for y in range(8):
            field[z, y] = node_of(acc_ref, width, z, y)


def scatter_first(recv):
    devices = recv.shape[0]
    return pl.pallas_call(
        scatter_first_kernel,
        out_shape=[
            jax.ShapeDtypeStruct((8, 8, 8, 256), F32),
            jax.ShapeDtypeStruct((2 * devices + 8,), jnp.int32),
            jax.ShapeDtypeStruct((2, devices, 128), jnp.int32),
        ],
        in_specs=[vmem()],
        out_specs=[vmem(), smem(), vmem()],
        scratch_shapes=[
            pltpu.VMEM((16, 128), jnp.int32),
            pltpu.SMEM((16, 128), jnp.int32),
            pltpu.VMEM((512, GROUP * 256), BF16),
            pltpu.VMEM((256, GROUP * 256), BF16),
            pltpu.VMEM((2, 512, 128), F32),
            pltpu.SemaphoreType.DMA,
        ],
        compiler_params=pltpu.CompilerParams(vmem_limit_bytes=VMEM_LIMIT),
        name="scatter_first",
    )(recv.reshape(-1, 128))


def scatter_second_kernel(
    list_ref, ids_ref, recv_ref, part_ref, field, z_low, z_high, y_low, y_high, left_ref, right_ref, acc_ref
):
    width = 16
    count = list_ref[list_ref.shape[0] - 1]

    def value_of(source, rank):
        return recv_ref[source, pl.ds(pl.multiple_of(rank * width, 8), width), :]

    add_blocks(count, list_ref, ids_ref, value_of, width, left_ref, right_ref, acc_ref)
    for z in range(8):
        for y in range(8):
            node = jnp.concatenate([node_of(acc_ref, width, z, y), part_ref[z, y]], axis=0)
            field[z, y] = node
            if z < 2:
                z_low[z, y] = node
            if z > 5:
                z_high[z - 6, y] = node
            if y < 2:
                y_low[z, y] = node
            if y > 5:
                y_high[z, y - 6] = node


def scatter_second(blocks, ids, recv, part):
    def shape(a, b):
        return jax.ShapeDtypeStruct((a, b, CH, 256), F32)

    return pl.pallas_call(
        scatter_second_kernel,
        out_shape=[shape(8, 8), shape(2, 8), shape(2, 8), shape(8, 2), shape(8, 2)],
        in_specs=[smem(), vmem(), vmem(), vmem()],
        out_specs=[vmem()] * 5,
        scratch_shapes=[
            pltpu.VMEM((1024, GROUP * 256), BF16),
            pltpu.VMEM((256, GROUP * 256), BF16),
            pltpu.VMEM((2, 1024, 128), F32),
        ],
        compiler_params=pltpu.CompilerParams(vmem_limit_bytes=VMEM_LIMIT),
        name="scatter_second",
    )(blocks, ids, recv, part)


def shift_down(v, lane):
    return jnp.where(lane == 255, 0.0, pltpu.roll(v, 255, axis=1))


def shift_up(v, lane):
    return jnp.where(lane == 0, 0.0, pltpu.roll(v, 1, axis=1))


def operator_kernel(
    flag_ref, field, z_low, z_high, y_low, y_high, mask_ref, k_both, k_high,
    s_out, q_out, gram_out,
    v32, vh, vl, s32, sh, sl, carry_ref, gram_ref,
):
    lane = lax.broadcasted_iota(jnp.int32, (CH, 256), 1)

    def put(full, high, low, z, y, v):
        full[z, y * CH : (y + 1) * CH, :] = v
        both = jnp.concatenate([v, shift_down(v, lane)], axis=0)
        top = both.astype(BF16)
        high[z, y * 48 : (y + 1) * 48, :] = top
        low[z, y * 48 : (y + 1) * 48, :] = (both - top.astype(F32)).astype(BF16)

    def rows(source, z_count, y_count, z_at, y_at):
        def one(z, carry):
            for y in range(y_count):
                put(v32, vh, vl, z + z_at, y + y_at, source[z, y])
            return carry

        lax.fori_loop(0, z_count, one, 0)

    rows(z_low, 2, 8, 0, 2)
    rows(field, 8, 8, 2, 2)
    rows(z_high, 2, 8, 10, 2)
    rows(y_low, 12, 2, 0, 0)
    rows(y_high, 12, 2, 0, 10)

    def element(high, low, ez, ey):
        def gather(ref):
            return jnp.concatenate(
                [ref[ez, ey * 48 : (ey + 2) * 48, :], ref[ez + 1, ey * 48 : (ey + 2) * 48, :]], axis=0
            )

        first = jnp.dot(k_both[...], gather(high), preferred_element_type=F32)
        second = jnp.dot(k_high[...], gather(low), preferred_element_type=F32)
        force = first[:192] + first[192:] + second
        return force * mask_ref[ez, ey : ey + 1, :]

    def layer(high, low, full, ez, start, stop, finish):
        before = None
        for ey in range(start, stop):
            force = element(high, low, ez, ey)
            if ey > start:
                lower = before[0] + force[0:48] + carry_ref[ey]
                carry_ref[ey] = before[1] + force[96:144]
                value = lower[:CH] + shift_up(lower[CH:], lane)
                finish(ey, value + SPRING * full[ez, ey * CH : (ey + 1) * CH, :])
            before = (force[48:96], force[144:192])

    carry_ref[...] = jnp.zeros_like(carry_ref)

    def first_pass(ez, carry):
        inside = jnp.where(ez == 10, flag_ref[0], 1.0)

        def finish(n, value):
            keep = inside * flag_ref[1] if n == 10 else inside
            put(s32, sh, sl, ez, n, value * keep)

        layer(vh, vl, v32, ez, 0, 11, finish)
        return carry

    lax.fori_loop(0, 11, first_pass, 0)
    carry_ref[...] = jnp.zeros_like(carry_ref)

    def second_pass(ez, carry):
        def finish(n, value):
            q_out[jnp.maximum(ez - 2, 0), n - 2] = value

        layer(sh, sl, s32, ez, 1, 10, finish)
        return carry

    lax.fori_loop(1, 10, second_pass, 0)

    gram_ref[...] = jnp.zeros_like(gram_ref)

    def products(z, carry):
        sums = [None] * 20
        for y in range(8):
            r_row = field[z, y]
            s_row = s32[z + 2, (y + 2) * CH : (y + 3) * CH, :]
            q_row = q_out[z, y]
            s_out[z, y] = s_row
            for k in range(3):
                for h in range(2):
                    r, s, q = (t[k * 8 : (k + 1) * 8, h * 128 : (h + 1) * 128] for t in (r_row, s_row, q_row))
                    for j in range(5):
                        if j == 0:
                            rj, sj, qj = r, s, q
                        else:
                            rj, sj, qj = (pltpu.roll(t, 8 - j, axis=0) for t in (r, s, q))
                        for n, term in enumerate((r * rj, r * sj, s * sj, s * qj)):
                            at = n * 5 + j
                            sums[at] = term if sums[at] is None else sums[at] + term
        for at in range(20):
            gram_ref[at] += sums[at]
        return carry

    lax.fori_loop(0, 8, products, 0)
    spot = lax.broadcasted_iota(jnp.int32, (8, 128), 1) - 16 * lax.broadcasted_iota(jnp.int32, (8, 128), 0)
    packed = [jnp.zeros((8, 128), F32)] * 2
    for at in range(20):
        total = jnp.sum(gram_ref[at], axis=1, keepdims=True)
        packed[at // 16] = packed[at // 16] + jnp.where(spot == at % 16, total, 0.0)
    for h in range(2):
        line = jnp.sum(packed[h], axis=0, keepdims=True)
        gram_out[:, h * 128 : (h + 1) * 128] = jnp.broadcast_to(line, (gram_out.shape[0], 128))


def operator(flags, fields, mask, k_both, k_high, devices):
    node = jax.ShapeDtypeStruct((8, 8, CH, 256), F32)
    return pl.pallas_call(
        operator_kernel,
        out_shape=[node, node, jax.ShapeDtypeStruct((devices, 256), F32)],
        in_specs=[smem()] + [vmem()] * 8,
        out_specs=[vmem()] * 3,
        scratch_shapes=[
            pltpu.VMEM((12, 12 * CH, 256), F32),
            pltpu.VMEM((12, 12 * 48, 256), BF16),
            pltpu.VMEM((12, 12 * 48, 256), BF16),
            pltpu.VMEM((11, 11 * CH, 256), F32),
            pltpu.VMEM((11, 11 * 48, 256), BF16),
            pltpu.VMEM((11, 11 * 48, 256), BF16),
            pltpu.VMEM((11, 48, 256), F32),
            pltpu.VMEM((20, 8, 128), F32),
        ],
        compiler_params=pltpu.CompilerParams(vmem_limit_bytes=VMEM_LIMIT),
        name="operator",
    )(flags, *fields, mask, k_both, k_high)


def final_kernel(
    gram_ref, r_hbm, s_hbm, q_hbm, u_hbm, e_hbm, r_ref, s_ref, q_ref, u_half, e_half, in_sem, out_sem
):
    pairs = ((r_hbm, r_ref), (s_hbm, s_ref), (q_hbm, q_ref))
    loads = [
        [pltpu.make_async_copy(far.at[z], near.at[z], in_sem.at[n, z]) for n, (far, near) in enumerate(pairs)]
        for z in range(8)
    ]
    for z in range(8):
        for n in range(3):
            loads[z][n].start()

    sub = lax.broadcasted_iota(jnp.int32, (8, 128), 0)
    lane = lax.broadcasted_iota(jnp.int32, (8, 128), 1)
    inside = lane < 8
    total = [
        jnp.broadcast_to(jnp.sum(gram_ref[:, h * 128 : (h + 1) * 128], axis=0, keepdims=True), (8, 128))
        for h in range(2)
    ]

    def entry(at, turn):
        here = lane == ((sub - turn) & 7) * 16 + at % 16
        return jnp.sum(jnp.where(here, total[at // 16], 0.0), axis=1, keepdims=True)

    def column(m, j):
        return jnp.sum(jnp.where(lane == j, m, 0.0), axis=1, keepdims=True)

    def row(m, i):
        return jnp.sum(jnp.where(sub == i, m, 0.0), axis=0, keepdims=True)

    def unpack(base):
        out = jnp.zeros((8, 128), F32)
        for j in range(5):
            out = jnp.where(inside & (((lane - sub) & 7) == j), entry(base + j, 0), out)
            if 0 < j < 4:
                out = jnp.where(inside & (((sub - lane) & 7) == j), entry(base + j, j), out)
        return out

    def mul(a, b):
        out = jnp.zeros((8, 128), F32)
        for i in range(8):
            out = out + column(a, i) * row(b, i)
        return out

    def flip(a):
        out = jnp.zeros((8, 128), F32)
        for i in range(8):
            out = jnp.where(lane == i, jnp.sum(jnp.where(lane == sub, row(a, i), 0.0), axis=1, keepdims=True), out)
        return out

    def solve(m, b):
        for i in range(8):
            pivot_row = row(m, i)
            scale = 1.0 / column(pivot_row, i)
            pivot_b = row(b, i) * scale
            pivot_row = pivot_row * scale
            factor = jnp.where(sub == i, 0.0, column(m, i))
            m = jnp.where(sub == i, pivot_row, m - factor * pivot_row)
            b = jnp.where(sub == i, pivot_b, b - factor * pivot_b)
        return b

    rr, w, ss, tt = (unpack(5 * n) for n in range(4))
    alpha = solve(w, rr)
    alpha_t = flip(alpha)
    w_alpha = mul(w, alpha)
    s_alpha = mul(ss, alpha)
    new = rr - w_alpha - flip(w_alpha) + mul(alpha_t, s_alpha)
    beta = solve(rr, new)
    one_beta = beta + jnp.where(lane == sub, 1.0, 0.0)
    turn = flip(one_beta)
    cross = mul(turn, s_alpha)
    w2 = mul(turn, mul(w, one_beta)) - cross - flip(cross) + mul(alpha_t, mul(tt, alpha))
    alpha2 = solve(0.5 * (w2 + flip(w2)), new)
    p_mat = alpha + mul(one_beta, alpha2)
    q_mat = mul(alpha, alpha2)

    wide = lax.broadcasted_iota(jnp.int32, (8, 256), 1)
    segment = wide // 72
    block = (wide - segment * 72) // 8

    def spread(mat):
        turned = flip(mat)
        out = jnp.zeros((8, 256), F32)
        for i in range(8):
            out = jnp.where((wide & 7) == i, column(turned, i), out)
        return out

    p_all, q_all = spread(p_mat), spread(q_mat)
    bands = [
        jnp.where(block == k, p_all, jnp.where(block == 3 + k, -q_all, 0.0)) for k in range(3)
    ] + [jnp.where(block == 3 + k, -p_all, jnp.where(block == 6 + k, q_all, 0.0)) for k in range(3)]
    exact = jnp.concatenate(bands, axis=0)
    segment = lax.broadcasted_iota(jnp.int32, (48, 256), 1) // 72
    high = exact.astype(BF16).astype(F32)
    factor = jnp.where(segment < 2, high, jnp.where(segment == 2, exact - high, 0.0))
    factor = factor[:, :216].astype(BF16)

    stores = []
    for z in range(8):
        for n in range(3):
            loads[z][n].wait()

        for y in range(8):
            r = r_ref[z, y]
            stack = jnp.concatenate([r, s_ref[z, y], q_ref[z, y]], axis=0)
            top = stack.astype(BF16)
            rest = (stack - top.astype(F32)).astype(BF16)
            both = jnp.dot(
                factor, jnp.concatenate([top, rest, top], axis=0), preferred_element_type=F32
            )
            for h in range(2):
                side = slice(h * 128, (h + 1) * 128)
                for k in range(3):
                    at = pl.ds(k * 64 + y, 8, stride=8)
                    u_half[z, h, at, :] = both[k * 8 : (k + 1) * 8, side]
                    e_half[z, h, at, :] = (
                        r[k * 8 : (k + 1) * 8, side] + both[24 + k * 8 : 32 + k * 8, side]
                    )
        for n, (half, far) in enumerate(((u_half, u_hbm), (e_half, e_hbm))):
            for h in range(2):
                copy = pltpu.make_async_copy(
                    half.at[z, h].reshape(CH, 8, 128),
                    far.at[:, z, :, h * 128 : (h + 1) * 128],
                    out_sem.at[n, z, h],
                )
                copy.start()
                stores.append(copy)
    for copy in stores:
        copy.wait()


def final(gram, field, s, q):
    out = jax.ShapeDtypeStruct((CH, 8, 8, 256), F32)
    far = pl.BlockSpec(memory_space=pl.ANY)
    return pl.pallas_call(
        final_kernel,
        out_shape=[out, out],
        in_specs=[vmem()] + [far] * 3,
        out_specs=[far] * 2,
        scratch_shapes=[pltpu.VMEM((8, 8, CH, 256), F32)] * 3
        + [pltpu.VMEM((8, 2, CH * 8, 128), F32)] * 2
        + [pltpu.SemaphoreType.DMA((3, 8)), pltpu.SemaphoreType.DMA((2, 8, 2))],
        compiler_params=pltpu.CompilerParams(vmem_limit_bytes=VMEM_LIMIT),
        name="final",
    )(gram, field, s, q)


def moved(value, axis, step):
    count = lax.axis_size(axis)
    return lax.ppermute(
        value, axis, [(i, i + step) for i in range(count) if 0 <= i + step < count]
    )


def exchange(value):
    return lax.all_to_all(value, AXES, split_axis=0, concat_axis=0, tiled=True)


def body(patch_force, patch_owner, patch_voxel, patch_live, voxel_mask, element_matrix):
    nz, ny = lax.axis_size("gz"), lax.axis_size("gy")
    devices = nz * ny

    live_t = patch_live.astype(F32).T
    packed = functools.partial(pack, patch_owner, live_t, patch_voxel, patch_force, devices)
    first = exchange(packed(8, 2, True))
    second = exchange(packed(16, 0, False))

    mask = voxel_mask
    mask = jnp.concatenate([moved(mask[6:8], "gz", 1), mask, moved(mask[0:1], "gz", -1)], axis=0)
    mask = jnp.concatenate([moved(mask[:, 6:8], "gy", 1), mask, moved(mask[:, 0:1], "gy", -1)], axis=1)
    mask = mask.astype(F32)

    big = jnp.einsum("ij,lm->iljm", element_matrix, jnp.eye(LOADS, dtype=F32)).reshape(192, 192)
    rounded = lax.reduce_precision(big, 8, 7)
    k_high = rounded.astype(BF16)
    k_both = jnp.concatenate([k_high, (big - rounded).astype(BF16)], axis=0)
    flags = jnp.stack([lax.axis_index("gz") + 1 < nz, lax.axis_index("gy") + 1 < ny]).astype(F32)

    part, blocks, ids = scatter_first(first)
    field, z_low, z_high, y_low, y_high = scatter_second(blocks, ids, second, part)
    below, above = moved(z_high, "gz", 1), moved(z_low, "gz", -1)
    y_low = jnp.concatenate([below[:, 0:2], y_low, above[:, 0:2]], axis=0)
    y_high = jnp.concatenate([below[:, 6:8], y_high, above[:, 6:8]], axis=0)
    around = (field, below, above, moved(y_high, "gy", 1), moved(y_low, "gy", -1))
    s, q, gram = operator(flags, around, mask, k_both, k_high, devices)
    return final(exchange(gram), field, s, q)


def solution(mesh):
    placed = (
        P(AXES, None, None),
        P(AXES),
        P(AXES, None),
        P(AXES, None),
        P("gz", "gy", None),
        P(),
    )
    return jax.shard_map(
        body,
        mesh=mesh,
        in_specs=placed,
        out_specs=(P(None, "gz", "gy", None), P(None, "gz", "gy", None)),
        check_vma=False,
    )
```

time: 231 us -> 212 us (0.918)
  starting transfers between devices: 59.5 us -> 42 us
  waiting for transfers between devices: 37.4 us -> 42 us
  local copies, waits for them, and re-layouts: 2.54 us -> 5.96 us
  other arithmetic: 6.84 us -> 3.64 us
    ppermute x12 -> x8, starting transfers between devices: 47.6 us -> 26.1 us  [moved(): lax.ppermute(value, axis, [(i, i + step) for i in range(count) if 0 <= i...]
    all_to_all x1 -> x2, waiting for transfers between devices: 19.9 us -> 30.7 us  [exchange(): return lax.all_to_all(value, AXES, split_axis=0, concat_axis=0, tiled=True)]
    ppermute x12 -> x8, waiting for transfers between devices: 17.5 us -> 11.3 us  [moved(): lax.ppermute(value, axis, [(i, i + step) for i in range(count) if 0 <= i...]
    all_to_all x1 -> x2, starting transfers between devices: 11.9 us -> 15.9 us  [exchange(): return lax.all_to_all(value, AXES, split_axis=0, concat_axis=0, tiled=True)]
    convert_element_type x1 -> x0, other arithmetic: 3.28 us -> none  [body(): valid = (recv[:, 48:50, 0] >= 0).astype(jnp.int32).reshape(-1)]
    unnamed x24 -> x25, local copies, waits for them, and re-layouts: 1.11 us -> 4.19 us
    pallas_call x3 -> x5, Pallas kernels: 52 us -> 50.4 us  [the longest x1 20.5 us: scatter_second(): pl.pallas_call(scatter_second_kernel, out_shape=[shape(8, 8), shape(2, 8)...]
  transfers between devices with their start and end apart: 13 -> 10, of which waited for: 4 -> 5; matrix products, arithmetic and copies ran while one was open for 3% -> 1% of each run, Pallas kernels for 14% -> 19%
where the time goes in v2:
time: 212 us
  Pallas kernels  81.3 us (38%)
  starting transfers between devices  42 us (20%)
  waiting for transfers between devices  42 us (20%)
  blocking collectives  36.5 us (17%)
  local copies, waits for them, and re-layouts  5.96 us (3%)
  other arithmetic  3.64 us (2%)
    all_to_all x1, blocking collectives, exchange(): return lax.all_to_all(value, AXES, split_axis=0, concat_axis=0, tiled=True)  36.5 us
    pallas_call x1, Pallas kernels, operator(): pl.pallas_call(operator_kernel, out_shape=[node, node, jax.ShapeDtypeStru...  30.9 us
    all_to_all x2, waiting for transfers between devices, exchange(): return lax.all_to_all(value, AXES, split_axis=0, concat_axis=0, tiled=True)  30.7 us
    ppermute x8, starting transfers between devices, moved(): lax.ppermute(value, axis, [(i, i + step) for i in range(count) if 0 <= i...  26.1 us
    pallas_call x1, Pallas kernels, scatter_second(): pl.pallas_call(scatter_second_kernel, out_shape=[shape(8, 8), shape(2, 8)...  20.5 us
    all_to_all x2, starting transfers between devices, exchange(): return lax.all_to_all(value, AXES, split_axis=0, concat_axis=0, tiled=True)  15.9 us
    pallas_call x1, Pallas kernels, scatter_first(): pl.pallas_call(scatter_first_kernel, out_shape=[jax.ShapeDtypeStruct((8,...  15.1 us
    ppermute x8, waiting for transfers between devices, moved(): lax.ppermute(value, axis, [(i, i + step) for i in range(count) if 0 <= i...  11.3 us
  transfers between devices with their start and end apart: 10, of which 5 were waited for; matrix products, arithmetic and copies ran while one was open for 1% of the time, Pallas kernels for 19%

profile of v2, /device:TPU:1, one launch (start us, length us, event | category | flops | bytes accessed | tf_op | source)
XLA Modules:
  0.0 212.2 jit_solution(13065473588378337956)
XLA Ops:
  0.6 1.3 convert_bitcast_fusion.live_ref
  1.9 3.8 %pack.2 = f32[128,24,128]{2,1,0:T(8,128)} custom-call(s32[128]{0:T(128)} %owner_ref.3, f32[8,128]{1,0:T(8,128)} %convert_bitcast_fusion.live_ref, s32[128,128]{1,0:T(8,128)} %voxel_ref.3, f32[128,24,128]{2,1,0:T(8,128)} %force_ref.3), custom_call_target="tpu_custom_call" | custom-call | tf_op jit(solution)/shard_map/pack/pallas_call | solution.py:60
  5.7 11.5 %all-to-all-start = ((f32[128,24,128]{2,1,0:T(8,128)}), f32[128,24,128]{2,1,0:T(8,128)S(1)}, u32[]{:S(2)}, u32[]{:S(2)}) async-start(f32[128,24,128]{2,1,0:T(8,128)} %pack.2), calls=%async_computation | async-start | bytes 3145728 | tf_op jit(solution)/shard_map/all_to_all | solution.py:529
  17.2 4.2 %pack.3 = f32[128,32,128]{2,1,0:T(8,128)} custom-call(s32[128]{0:T(128)} %owner_ref.3, f32[8,128]{1,0:T(8,128)} %convert_bitcast_fusion.live_ref, s32[128,128]{1,0:T(8,128)} %voxel_ref.3, f32[128,24,128]{2,1,0:T(8,128)} %force_ref.3), custom_call_target="tpu_custom_call" | custom-call | tf_op jit(solution)/shard_map/pack/pallas_call | solution.py:60
  21.4 20.7 %all-to-all-done = f32[128,24,128]{2,1,0:T(8,128)S(1)} async-done(((f32[128,24,128]{2,1,0:T(8,128)}), f32[128,24,128]{2,1,0:T(8,128)S(1)}, u32[]{:S(2)}, u32[]{:S(2)}) %all-to-all-start) | async-done | bytes 1572896 | tf_op jit(solution)/shard_map/all_to_all | solution.py:529
  43.2 4.4 %all-to-all-start.1 = ((f32[128,32,128]{2,1,0:T(8,128)}), f32[128,32,128]{2,1,0:T(8,128)S(1)}, u32[]{:S(2)}, u32[]{:S(2)}) async-start(f32[128,32,128]{2,1,0:T(8,128)} %pack.3), calls=%async_computation.1 | async-start | bytes 4194304 | tf_op jit(solution)/shard_map/all_to_all | solution.py:529
  47.6 1.3 collective-permute-start.5
  48.9 4.2 %collective-permute-start.4 = (s32[2,8,256]{2,1,0:T(8,128)S(1)}, s32[2,8,256]{2,1,0:T(8,128)S(1)}, u32[]{:S(2)}, u32[]{:S(2)}) collective-permute-start(s32[2,8,256]{2,1,0:T(8,128)S(1)} %slice.28), channel_id=1, source_target_pairs={{0,8},{8,16},{16,24},{24,32},{32,40},{40,48},{48,56},{56,64},{64,7... | collective-permute-start | bytes 49160 | tf_op jit(solution)/shard_map/ppermute | solution.py:523
  53.1 15.1 %scatter_first.1 = (f32[8,8,8,256]{3,2,1,0:T(8,128)}, s32[264]{0:T(512)}, s32[2,128,128]{2,1,0:T(8,128)}) custom-call(f32[3072,128]{1,0:T(8,128)} %bitcast.13), custom_call_target="tpu_custom_call" | custom-call | tf_op jit(solution)/shard_map/scatter_first/pallas_call | solution.py:170
  68.2 10.0 %all-to-all-done.1.recv_ref = f32[128,32,128]{2,1,0:T(8,128)S(1)} async-done(((f32[128,32,128]{2,1,0:T(8,128)}), f32[128,32,128]{2,1,0:T(8,128)S(1)}, u32[]{:S(2)}, u32[]{:S(2)}) %all-to-all-start.1) | async-done | bytes 2097184 | tf_op jit(solution)/shard_map/all_to_all | solution.py:529
  78.2 1.3 copy-done
  79.6 20.5 %scatter_second.1 = (f32[8,8,24,256]{3,2,1,0:T(8,128)}, f32[2,8,24,256]{3,2,1,0:T(8,128)}, f32[2,8,24,256]{3,2,1,0:T(8,128)}, f32[8,2,24,256]{3,2,1,0:T(8,128)}, f32[8,2,24,256]{3,2,1,0:T(8,128)}) custom-call(s32[264]{0:T(512)} %get-tuple-element.13.list_ref, s32[2,128,128]{2,1,0:T(8,128)} %get-tuple-element.14.ids_ref, f32[128,32,128]{2,1,0:T(8,128)} %copy-done, ...), custom_call_target="tpu_custom_call" | custom-call | tf_op jit(solution)/shard_map/scatter_second/pallas_call | solution.py:220
  100.0 4.2 %collective-permute-start = (f32[2,8,24,256]{3,2,1,0:T(8,128)}, f32[2,8,24,256]{3,2,1,0:T(8,128)S(1)}, u32[]{:S(2)}, u32[]{:S(2)}) collective-permute-start(f32[2,8,24,256]{3,2,1,0:T(8,128)} %get-tuple-element.17), channel_id=1, source_target_pairs={{0,8},{8,16},{16,24},{24,32},{32,40},{40,48},{48,56},{56,64},{64,7... | collective-permute-start | bytes 1179656 | tf_op jit(solution)/shard_map/ppermute | solution.py:523
  105.2 1.4 collective-permute-start.1
  106.7 5.2 %collective-permute-done.z_low = f32[2,8,24,256]{3,2,1,0:T(8,128)S(1)} collective-permute-done((f32[2,8,24,256]{3,2,1,0:T(8,128)}, f32[2,8,24,256]{3,2,1,0:T(8,128)S(1)}, u32[]{:S(2)}, u32[]{:S(2)}) %collective-permute-start) | collective-permute-done | bytes 393248 | tf_op jit(solution)/shard_map/ppermute | solution.py:523
  111.9 3.7 %collective-permute-done.1.z_high = f32[2,8,24,256]{3,2,1,0:T(8,128)S(1)} collective-permute-done((f32[2,8,24,256]{3,2,1,0:T(8,128)}, f32[2,8,24,256]{3,2,1,0:T(8,128)S(1)}, u32[]{:S(2)}, u32[]{:S(2)}) %collective-permute-start.1) | collective-permute-done | bytes 393248 | tf_op jit(solution)/shard_map/ppermute | solution.py:523
  115.7 7.5 %collective-permute-start.2 = (f32[12,2,24,256]{3,2,1,0:T(8,128)S(1)}, f32[12,2,24,256]{3,2,1,0:T(8,128)S(1)}, u32[]{:S(2)}, u32[]{:S(2)}) collective-permute-start(f32[12,2,24,256]{3,2,1,0:T(8,128)S(1)} %pad_maximum_fusion), channel_id=1, source_target_pairs={{0,1},{1,2},{2,3},{3,4},{4,5},{5,6},{6,7},{8,9},{9,10},{10,11},{11... | collective-permute-start | bytes 1769480 | tf_op jit(solution)/shard_map/ppermute | solution.py:523
  123.2 1.9 collective-permute-start.3
  125.9 1.9 collective-permute-start.7
  127.9 3.6 %collective-permute-start.6 = (s32[11,2,256]{2,1,0:T(2,128)S(1)}, s32[11,2,256]{2,1,0:T(2,128)S(1)}, u32[]{:S(2)}, u32[]{:S(2)}) collective-permute-start(s32[11,2,256]{2,1,0:T(2,128)S(1)} %slice.36), channel_id=1, source_target_pairs={{0,1},{1,2},{2,3},{3,4},{4,5},{5,6},{6,7},{8,9},{9,10},{10,11},{11... | collective-permute-start | bytes 67592 | tf_op jit(solution)/shard_map/ppermute | solution.py:523
  132.1 2.4 %collective-permute-done.7 = s32[11,1,256]{2,1,0:T(1,128)S(1)} collective-permute-done((s32[11,1,256]{2,1,0:T(1,128)S(1)}, s32[11,1,256]{2,1,0:T(1,128)S(1)}, u32[]{:S(2)}, u32[]{:S(2)}) %collective-permute-start.7) | collective-permute-done | bytes 11296 | tf_op jit(solution)/shard_map/ppermute | solution.py:523
  136.2 30.9 %operator.1 = (f32[8,8,24,256]{3,2,1,0:T(8,128)}, f32[8,8,24,256]{3,2,1,0:T(8,128)}, f32[128,256]{1,0:T(8,128)}) custom-call(f32[2]{0:T(128)} %add_convert_fusion.1.flag_ref, f32[8,8,24,256]{3,2,1,0:T(8,128)} %get-tuple-element.16.field.r_hbm, f32[2,8,24,256]{3,2,1,0:T(8,128)} %copy-done.2, f32[2,8,24,256]{3,2,1,0:T(8,128)} %copy-done.3, ...), custom_call_target="tpu_custom_call" | custom-call | tf_op jit(solution)/shard_map/operator/pallas_call | solution.py:354
  168.2 36.5 %all_to_all.21 = f32[128,1,256]{2,1,0:T(1,128)S(1)} all-to-all(f32[128,1,256]{2,1,0:T(1,128)S(1)} %copy.8), channel_id=1, replica_groups=mesh['gz'=16,'gy'=8] {'gz','gy'}, dimensions={0} | all-to-all | bytes 262144 | tf_op jit(solution)/shard_map/all_to_all | solution.py:529
  205.3 6.9 %final.1 = (f32[24,8,8,256]{3,2,1,0:T(8,128)}, f32[24,8,8,256]{3,2,1,0:T(8,128)}) custom-call(f32[128,256]{1,0:T(8,128)} %bitcast.14, f32[8,8,24,256]{3,2,1,0:T(8,128)} %get-tuple-element.16.field.r_hbm, f32[8,8,24,256]{3,2,1,0:T(8,128)} %get-tuple-element.22.s_hbm, f32[8,8,24,256]{3,2,1,0:T(8,128)} %get-tuple-element.23.q_hbm), custom_call_target="tpu_custom_call" | custom-call | tf_op jit(solution)/shard_map/final/pallas_call | solution.py:508
  (46 shorter events, 7.0 us)
Async XLA Ops:
  5.7 36.3 %all-to-all-start = ((f32[128,24,128]{2,1,0:T(8,128)}), f32[128,24,128]{2,1,0:T(8,128)S(1)}, u32[]{:S(2)}, u32[]{:S(2)}) async-start(f32[128,24,128]{2,1,0:T(8,128)} %pack.2), calls=%async_computation | async-start | bytes 3145728 | tf_op jit(solution)/shard_map/all_to_all | solution.py:529
  21.4 26.2 %copy-start.9 = (s32[8,8,256]{2,1,0:T(8,128)S(1)}, s32[8,8,256]{2,1,0:T(8,128)}, u32[]{:S(2)}) copy-start(s32[8,8,256]{2,1,0:T(8,128)} %param.10) | copy-start | bytes 196612
  42.1 1.1 copy-start.1
  43.2 35.0 %all-to-all-start.1 = ((f32[128,32,128]{2,1,0:T(8,128)}), f32[128,32,128]{2,1,0:T(8,128)S(1)}, u32[]{:S(2)}, u32[]{:S(2)}) async-start(f32[128,32,128]{2,1,0:T(8,128)} %pack.3), calls=%async_computation.1 | async-start | bytes 4194304 | tf_op jit(solution)/shard_map/all_to_all | solution.py:529
  47.6 78.3 %collective-permute-start.5 = (s32[1,8,256]{2,1,0:T(8,128)S(1)}, s32[1,8,256]{2,1,0:T(8,128)S(1)}, u32[]{:S(2)}, u32[]{:S(2)}) collective-permute-start(s32[1,8,256]{2,1,0:T(8,128)S(1)} %slice.29), channel_id=1, source_target_pairs={{8,0},{16,8},{24,16},{32,24},{40,32},{48,40},{56,48},{64,56},{72,6... | collective-permute-start | bytes 24584 | tf_op jit(solution)/shard_map/ppermute | solution.py:523
  48.9 76.9 %collective-permute-start.4 = (s32[2,8,256]{2,1,0:T(8,128)S(1)}, s32[2,8,256]{2,1,0:T(8,128)S(1)}, u32[]{:S(2)}, u32[]{:S(2)}) collective-permute-start(s32[2,8,256]{2,1,0:T(8,128)S(1)} %slice.28), channel_id=1, source_target_pairs={{0,8},{8,16},{16,24},{24,32},{32,40},{40,48},{48,56},{56,64},{64,7... | collective-permute-start | bytes 49160 | tf_op jit(solution)/shard_map/ppermute | solution.py:523
  68.2 36.1 %copy-start.10 = (f32[24,24]{1,0:T(8,128)S(1)}, f32[24,24]{1,0:T(8,128)}, u32[]{:S(2)}) copy-start(f32[24,24]{1,0:T(8,128)} %param.11) | copy-start | bytes 6916
  78.2 1.3 copy-start
  100.0 11.9 %collective-permute-start = (f32[2,8,24,256]{3,2,1,0:T(8,128)}, f32[2,8,24,256]{3,2,1,0:T(8,128)S(1)}, u32[]{:S(2)}, u32[]{:S(2)}) collective-permute-start(f32[2,8,24,256]{3,2,1,0:T(8,128)} %get-tuple-element.17), channel_id=1, source_target_pairs={{0,8},{8,16},{16,24},{24,32},{32,40},{40,48},{48,56},{56,64},{64,7... | collective-permute-start | bytes 1179656 | tf_op jit(solution)/shard_map/ppermute | solution.py:523
  104.5 11.1 %copy-start.8 = (f32[8,2,24,256]{3,2,1,0:T(8,128)S(1)}, f32[8,2,24,256]{3,2,1,0:T(8,128)}, u32[]{:S(2)}) copy-start(f32[8,2,24,256]{3,2,1,0:T(8,128)} %get-tuple-element.19) | copy-start | bytes 1179652
  105.2 17.9 %copy-start.7 = (f32[8,2,24,256]{3,2,1,0:T(8,128)S(1)}, f32[8,2,24,256]{3,2,1,0:T(8,128)}, u32[]{:S(2)}) copy-start(f32[8,2,24,256]{3,2,1,0:T(8,128)} %get-tuple-element.20) | copy-start | bytes 1179652
  105.2 10.4 %collective-permute-start.1 = (f32[2,8,24,256]{3,2,1,0:T(8,128)}, f32[2,8,24,256]{3,2,1,0:T(8,128)S(1)}, u32[]{:S(2)}, u32[]{:S(2)}) collective-permute-start(f32[2,8,24,256]{3,2,1,0:T(8,128)} %get-tuple-element.18), channel_id=1, source_target_pairs={{8,0},{16,8},{24,16},{32,24},{40,32},{48,40},{56,48},{64,56},{72,6... | collective-permute-start | bytes 1179656 | tf_op jit(solution)/shard_map/ppermute | solution.py:523
  106.7 18.4 %copy-start.4 = (bf16[192,192]{1,0:T(8,128)(2,1)}, bf16[192,192]{1,0:T(8,128)(2,1)S(1)}, u32[]{:S(2)}) copy-start(bf16[192,192]{1,0:T(8,128)(2,1)S(1)} %get-tuple-element.28.k_high) | copy-start | bytes 221188
  111.9 11.3 %copy-start.2 = (f32[2,8,24,256]{3,2,1,0:T(8,128)}, f32[2,8,24,256]{3,2,1,0:T(8,128)S(1)}, u32[]{:S(2)}) copy-start(f32[2,8,24,256]{3,2,1,0:T(8,128)S(1)} %collective-permute-done.z_low) | copy-start | bytes 1179652
  115.6 10.3 %copy-start.3 = (f32[2,8,24,256]{3,2,1,0:T(8,128)}, f32[2,8,24,256]{3,2,1,0:T(8,128)S(1)}, u32[]{:S(2)}) copy-start(f32[2,8,24,256]{3,2,1,0:T(8,128)S(1)} %collective-permute-done.1.z_high) | copy-start | bytes 1179652
  115.7 19.6 %collective-permute-start.2 = (f32[12,2,24,256]{3,2,1,0:T(8,128)S(1)}, f32[12,2,24,256]{3,2,1,0:T(8,128)S(1)}, u32[]{:S(2)}, u32[]{:S(2)}) collective-permute-start(f32[12,2,24,256]{3,2,1,0:T(8,128)S(1)} %pad_maximum_fusion), channel_id=1, source_target_pairs={{0,1},{1,2},{2,3},{3,4},{4,5},{5,6},{6,7},{8,9},{9,10},{10,11},{11... | collective-permute-start | bytes 1769480 | tf_op jit(solution)/shard_map/ppermute | solution.py:523
  123.2 12.0 %collective-permute-start.3 = (f32[12,2,24,256]{3,2,1,0:T(8,128)S(1)}, f32[12,2,24,256]{3,2,1,0:T(8,128)S(1)}, u32[]{:S(2)}, u32[]{:S(2)}) collective-permute-start(f32[12,2,24,256]{3,2,1,0:T(8,128)S(1)} %pad_maximum_fusion.1), channel_id=1, source_target_pairs={{1,0},{2,1},{3,2},{4,3},{5,4},{6,5},{7,6},{9,8},{10,9},{11,10},{12... | collective-permute-start | bytes 1769480 | tf_op jit(solution)/shard_map/ppermute | solution.py:523
  125.9 8.6 %collective-permute-start.7 = (s32[11,1,256]{2,1,0:T(1,128)S(1)}, s32[11,1,256]{2,1,0:T(1,128)S(1)}, u32[]{:S(2)}, u32[]{:S(2)}) collective-permute-start(s32[11,1,256]{2,1,0:T(1,128)S(1)} %slice.37), channel_id=1, source_target_pairs={{1,0},{2,1},{3,2},{4,3},{5,4},{6,5},{7,6},{9,8},{10,9},{11,10},{12... | collective-permute-start | bytes 33800 | tf_op jit(solution)/shard_map/ppermute | solution.py:523
  127.9 6.7 %collective-permute-start.6 = (s32[11,2,256]{2,1,0:T(2,128)S(1)}, s32[11,2,256]{2,1,0:T(2,128)S(1)}, u32[]{:S(2)}, u32[]{:S(2)}) collective-permute-start(s32[11,2,256]{2,1,0:T(2,128)S(1)} %slice.36), channel_id=1, source_target_pairs={{0,1},{1,2},{2,3},{3,4},{4,5},{5,6},{6,7},{8,9},{9,10},{10,11},{11... | collective-permute-start | bytes 67592 | tf_op jit(solution)/shard_map/ppermute | solution.py:523
  135.2 0.8 copy-start.5
  135.2 1.0 copy-start.6

commit v3 on v2

--- a/solution.py
+++ b/solution.py
@@ -9,6 +9,7 @@
 LOADS = 8
 CH = 24
 GROUP = 4
+UNROLL = 2
 AXES = ("gz", "gy")
 SPRING = 0.5
 F32 = jnp.float32
@@ -24,124 +25,121 @@
     return pl.BlockSpec(memory_space=pltpu.SMEM)
 
 
-def pack_kernel(with_ids, owner_ref, live_ref, voxel_ref, force_ref, out_ref, count_ref):
+def pack_kernel(owner_ref, row_ref, live_ref, voxel_ref, force_hbm, out_ref, force_ref, rank_v, rank_s, sems):
     devices = out_ref.shape[0]
-    blocks, width = force_ref.shape[0], force_ref.shape[1]
+    blocks = force_ref.shape[0]
     lane = lax.broadcasted_iota(jnp.int32, (8, 128), 1)
+    load = pltpu.make_async_copy(force_hbm, force_ref, sems.at[0])
+    load.start()
+
+    owners = jnp.broadcast_to(row_ref[...], (128, 128)).astype(F32)
+    before = lax.broadcasted_iota(jnp.int32, (128, 128), 0) < lax.broadcasted_iota(jnp.int32, (128, 128), 1)
+    same = jnp.where((owners.T == owners) & before, 1.0, 0.0)
+    rank_v[...] = jnp.broadcast_to(jnp.sum(same, axis=0, keepdims=True), (8, 128)).astype(jnp.int32)
+    ranks = pltpu.make_async_copy(rank_v, rank_s, sems.at[1])
+    ranks.start()
 
     def clear(i, carry):
-        count_ref[i] = 0
-        if with_ids:
-            out_ref[i, 2 * width : 2 * width + 8, :] = jnp.full((8, 128), -1.0, F32)
+        out_ref[i, 2 * CH : 2 * CH + 8, :] = jnp.full((8, 128), -1.0, F32)
         return carry
 
     lax.fori_loop(0, devices, clear, 0, unroll=8)
-    live = live_ref[...]
+    live = live_ref[...].astype(F32).T
+    ranks.wait()
+    load.wait()
 
     def one(p, carry):
         owner = owner_ref[p]
-        rank = count_ref[owner]
-        count_ref[owner] = rank + 1
+        rank = rank_s[0, p]
         limit = jnp.sum(jnp.where(lane == p, live, 0.0), axis=1, keepdims=True)
         keep = lane.astype(F32) < limit
-        for k in range(0, width, 8):
-            base = pl.multiple_of(rank * width + k, 8)
+        for k in range(0, CH, 8):
+            base = pl.multiple_of(rank * CH + k, 8)
             out_ref[owner, pl.ds(base, 8), :] = jnp.where(keep, force_ref[p, k : k + 8, :], 0.0)
-        if with_ids:
-            out_ref[owner, pl.ds(2 * width + rank, 1), :] = voxel_ref[pl.ds(p, 1), :].astype(F32)
+        out_ref[owner, pl.ds(2 * CH + rank, 1), :] = voxel_ref[pl.ds(p, 1), :].astype(F32)
         return carry
 
     lax.fori_loop(0, blocks, one, 0, unroll=8)
 
 
-def pack(owner, live_t, voxel, force, devices, width, place, with_ids):
-    blocks = force.shape[0]
-    rows = 2 * width + (8 if with_ids else 0)
+def pack(owner, live, voxel, force, devices):
     return pl.pallas_call(
-        functools.partial(pack_kernel, with_ids),
-        out_shape=jax.ShapeDtypeStruct((devices, rows, 128), F32),
-        grid=(1,),
-        in_specs=[
-            smem(),
-            pl.BlockSpec(live_t.shape, lambda i: (0, 0)),
-            pl.BlockSpec(voxel.shape, lambda i: (0, 0)),
-            pl.BlockSpec((blocks, width, 128), lambda i: (0, place, 0)),
+        pack_kernel,
+        out_shape=jax.ShapeDtypeStruct((devices, 2 * CH + 8, 128), F32),
+        in_specs=[smem(), vmem(), vmem(), vmem(), pl.BlockSpec(memory_space=pl.ANY)],
+        out_specs=vmem(),
+        scratch_shapes=[
+            pltpu.VMEM(force.shape, F32),
+            pltpu.VMEM((8, 128), jnp.int32),
+            pltpu.SMEM((8, 128), jnp.int32),
+            pltpu.SemaphoreType.DMA((2,)),
         ],
-        out_specs=pl.BlockSpec((devices, rows, 128), lambda i: (0, 0, 0)),
-        scratch_shapes=[pltpu.SMEM((devices,), jnp.int32)],
         compiler_params=pltpu.CompilerParams(vmem_limit_bytes=VMEM_LIMIT),
         name="pack",
-    )(owner, live_t, voxel, force)
-
-
-def add_blocks(count, list_ref, ids_ref, value_of, width, left_ref, right_ref, acc_ref):
-    acc_ref[...] = jnp.zeros_like(acc_ref)
+    )(owner, owner.reshape(1, -1), live, voxel, force)
+
+
+def add_blocks(count, list_ref, ids_ref, value_of, acc_ref):
     row_x = lax.broadcasted_iota(jnp.int32, (256, 128), 0)
     row_zy = lax.broadcasted_iota(jnp.int32, (64, 128), 0)
-
-    def group(g, carry):
+    last = jnp.maximum(count - 1, 0)
+
+    def one(g):
+        hots, rights, parts = [], [], []
         for j in range(GROUP):
             place = g * GROUP + j
-            index = list_ref[jnp.minimum(place, count - 1)]
+            index = list_ref[jnp.minimum(place, last)]
             source = index & 127
             rank = index >> 7
             ids = ids_ref[rank, pl.ds(source, 1), :]
             zy = jnp.where(place < count, ids >> 8, -1)
             x = ids & 255
             hot_x = jnp.where(row_x == x, 1.0, 0.0).astype(BF16)
-            right_ref[:, j * 256 : j * 256 + 128] = hot_x
-            right_ref[:, j * 256 + 128 : (j + 1) * 256] = hot_x
-            hot_zy = jnp.where(row_zy == zy, 1.0, 0.0).astype(BF16)
+            rights += [hot_x, hot_x]
+            hots.append(jnp.where(row_zy == zy, 1.0, 0.0).astype(BF16))
             value = value_of(source, rank)
             high = value.astype(BF16).astype(F32)
-            low = value - high
-            for c in range(width):
-                for half, part in enumerate((high, low)):
-                    line = jnp.broadcast_to(part[c : c + 1, :], (16, 128)).astype(BF16)
-                    tile = jnp.concatenate([line] * 4, axis=0) * hot_zy
-                    at = j * 256 + half * 128
-                    left_ref[c * 64 : (c + 1) * 64, at : at + 128] = tile
-        for m in range(width // 8):
-            part = lax.dot_general(
-                left_ref[m * 512 : (m + 1) * 512, :],
-                right_ref[...],
-                (((1,), (1,)), ((), ())),
-                preferred_element_type=F32,
+            parts.append((high, value - high))
+        right = jnp.concatenate(rights, axis=1)
+        for m in range(3):
+            lines = []
+            for c in range(m * 8, (m + 1) * 8):
+                tiles = []
+                for j in range(GROUP):
+                    for part in parts[j]:
+                        line = jnp.broadcast_to(part[c : c + 1, :], (16, 128)).astype(BF16)
+                        tiles.append(jnp.concatenate([line] * 4, axis=0) * hots[j])
+                lines.append(jnp.concatenate(tiles, axis=1))
+            product = lax.dot_general(
+                jnp.concatenate(lines, axis=0), right, (((1,), (1,)), ((), ())), preferred_element_type=F32
             )
             for h in range(2):
-                acc_ref[h, m * 512 : (m + 1) * 512, :] += part[:, h * 128 : (h + 1) * 128]
+                acc_ref[h, m * 512 : (m + 1) * 512, :] += product[:, h * 128 : (h + 1) * 128]
+
+    def several(i, carry):
+        for u in range(UNROLL):
+            one(UNROLL * i + u)
         return carry
 
-    lax.fori_loop(0, (count + GROUP - 1) // GROUP, group, 0)
-
-
-def node_of(acc_ref, width, z, y):
-    return jnp.concatenate(
-        [
-            jnp.concatenate(
-                [acc_ref[h, pl.ds(k * 64 + z * 8 + y, 8, stride=64), :] for k in range(0, width, 8)], axis=0
-            )
-            for h in range(2)
-        ],
-        axis=1,
-    )
-
-
-def scatter_first_kernel(
-    recv_ref, field, list_out, ids_out, flag_v, flag_s, left_ref, right_ref, acc_ref, sem
+    lax.fori_loop(0, (count + UNROLL * GROUP - 1) // (UNROLL * GROUP), several, 0)
+
+
+def scatter_kernel(
+    recv_ref, field, z_low, z_high, y_low, y_high,
+    list_ref, ids_ref, flag_v, flag_s, acc_ref, sem,
 ):
-    width = 8
-    rows = 2 * width + 8
+    rows = 2 * CH + 8
     lane = lax.broadcasted_iota(jnp.int32, (8, 128), 1)
     for rank in range(2):
         flags = jnp.zeros((8, 128), jnp.int32)
         for t in range(16):
-            ids = recv_ref[pl.ds(t * 8 * rows + 2 * width + rank, 8, stride=rows), :].astype(jnp.int32)
-            ids_out[rank, t * 8 : (t + 1) * 8, :] = ids
+            ids = recv_ref[pl.ds(t * 8 * rows + 2 * CH + rank, 8, stride=rows), :].astype(jnp.int32)
+            ids_ref[rank, t * 8 : (t + 1) * 8, :] = ids
             flags = jnp.where(lane == t, jnp.where(ids[:, 0:1] >= 0, 1, 0), flags)
         flag_v[rank * 8 : (rank + 1) * 8, :] = flags
     copy = pltpu.make_async_copy(flag_v, flag_s, sem)
     copy.start()
+    acc_ref[...] = jnp.zeros_like(acc_ref)
     copy.wait()
 
     count = jnp.int32(0)
@@ -149,59 +147,27 @@
 
         def collect(t, n):
             for s in range(8):
-                list_out[n] = rank * 128 + t * 8 + s
+                list_ref[n] = rank * 128 + t * 8 + s
                 n = n + flag_s[rank * 8 + s, t]
             return n
 
         count = lax.fori_loop(0, 16, collect, count)
-    list_out[list_out.shape[0] - 1] = count
 
     def value_of(source, rank):
-        return recv_ref[pl.ds(pl.multiple_of(source * rows + rank * width, 8), width), :]
-
-    add_blocks(count, list_out, ids_out, value_of, width, left_ref, right_ref, acc_ref)
+        return recv_ref[pl.ds(pl.multiple_of(source * rows + rank * CH, 8), CH), :]
+
+    add_blocks(count, list_ref, ids_ref, value_of, acc_ref)
     for z in range(8):
         for y in range(8):
-            field[z, y] = node_of(acc_ref, width, z, y)
-
-
-def scatter_first(recv):
-    devices = recv.shape[0]
-    return pl.pallas_call(
-        scatter_first_kernel,
-        out_shape=[
-            jax.ShapeDtypeStruct((8, 8, 8, 256), F32),
-            jax.ShapeDtypeStruct((2 * devices + 8,), jnp.int32),
-            jax.ShapeDtypeStruct((2, devices, 128), jnp.int32),
-        ],
-        in_specs=[vmem()],
-        out_specs=[vmem(), smem(), vmem()],
-        scratch_shapes=[
-            pltpu.VMEM((16, 128), jnp.int32),
-            pltpu.SMEM((16, 128), jnp.int32),
-            pltpu.VMEM((512, GROUP * 256), BF16),
-            pltpu.VMEM((256, GROUP * 256), BF16),
-            pltpu.VMEM((2, 512, 128), F32),
-            pltpu.SemaphoreType.DMA,
-        ],
-        compiler_params=pltpu.CompilerParams(vmem_limit_bytes=VMEM_LIMIT),
-        name="scatter_first",
-    )(recv.reshape(-1, 128))
-
-
-def scatter_second_kernel(
-    list_ref, ids_ref, recv_ref, part_ref, field, z_low, z_high, y_low, y_high, left_ref, right_ref, acc_ref
-):
-    width = 16
-    count = list_ref[list_ref.shape[0] - 1]
-
-    def value_of(source, rank):
-        return recv_ref[source, pl.ds(pl.multiple_of(rank * width, 8), width), :]
-
-    add_blocks(count, list_ref, ids_ref, value_of, width, left_ref, right_ref, acc_ref)
-    for z in range(8):
-        for y in range(8):
-            node = jnp.concatenate([node_of(acc_ref, width, z, y), part_ref[z, y]], axis=0)
+            node = jnp.concatenate(
+                [
+                    jnp.concatenate(
+                        [acc_ref[h, pl.ds(k * 512 + z * 8 + y, 8, stride=64), :] for k in range(3)], axis=0
+                    )
+                    for h in range(2)
+                ],
+                axis=1,
+            )
             field[z, y] = node
             if z < 2:
                 z_low[z, y] = node
@@ -213,23 +179,28 @@
                 y_high[z, y - 6] = node
 
 
-def scatter_second(blocks, ids, recv, part):
+def scatter(recv):
+    devices = recv.shape[0]
+
     def shape(a, b):
         return jax.ShapeDtypeStruct((a, b, CH, 256), F32)
 
     return pl.pallas_call(
-        scatter_second_kernel,
+        scatter_kernel,
         out_shape=[shape(8, 8), shape(2, 8), shape(2, 8), shape(8, 2), shape(8, 2)],
-        in_specs=[smem(), vmem(), vmem(), vmem()],
+        in_specs=[vmem()],
         out_specs=[vmem()] * 5,
         scratch_shapes=[
-            pltpu.VMEM((1024, GROUP * 256), BF16),
-            pltpu.VMEM((256, GROUP * 256), BF16),
-            pltpu.VMEM((2, 1024, 128), F32),
+            pltpu.SMEM((2 * devices + 8,), jnp.int32),
+            pltpu.VMEM((2, devices, 128), jnp.int32),
+            pltpu.VMEM((16, 128), jnp.int32),
+            pltpu.SMEM((16, 128), jnp.int32),
+            pltpu.VMEM((2, CH * 64, 128), F32),
+            pltpu.SemaphoreType.DMA,
         ],
         compiler_params=pltpu.CompilerParams(vmem_limit_bytes=VMEM_LIMIT),
-        name="scatter_second",
-    )(blocks, ids, recv, part)
+        name="scatter",
+    )(recv.reshape(-1, 128))
 
 
 def shift_down(v, lane):
@@ -241,7 +212,7 @@
 
 
 def operator_kernel(
-    flag_ref, field, z_low, z_high, y_low, y_high, mask_ref, k_both, k_high,
+    flag_ref, field, z_low, z_high, y_low, y_high, c_low, c_high, mask_ref, k_both, k_high,
     s_out, q_out, gram_out,
     v32, vh, vl, s32, sh, sl, carry_ref, gram_ref,
 ):
@@ -265,8 +236,13 @@
     rows(z_low, 2, 8, 0, 2)
     rows(field, 8, 8, 2, 2)
     rows(z_high, 2, 8, 10, 2)
-    rows(y_low, 12, 2, 0, 0)
-    rows(y_high, 12, 2, 0, 10)
+    rows(y_low, 8, 2, 2, 0)
+    rows(y_high, 8, 2, 2, 10)
+    for part, z_at in ((0, 0), (2, 10)):
+        for z in range(2):
+            for y in range(2):
+                put(v32, vh, vl, z_at + z, y, c_low[part + z, y])
+                put(v32, vh, vl, z_at + z, y + 10, c_high[part + z, y])
 
     def element(high, low, ez, ey):
         def gather(ref):
@@ -346,15 +322,15 @@
         packed[at // 16] = packed[at // 16] + jnp.where(spot == at % 16, total, 0.0)
     for h in range(2):
         line = jnp.sum(packed[h], axis=0, keepdims=True)
-        gram_out[:, h * 128 : (h + 1) * 128] = jnp.broadcast_to(line, (gram_out.shape[0], 128))
+        gram_out[:, :, h * 128 : (h + 1) * 128] = jnp.broadcast_to(line[None], (gram_out.shape[0], 1, 128))
 
 
 def operator(flags, fields, mask, k_both, k_high, devices):
     node = jax.ShapeDtypeStruct((8, 8, CH, 256), F32)
     return pl.pallas_call(
         operator_kernel,
-        out_shape=[node, node, jax.ShapeDtypeStruct((devices, 256), F32)],
-        in_specs=[smem()] + [vmem()] * 8,
+        out_shape=[node, node, jax.ShapeDtypeStruct((devices, 1, 256), F32)],
+        in_specs=[smem()] + [vmem()] * 10,
         out_specs=[vmem()] * 3,
         scratch_shapes=[
             pltpu.VMEM((12, 12 * CH, 256), F32),
@@ -387,7 +363,7 @@
     lane = lax.broadcasted_iota(jnp.int32, (8, 128), 1)
     inside = lane < 8
     total = [
-        jnp.broadcast_to(jnp.sum(gram_ref[:, h * 128 : (h + 1) * 128], axis=0, keepdims=True), (8, 128))
+        jnp.broadcast_to(jnp.sum(gram_ref[:, :, h * 128 : (h + 1) * 128], axis=0), (8, 128))
         for h in range(2)
     ]
 
@@ -533,12 +509,9 @@
     nz, ny = lax.axis_size("gz"), lax.axis_size("gy")
     devices = nz * ny
 
-    live_t = patch_live.astype(F32).T
-    packed = functools.partial(pack, patch_owner, live_t, patch_voxel, patch_force, devices)
-    first = exchange(packed(8, 2, True))
-    second = exchange(packed(16, 0, False))
-
-    mask = voxel_mask
+    send = pack(patch_owner, patch_live, patch_voxel, patch_force, devices)
+    send, mask = lax.optimization_barrier((send, voxel_mask))
+    recv = exchange(send)
     mask = jnp.concatenate([moved(mask[6:8], "gz", 1), mask, moved(mask[0:1], "gz", -1)], axis=0)
     mask = jnp.concatenate([moved(mask[:, 6:8], "gy", 1), mask, moved(mask[:, 0:1], "gy", -1)], axis=1)
     mask = mask.astype(F32)
@@ -549,12 +522,13 @@
     k_both = jnp.concatenate([k_high, (big - rounded).astype(BF16)], axis=0)
     flags = jnp.stack([lax.axis_index("gz") + 1 < nz, lax.axis_index("gy") + 1 < ny]).astype(F32)
 
-    part, blocks, ids = scatter_first(first)
-    field, z_low, z_high, y_low, y_high = scatter_second(blocks, ids, second, part)
+    recv, mask, k_high, k_both, flags = lax.optimization_barrier((recv, mask, k_high, k_both, flags))
+    field, z_low, z_high, y_low, y_high = scatter(recv)
     below, above = moved(z_high, "gz", 1), moved(z_low, "gz", -1)
-    y_low = jnp.concatenate([below[:, 0:2], y_low, above[:, 0:2]], axis=0)
-    y_high = jnp.concatenate([below[:, 6:8], y_high, above[:, 6:8]], axis=0)
-    around = (field, below, above, moved(y_high, "gy", 1), moved(y_low, "gy", -1))
+    beside = (moved(y_high, "gy", 1), moved(y_low, "gy", -1))
+    low = jnp.concatenate([below[:, 0:2], above[:, 0:2]], axis=0)
+    high = jnp.concatenate([below[:, 6:8], above[:, 6:8]], axis=0)
+    around = (field, below, above, *beside, moved(high, "gy", 1), moved(low, "gy", -1))
     s, q, gram = operator(flags, around, mask, k_both, k_high, devices)
     return final(exchange(gram), field, s, q)
 

time: 212 us -> 198 us (0.934)
  Pallas kernels: 81.3 us -> 67.2 us
  waiting for transfers between devices: 42 us -> 28.7 us
  starting transfers between devices: 42 us -> 54.4 us
  blocking collectives: 36.5 us -> 41.4 us
  local copies, waits for them, and re-layouts: 5.96 us -> 2.84 us
    all_to_all x2 -> x1, waiting for transfers between devices: 30.7 us -> 5.21 us  [exchange(): return lax.all_to_all(value, AXES, split_axis=0, concat_axis=0, tiled=True)]
    ppermute x8 -> x10, starting transfers between devices: 26.1 us -> 42.5 us  [moved(): lax.ppermute(value, axis, [(i, i + step) for i in range(count) if 0 <= i...]
    pallas_call x4 -> x2, Pallas kernels: 43.5 us -> 29.8 us  [the longest x1 24.2 us: scatter(): pl.pallas_call(scatter_kernel, out_shape=[shape(8, 8), shape(2, 8), shape...]
    ppermute x8 -> x10, waiting for transfers between devices: 11.3 us -> 23.5 us  [moved(): lax.ppermute(value, axis, [(i, i + step) for i in range(count) if 0 <= i...]
    all_to_all x1, blocking collectives: 36.5 us -> 41.4 us  [exchange(): return lax.all_to_all(value, AXES, split_axis=0, concat_axis=0, tiled=True)]
    all_to_all x2 -> x1, starting transfers between devices: 15.9 us -> 11.9 us  [exchange(): return lax.all_to_all(value, AXES, split_axis=0, concat_axis=0, tiled=True)]
  transfers between devices with their start and end apart: 10 -> 11, of which waited for: 5 -> 6; matrix products, arithmetic and copies ran while one was open for 1% -> 2% of each run, Pallas kernels for 19% -> 0%
where the time goes in v3:
time: 198 us
  Pallas kernels  67.2 us (34%)
  starting transfers between devices  54.4 us (27%)
  blocking collectives  41.4 us (21%)
  waiting for transfers between devices  28.7 us (14%)
  local copies, waits for them, and re-layouts  2.84 us (1%)
  other arithmetic  2.26 us (1%)
    ppermute x10, starting transfers between devices, moved(): lax.ppermute(value, axis, [(i, i + step) for i in range(count) if 0 <= i...  42.5 us
    all_to_all x1, blocking collectives, exchange(): return lax.all_to_all(value, AXES, split_axis=0, concat_axis=0, tiled=True)  41.4 us
    pallas_call x1, Pallas kernels, operator(): pl.pallas_call(operator_kernel, out_shape=[node, node, jax.ShapeDtypeStru...  30.4 us
    pallas_call x1, Pallas kernels, scatter(): pl.pallas_call(scatter_kernel, out_shape=[shape(8, 8), shape(2, 8), shape...  24.2 us
    ppermute x10, waiting for transfers between devices, moved(): lax.ppermute(value, axis, [(i, i + step) for i in range(count) if 0 <= i...  23.5 us
    all_to_all x1, starting transfers between devices, exchange(): return lax.all_to_all(value, AXES, split_axis=0, concat_axis=0, tiled=True)  11.9 us
    pallas_call x1, Pallas kernels, final(): pl.pallas_call(final_kernel, out_shape=[out, out], in_specs=[vmem()] + [f...  7.02 us
    pallas_call x1, Pallas kernels, pack(): pl.pallas_call(pack_kernel, out_shape=jax.ShapeDtypeStruct((devices, 2 *...  5.6 us
  transfers between devices with their start and end apart: 11, of which 6 were waited for; matrix products, arithmetic and copies ran while one was open for 2% of the time, Pallas kernels for 0%

profile of v3, /device:TPU:1, one launch (start us, length us, event | category | flops | bytes accessed | tf_op | source)
XLA Modules:
  0.0 197.8 jit_solution(12524357713671001796)
XLA Ops:
  0.6 1.4 copy.9.live_ref
  2.0 5.6 %pack.1 = f32[128,56,128]{2,1,0:T(8,128)} custom-call(s32[128]{0:T(128)} %owner_ref.1, s32[1,128]{1,0:T(1,128)} %bitcast.8, s32[128,8]{1,0:T(8,128)} %copy.9.live_ref, s32[128,128]{1,0:T(8,128)} %voxel_ref.1, f32[128,24,128]{2,1,0:T(8,128)} %force_hbm.1), custom_call_target="tpu_custom_call" | custom-call | tf_op jit(solution)/shard_map/pack/pallas_call | solution.py:66
  7.7 11.9 %all-to-all-start = ((f32[128,56,128]{2,1,0:T(8,128)}), f32[128,56,128]{2,1,0:T(8,128)}, u32[]{:S(2)}, u32[]{:S(2)}) async-start(f32[128,56,128]{2,1,0:T(8,128)} %pack.1), calls=%async_computation | async-start | bytes 7340032 | tf_op jit(solution)/shard_map/all_to_all | solution.py:505
  19.6 1.3 collective-permute-start.1
  20.9 4.0 %collective-permute-start = (s32[2,8,256]{2,1,0:T(8,128)S(1)}, s32[2,8,256]{2,1,0:T(8,128)S(1)}, u32[]{:S(2)}, u32[]{:S(2)}) collective-permute-start(s32[2,8,256]{2,1,0:T(8,128)S(1)} %slice.24), channel_id=1, source_target_pairs={{0,8},{8,16},{16,24},{24,32},{32,40},{40,48},{48,56},{56,64},{64,7... | collective-permute-start | bytes 49160 | tf_op jit(solution)/shard_map/ppermute | solution.py:499
  25.2 0.7 reshape.14
  25.9 0.7 pad_maximum_fusion.k_both
  26.7 18.1 %collective-permute-start.3 = (s32[11,1,256]{2,1,0:T(1,128)S(1)}, s32[11,1,256]{2,1,0:T(1,128)S(1)}, u32[]{:S(2)}, u32[]{:S(2)}) collective-permute-start(s32[11,1,256]{2,1,0:T(1,128)S(1)} %slice.33), channel_id=1, source_target_pairs={{1,0},{2,1},{3,2},{4,3},{5,4},{6,5},{7,6},{9,8},{10,9},{11,10},{12... | collective-permute-start | bytes 33800 | tf_op jit(solution)/shard_map/ppermute | solution.py:499
  44.8 1.9 collective-permute-start.2
  47.3 13.4 %collective-permute-done.3 = s32[11,1,256]{2,1,0:T(1,128)S(1)} collective-permute-done((s32[11,1,256]{2,1,0:T(1,128)S(1)}, s32[11,1,256]{2,1,0:T(1,128)S(1)}, u32[]{:S(2)}, u32[]{:S(2)}) %collective-permute-start.3) | collective-permute-done | bytes 11296 | tf_op jit(solution)/shard_map/ppermute | solution.py:499
  60.7 0.7 add_convert_fusion.mask_ref
  61.4 5.2 %all-to-all-done = f32[128,56,128]{2,1,0:T(8,128)} async-done(((f32[128,56,128]{2,1,0:T(8,128)}), f32[128,56,128]{2,1,0:T(8,128)}, u32[]{:S(2)}, u32[]{:S(2)}) %all-to-all-start) | async-done | bytes 3670048 | tf_op jit(solution)/shard_map/all_to_all | solution.py:505
  66.6 24.2 %scatter.1 = (f32[8,8,24,256]{3,2,1,0:T(8,128)}, f32[2,8,24,256]{3,2,1,0:T(8,128)}, f32[2,8,24,256]{3,2,1,0:T(8,128)}, f32[8,2,24,256]{3,2,1,0:T(8,128)}, f32[8,2,24,256]{3,2,1,0:T(8,128)}) custom-call(f32[7168,128]{1,0:T(8,128)} %bitcast.4.recv_ref), custom_call_target="tpu_custom_call" | custom-call | tf_op jit(solution)/shard_map/scatter/pallas_call | solution.py:188
  90.8 4.9 %collective-permute-start.4 = (f32[2,8,24,256]{3,2,1,0:T(8,128)}, f32[2,8,24,256]{3,2,1,0:T(8,128)S(1)}, u32[]{:S(2)}, u32[]{:S(2)}) collective-permute-start(f32[2,8,24,256]{3,2,1,0:T(8,128)} %get-tuple-element.22), channel_id=1, source_target_pairs={{0,8},{8,16},{16,24},{24,32},{32,40},{40,48},{48,56},{56,64},{64,7... | collective-permute-start | bytes 1179656 | tf_op jit(solution)/shard_map/ppermute | solution.py:499
  95.7 1.3 collective-permute-start.5
  97.0 3.1 %collective-permute-start.6 = (f32[8,2,24,256]{3,2,1,0:T(8,128)}, f32[8,2,24,256]{3,2,1,0:T(8,128)S(1)}, u32[]{:S(2)}, u32[]{:S(2)}) collective-permute-start(f32[8,2,24,256]{3,2,1,0:T(8,128)} %get-tuple-element.24), channel_id=1, source_target_pairs={{0,1},{1,2},{2,3},{3,4},{4,5},{5,6},{6,7},{8,9},{9,10},{10,11},{11... | collective-permute-start | bytes 1179656 | tf_op jit(solution)/shard_map/ppermute | solution.py:499
  100.2 2.2 %collective-permute-start.7 = (f32[8,2,24,256]{3,2,1,0:T(8,128)}, f32[8,2,24,256]{3,2,1,0:T(8,128)S(1)}, u32[]{:S(2)}, u32[]{:S(2)}) collective-permute-start(f32[8,2,24,256]{3,2,1,0:T(8,128)} %get-tuple-element.25), channel_id=1, source_target_pairs={{1,0},{2,1},{3,2},{4,3},{5,4},{6,5},{7,6},{9,8},{10,9},{11,10},{12... | collective-permute-start | bytes 1179656 | tf_op jit(solution)/shard_map/ppermute | solution.py:499
  102.6 5.0 %collective-permute-done.5.z_high = f32[2,8,24,256]{3,2,1,0:T(8,128)S(1)} collective-permute-done((f32[2,8,24,256]{3,2,1,0:T(8,128)}, f32[2,8,24,256]{3,2,1,0:T(8,128)S(1)}, u32[]{:S(2)}, u32[]{:S(2)}) %collective-permute-start.5) | collective-permute-done | bytes 393248 | tf_op jit(solution)/shard_map/ppermute | solution.py:499
  107.7 3.6 %collective-permute-start.8 = (f32[4,2,24,256]{3,2,1,0:T(8,128)S(1)}, f32[4,2,24,256]{3,2,1,0:T(8,128)S(1)}, u32[]{:S(2)}, u32[]{:S(2)}) collective-permute-start(f32[4,2,24,256]{3,2,1,0:T(8,128)S(1)} %pad_maximum_fusion.1), channel_id=1, source_target_pairs={{0,1},{1,2},{2,3},{3,4},{4,5},{5,6},{6,7},{8,9},{9,10},{10,11},{11... | collective-permute-start | bytes 589832 | tf_op jit(solution)/shard_map/ppermute | solution.py:499
  111.3 2.0 %collective-permute-start.9 = (f32[4,2,24,256]{3,2,1,0:T(8,128)S(1)}, f32[4,2,24,256]{3,2,1,0:T(8,128)S(1)}, u32[]{:S(2)}, u32[]{:S(2)}) collective-permute-start(f32[4,2,24,256]{3,2,1,0:T(8,128)S(1)} %pad_maximum_fusion.2), channel_id=1, source_target_pairs={{1,0},{2,1},{3,2},{4,3},{5,4},{6,5},{7,6},{9,8},{10,9},{11,10},{12... | collective-permute-start | bytes 589832 | tf_op jit(solution)/shard_map/ppermute | solution.py:499
  113.9 4.4 %collective-permute-done.9.c_high = f32[4,2,24,256]{3,2,1,0:T(8,128)S(1)} collective-permute-done((f32[4,2,24,256]{3,2,1,0:T(8,128)S(1)}, f32[4,2,24,256]{3,2,1,0:T(8,128)S(1)}, u32[]{:S(2)}, u32[]{:S(2)}) %collective-permute-start.9) | collective-permute-done | bytes 196640 | tf_op jit(solution)/shard_map/ppermute | solution.py:499
  119.0 30.4 %operator.1 = (f32[8,8,24,256]{3,2,1,0:T(8,128)}, f32[8,8,24,256]{3,2,1,0:T(8,128)}, f32[128,1,256]{2,1,0:T(1,128)}) custom-call(f32[2]{0:T(128)} %add_convert_fusion.1.flag_ref, f32[8,8,24,256]{3,2,1,0:T(8,128)} %get-tuple-element.21.field.r_hbm, f32[2,8,24,256]{3,2,1,0:T(8,128)} %copy-done, f32[2,8,24,256]{3,2,1,0:T(8,128)} %copy-done.1, ...), custom_call_target="tpu_custom_call" | custom-call | tf_op jit(solution)/shard_map/operator/pallas_call | solution.py:330
  149.3 41.4 %all_to_all.10.gram_ref = f32[128,1,256]{2,1,0:T(1,128)} all-to-all(f32[128,1,256]{2,1,0:T(1,128)} %get-tuple-element.29), channel_id=1, replica_groups=mesh['gz'=16,'gy'=8] {'gz','gy'}, dimensions={0} | all-to-all | bytes 262144 | tf_op jit(solution)/shard_map/all_to_all | solution.py:505
  190.7 7.0 %final.1 = (f32[24,8,8,256]{3,2,1,0:T(8,128)}, f32[24,8,8,256]{3,2,1,0:T(8,128)}) custom-call(f32[128,1,256]{2,1,0:T(1,128)} %all_to_all.10.gram_ref, f32[8,8,24,256]{3,2,1,0:T(8,128)} %get-tuple-element.21.field.r_hbm, f32[8,8,24,256]{3,2,1,0:T(8,128)} %get-tuple-element.30.s_hbm, f32[8,8,24,256]{3,2,1,0:T(8,128)} %get-tuple-element.31.q_hbm), custom_call_target="tpu_custom_call" | custom-call | tf_op jit(solution)/shard_map/final/pallas_call | solution.py:484
  (40 shorter events, 2.3 us)
Async XLA Ops:
  7.7 11.9 %copy-start.7 = (s32[8,8,256]{2,1,0:T(8,128)S(1)}, s32[8,8,256]{2,1,0:T(8,128)}, u32[]{:S(2)}) copy-start(s32[8,8,256]{2,1,0:T(8,128)} %param.10) | copy-start | bytes 196612
  7.7 17.3 %copy-start.8 = (f32[24,24]{1,0:T(8,128)S(1)}, f32[24,24]{1,0:T(8,128)}, u32[]{:S(2)}) copy-start(f32[24,24]{1,0:T(8,128)} %param.11) | copy-start | bytes 6916
  7.7 58.9 %all-to-all-start = ((f32[128,56,128]{2,1,0:T(8,128)}), f32[128,56,128]{2,1,0:T(8,128)}, u32[]{:S(2)}, u32[]{:S(2)}) async-start(f32[128,56,128]{2,1,0:T(8,128)} %pack.1), calls=%async_computation | async-start | bytes 7340032 | tf_op jit(solution)/shard_map/all_to_all | solution.py:505
  19.6 7.0 %collective-permute-start.1 = (s32[1,8,256]{2,1,0:T(8,128)S(1)}, s32[1,8,256]{2,1,0:T(8,128)S(1)}, u32[]{:S(2)}, u32[]{:S(2)}) collective-permute-start(s32[1,8,256]{2,1,0:T(8,128)S(1)} %slice.25), channel_id=1, source_target_pairs={{8,0},{16,8},{24,16},{32,24},{40,32},{48,40},{56,48},{64,56},{72,6... | collective-permute-start | bytes 24584 | tf_op jit(solution)/shard_map/ppermute | solution.py:499
  20.9 5.7 %collective-permute-start = (s32[2,8,256]{2,1,0:T(8,128)S(1)}, s32[2,8,256]{2,1,0:T(8,128)S(1)}, u32[]{:S(2)}, u32[]{:S(2)}) collective-permute-start(s32[2,8,256]{2,1,0:T(8,128)S(1)} %slice.24), channel_id=1, source_target_pairs={{0,8},{8,16},{16,24},{24,32},{32,40},{40,48},{48,56},{56,64},{64,7... | collective-permute-start | bytes 49160 | tf_op jit(solution)/shard_map/ppermute | solution.py:499
  25.9 76.7 %copy-start.2 = (bf16[192,192]{1,0:T(8,128)(2,1)}, bf16[192,192]{1,0:T(8,128)(2,1)S(1)}, u32[]{:S(2)}) copy-start(bf16[192,192]{1,0:T(8,128)(2,1)S(1)} %get-tuple-element.28.k_high) | copy-start | bytes 221188
  26.7 34.0 %collective-permute-start.3 = (s32[11,1,256]{2,1,0:T(1,128)S(1)}, s32[11,1,256]{2,1,0:T(1,128)S(1)}, u32[]{:S(2)}, u32[]{:S(2)}) collective-permute-start(s32[11,1,256]{2,1,0:T(1,128)S(1)} %slice.33), channel_id=1, source_target_pairs={{1,0},{2,1},{3,2},{4,3},{5,4},{6,5},{7,6},{9,8},{10,9},{11,10},{12... | collective-permute-start | bytes 33800 | tf_op jit(solution)/shard_map/ppermute | solution.py:499
  44.8 15.9 %collective-permute-start.2 = (s32[11,2,256]{2,1,0:T(2,128)S(1)}, s32[11,2,256]{2,1,0:T(2,128)S(1)}, u32[]{:S(2)}, u32[]{:S(2)}) collective-permute-start(s32[11,2,256]{2,1,0:T(2,128)S(1)} %slice.32), channel_id=1, source_target_pairs={{0,1},{1,2},{2,3},{3,4},{4,5},{5,6},{6,7},{8,9},{9,10},{10,11},{11... | collective-permute-start | bytes 67592 | tf_op jit(solution)/shard_map/ppermute | solution.py:499
  90.8 11.8 %collective-permute-start.4 = (f32[2,8,24,256]{3,2,1,0:T(8,128)}, f32[2,8,24,256]{3,2,1,0:T(8,128)S(1)}, u32[]{:S(2)}, u32[]{:S(2)}) collective-permute-start(f32[2,8,24,256]{3,2,1,0:T(8,128)} %get-tuple-element.22), channel_id=1, source_target_pairs={{0,8},{8,16},{16,24},{24,32},{32,40},{40,48},{48,56},{56,64},{64,7... | collective-permute-start | bytes 1179656 | tf_op jit(solution)/shard_map/ppermute | solution.py:499
  95.7 11.9 %collective-permute-start.5 = (f32[2,8,24,256]{3,2,1,0:T(8,128)}, f32[2,8,24,256]{3,2,1,0:T(8,128)S(1)}, u32[]{:S(2)}, u32[]{:S(2)}) collective-permute-start(f32[2,8,24,256]{3,2,1,0:T(8,128)} %get-tuple-element.23), channel_id=1, source_target_pairs={{8,0},{16,8},{24,16},{32,24},{40,32},{48,40},{56,48},{64,56},{72,6... | collective-permute-start | bytes 1179656 | tf_op jit(solution)/shard_map/ppermute | solution.py:499
  97.0 16.3 %collective-permute-start.6 = (f32[8,2,24,256]{3,2,1,0:T(8,128)}, f32[8,2,24,256]{3,2,1,0:T(8,128)S(1)}, u32[]{:S(2)}, u32[]{:S(2)}) collective-permute-start(f32[8,2,24,256]{3,2,1,0:T(8,128)} %get-tuple-element.24), channel_id=1, source_target_pairs={{0,1},{1,2},{2,3},{3,4},{4,5},{5,6},{6,7},{8,9},{9,10},{10,11},{11... | collective-permute-start | bytes 1179656 | tf_op jit(solution)/shard_map/ppermute | solution.py:499
  100.2 13.1 %collective-permute-start.7 = (f32[8,2,24,256]{3,2,1,0:T(8,128)}, f32[8,2,24,256]{3,2,1,0:T(8,128)S(1)}, u32[]{:S(2)}, u32[]{:S(2)}) collective-permute-start(f32[8,2,24,256]{3,2,1,0:T(8,128)} %get-tuple-element.25), channel_id=1, source_target_pairs={{1,0},{2,1},{3,2},{4,3},{5,4},{6,5},{7,6},{9,8},{10,9},{11,10},{12... | collective-permute-start | bytes 1179656 | tf_op jit(solution)/shard_map/ppermute | solution.py:499
  102.6 15.7 %copy-start = (f32[2,8,24,256]{3,2,1,0:T(8,128)}, f32[2,8,24,256]{3,2,1,0:T(8,128)S(1)}, u32[]{:S(2)}) copy-start(f32[2,8,24,256]{3,2,1,0:T(8,128)S(1)} %collective-permute-done.4.z_low) | copy-start | bytes 1179652
  107.6 10.7 %copy-start.1 = (f32[2,8,24,256]{3,2,1,0:T(8,128)}, f32[2,8,24,256]{3,2,1,0:T(8,128)S(1)}, u32[]{:S(2)}) copy-start(f32[2,8,24,256]{3,2,1,0:T(8,128)S(1)} %collective-permute-done.5.z_high) | copy-start | bytes 1179652
  107.7 6.2 %collective-permute-start.8 = (f32[4,2,24,256]{3,2,1,0:T(8,128)S(1)}, f32[4,2,24,256]{3,2,1,0:T(8,128)S(1)}, u32[]{:S(2)}, u32[]{:S(2)}) collective-permute-start(f32[4,2,24,256]{3,2,1,0:T(8,128)S(1)} %pad_maximum_fusion.1), channel_id=1, source_target_pairs={{0,1},{1,2},{2,3},{3,4},{4,5},{5,6},{6,7},{8,9},{9,10},{10,11},{11... | collective-permute-start | bytes 589832 | tf_op jit(solution)/shard_map/ppermute | solution.py:499
  111.3 7.0 %collective-permute-start.9 = (f32[4,2,24,256]{3,2,1,0:T(8,128)S(1)}, f32[4,2,24,256]{3,2,1,0:T(8,128)S(1)}, u32[]{:S(2)}, u32[]{:S(2)}) collective-permute-start(f32[4,2,24,256]{3,2,1,0:T(8,128)S(1)} %pad_maximum_fusion.2), channel_id=1, source_target_pairs={{1,0},{2,1},{3,2},{4,3},{5,4},{6,5},{7,6},{9,8},{10,9},{11,10},{12... | collective-permute-start | bytes 589832 | tf_op jit(solution)/shard_map/ppermute | solution.py:499
  113.3 5.0 %copy-start.3 = (f32[8,2,24,256]{3,2,1,0:T(8,128)}, f32[8,2,24,256]{3,2,1,0:T(8,128)S(1)}, u32[]{:S(2)}) copy-start(f32[8,2,24,256]{3,2,1,0:T(8,128)S(1)} %collective-permute-done.6.y_low) | copy-start | bytes 1179652
  113.3 5.0 %copy-start.4 = (f32[8,2,24,256]{3,2,1,0:T(8,128)}, f32[8,2,24,256]{3,2,1,0:T(8,128)S(1)}, u32[]{:S(2)}) copy-start(f32[8,2,24,256]{3,2,1,0:T(8,128)S(1)} %collective-permute-done.7.y_high) | copy-start | bytes 1179652
  113.9 4.4 %copy-start.5 = (f32[4,2,24,256]{3,2,1,0:T(8,128)}, f32[4,2,24,256]{3,2,1,0:T(8,128)S(1)}, u32[]{:S(2)}) copy-start(f32[4,2,24,256]{3,2,1,0:T(8,128)S(1)} %collective-permute-done.8.c_low) | copy-start | bytes 589828
  118.3 0.7 copy-start.6

commit v4 on v3

--- a/solution.py
+++ b/solution.py
@@ -44,7 +44,7 @@
         return carry
 
     lax.fori_loop(0, devices, clear, 0, unroll=8)
-    live = live_ref[...].astype(F32).T
+    live = live_ref[...].astype(F32)
     ranks.wait()
     load.wait()
 
@@ -76,7 +76,7 @@
         ],
         compiler_params=pltpu.CompilerParams(vmem_limit_bytes=VMEM_LIMIT),
         name="pack",
-    )(owner, owner.reshape(1, -1), live, voxel, force)
+    )(owner, owner.reshape(1, -1), live.T, voxel, force)
 
 
 def add_blocks(count, list_ref, ids_ref, value_of, acc_ref):
@@ -213,8 +213,8 @@
 
 def operator_kernel(
     flag_ref, field, z_low, z_high, y_low, y_high, c_low, c_high, mask_ref, k_both, k_high,
-    s_out, q_out, gram_out,
-    v32, vh, vl, s32, sh, sl, carry_ref, gram_ref,
+    s_hbm, q_hbm, gram_out,
+    v32, vh, vl, s32, sh, sl, q32, carry_ref, gram_ref, sems,
 ):
     lane = lax.broadcasted_iota(jnp.int32, (CH, 256), 1)
 
@@ -280,15 +280,19 @@
 
     lax.fori_loop(0, 11, first_pass, 0)
     carry_ref[...] = jnp.zeros_like(carry_ref)
+    store_s = pltpu.make_async_copy(s32.at[2:10, 2 * CH : 10 * CH, :], s_hbm, sems.at[0])
+    store_s.start()
 
     def second_pass(ez, carry):
         def finish(n, value):
-            q_out[jnp.maximum(ez - 2, 0), n - 2] = value
+            q32[jnp.maximum(ez - 2, 0), (n - 2) * CH : (n - 1) * CH, :] = value
 
         layer(sh, sl, s32, ez, 1, 10, finish)
         return carry
 
     lax.fori_loop(1, 10, second_pass, 0)
+    store_q = pltpu.make_async_copy(q32, q_hbm, sems.at[1])
+    store_q.start()
 
     gram_ref[...] = jnp.zeros_like(gram_ref)
 
@@ -297,8 +301,7 @@
         for y in range(8):
             r_row = field[z, y]
             s_row = s32[z + 2, (y + 2) * CH : (y + 3) * CH, :]
-            q_row = q_out[z, y]
-            s_out[z, y] = s_row
+            q_row = q32[z, y * CH : (y + 1) * CH, :]
             for k in range(3):
                 for h in range(2):
                     r, s, q = (t[k * 8 : (k + 1) * 8, h * 128 : (h + 1) * 128] for t in (r_row, s_row, q_row))
@@ -323,15 +326,18 @@
     for h in range(2):
         line = jnp.sum(packed[h], axis=0, keepdims=True)
         gram_out[:, :, h * 128 : (h + 1) * 128] = jnp.broadcast_to(line[None], (gram_out.shape[0], 1, 128))
+    store_s.wait()
+    store_q.wait()
 
 
 def operator(flags, fields, mask, k_both, k_high, devices):
-    node = jax.ShapeDtypeStruct((8, 8, CH, 256), F32)
+    node = jax.ShapeDtypeStruct((8, 8 * CH, 256), F32)
+    far = pl.BlockSpec(memory_space=pl.ANY)
     return pl.pallas_call(
         operator_kernel,
         out_shape=[node, node, jax.ShapeDtypeStruct((devices, 1, 256), F32)],
         in_specs=[smem()] + [vmem()] * 10,
-        out_specs=[vmem()] * 3,
+        out_specs=[far, far, vmem()],
         scratch_shapes=[
             pltpu.VMEM((12, 12 * CH, 256), F32),
             pltpu.VMEM((12, 12 * 48, 256), BF16),
@@ -339,8 +345,10 @@
             pltpu.VMEM((11, 11 * CH, 256), F32),
             pltpu.VMEM((11, 11 * 48, 256), BF16),
             pltpu.VMEM((11, 11 * 48, 256), BF16),
+            pltpu.VMEM((8, 8 * CH, 256), F32),
             pltpu.VMEM((11, 48, 256), F32),
             pltpu.VMEM((20, 8, 128), F32),
+            pltpu.SemaphoreType.DMA((2,)),
         ],
         compiler_params=pltpu.CompilerParams(vmem_limit_bytes=VMEM_LIMIT),
         name="operator",
@@ -451,7 +459,8 @@
 
         for y in range(8):
             r = r_ref[z, y]
-            stack = jnp.concatenate([r, s_ref[z, y], q_ref[z, y]], axis=0)
+            at_y = slice(y * CH, (y + 1) * CH)
+            stack = jnp.concatenate([r, s_ref[z, at_y, :], q_ref[z, at_y, :]], axis=0)
             top = stack.astype(BF16)
             rest = (stack - top.astype(F32)).astype(BF16)
             both = jnp.dot(
@@ -486,7 +495,8 @@
         out_shape=[out, out],
         in_specs=[vmem()] + [far] * 3,
         out_specs=[far] * 2,
-        scratch_shapes=[pltpu.VMEM((8, 8, CH, 256), F32)] * 3
+        scratch_shapes=[pltpu.VMEM((8, 8, CH, 256), F32)]
+        + [pltpu.VMEM((8, 8 * CH, 256), F32)] * 2
         + [pltpu.VMEM((8, 2, CH * 8, 128), F32)] * 2
         + [pltpu.SemaphoreType.DMA((3, 8)), pltpu.SemaphoreType.DMA((2, 8, 2))],
         compiler_params=pltpu.CompilerParams(vmem_limit_bytes=VMEM_LIMIT),

time: 198 us -> 195 us (0.985)
  blocking collectives: 41.4 us -> 39.4 us
where the time goes in v4:
time: 195 us; the launch traced here: 196 us
  Pallas kernels  66.7 us (34%)
  starting transfers between devices  55.8 us (29%)
  blocking collectives  39.4 us (20%)
  waiting for transfers between devices  29.3 us (15%)
  other arithmetic  2.26 us (1%)
    ppermute x10, starting transfers between devices, moved(): lax.ppermute(value, axis, [(i, i + step) for i in range(count) if 0 <= i...  43.9 us
    all_to_all x1, blocking collectives, exchange(): return lax.all_to_all(value, AXES, split_axis=0, concat_axis=0, tiled=True)  39.4 us
    pallas_call x1, Pallas kernels, operator(): pl.pallas_call(operator_kernel, out_shape=[node, node, jax.ShapeDtypeStru...  29.9 us
    pallas_call x1, Pallas kernels, scatter(): pl.pallas_call(scatter_kernel, out_shape=[shape(8, 8), shape(2, 8), shape...  24.2 us
    ppermute x10, waiting for transfers between devices, moved(): lax.ppermute(value, axis, [(i, i + step) for i in range(count) if 0 <= i...  24.1 us
    all_to_all x1, starting transfers between devices, exchange(): return lax.all_to_all(value, AXES, split_axis=0, concat_axis=0, tiled=True)  11.9 us
    pallas_call x1, Pallas kernels, final(): pl.pallas_call(final_kernel, out_shape=[out, out], in_specs=[vmem()] + [f...  7.01 us
    pallas_call x1, Pallas kernels, pack(): pl.pallas_call(pack_kernel, out_shape=jax.ShapeDtypeStruct((devices, 2 *...  5.59 us
  transfers between devices with their start and end apart: 11, of which 6 were waited for; matrix products, arithmetic and copies ran while one was open for 2% of the time, Pallas kernels for 0%

profile of v4, /device:TPU:1, one launch (start us, length us, event | category | flops | bytes accessed | tf_op | source)
XLA Modules:
  0.0 195.8 jit_solution(5541928084608833726)
XLA Ops:
  0.6 5.6 %pack.1 = f32[128,56,128]{2,1,0:T(8,128)} custom-call(s32[128]{0:T(128)} %owner_ref.1, s32[1,128]{1,0:T(1,128)} %bitcast.10, s32[8,128]{1,0:T(8,128)} %bitcast.9, s32[128,128]{1,0:T(8,128)} %voxel_ref.1, f32[128,24,128]{2,1,0:T(8,128)} %force_hbm.1), custom_call_target="tpu_custom_call" | custom-call | tf_op jit(solution)/shard_map/pack/pallas_call | solution.py:66
  6.2 11.9 %all-to-all-start = ((f32[128,56,128]{2,1,0:T(8,128)}), f32[128,56,128]{2,1,0:T(8,128)}, u32[]{:S(2)}, u32[]{:S(2)}) async-start(f32[128,56,128]{2,1,0:T(8,128)} %pack.1), calls=%async_computation | async-start | bytes 7340032 | tf_op jit(solution)/shard_map/all_to_all | solution.py:515
  18.2 1.3 collective-permute-start.1
  19.5 4.0 %collective-permute-start = (s32[2,8,256]{2,1,0:T(8,128)S(1)}, s32[2,8,256]{2,1,0:T(8,128)S(1)}, u32[]{:S(2)}, u32[]{:S(2)}) collective-permute-start(s32[2,8,256]{2,1,0:T(8,128)S(1)} %slice.24), channel_id=1, source_target_pairs={{0,8},{8,16},{16,24},{24,32},{32,40},{40,48},{48,56},{56,64},{64,7... | collective-permute-start | bytes 49160 | tf_op jit(solution)/shard_map/ppermute | solution.py:509
  23.8 0.7 reshape.14
  24.5 0.7 pad_maximum_fusion.k_both
  25.2 18.1 %collective-permute-start.3 = (s32[11,1,256]{2,1,0:T(1,128)S(1)}, s32[11,1,256]{2,1,0:T(1,128)S(1)}, u32[]{:S(2)}, u32[]{:S(2)}) collective-permute-start(s32[11,1,256]{2,1,0:T(1,128)S(1)} %slice.33), channel_id=1, source_target_pairs={{1,0},{2,1},{3,2},{4,3},{5,4},{6,5},{7,6},{9,8},{10,9},{11,10},{12... | collective-permute-start | bytes 33800 | tf_op jit(solution)/shard_map/ppermute | solution.py:509
  43.4 1.9 collective-permute-start.2
  45.9 13.4 %collective-permute-done.3 = s32[11,1,256]{2,1,0:T(1,128)S(1)} collective-permute-done((s32[11,1,256]{2,1,0:T(1,128)S(1)}, s32[11,1,256]{2,1,0:T(1,128)S(1)}, u32[]{:S(2)}, u32[]{:S(2)}) %collective-permute-start.3) | collective-permute-done | bytes 11296 | tf_op jit(solution)/shard_map/ppermute | solution.py:509
  59.2 0.7 add_convert_fusion.mask_ref
  60.0 5.2 %all-to-all-done = f32[128,56,128]{2,1,0:T(8,128)} async-done(((f32[128,56,128]{2,1,0:T(8,128)}), f32[128,56,128]{2,1,0:T(8,128)}, u32[]{:S(2)}, u32[]{:S(2)}) %all-to-all-start) | async-done | bytes 3670048 | tf_op jit(solution)/shard_map/all_to_all | solution.py:515
  65.2 24.2 %scatter.1 = (f32[8,8,24,256]{3,2,1,0:T(8,128)}, f32[2,8,24,256]{3,2,1,0:T(8,128)}, f32[2,8,24,256]{3,2,1,0:T(8,128)}, f32[8,2,24,256]{3,2,1,0:T(8,128)}, f32[8,2,24,256]{3,2,1,0:T(8,128)}) custom-call(f32[7168,128]{1,0:T(8,128)} %bitcast.5.recv_ref), custom_call_target="tpu_custom_call" | custom-call | tf_op jit(solution)/shard_map/scatter/pallas_call | solution.py:188
  89.4 8.6 %collective-permute-start.4 = (f32[2,8,24,256]{3,2,1,0:T(8,128)}, f32[2,8,24,256]{3,2,1,0:T(8,128)S(1)}, u32[]{:S(2)}, u32[]{:S(2)}) collective-permute-start(f32[2,8,24,256]{3,2,1,0:T(8,128)} %get-tuple-element.22), channel_id=1, source_target_pairs={{0,8},{8,16},{16,24},{24,32},{32,40},{40,48},{48,56},{56,64},{64,7... | collective-permute-start | bytes 1179656 | tf_op jit(solution)/shard_map/ppermute | solution.py:509
  98.0 1.3 collective-permute-start.5
  99.3 1.9 collective-permute-start.6
  101.2 2.4 %collective-permute-start.7 = (f32[8,2,24,256]{3,2,1,0:T(8,128)}, f32[8,2,24,256]{3,2,1,0:T(8,128)S(1)}, u32[]{:S(2)}, u32[]{:S(2)}) collective-permute-start(f32[8,2,24,256]{3,2,1,0:T(8,128)} %get-tuple-element.25), channel_id=1, source_target_pairs={{1,0},{2,1},{3,2},{4,3},{5,4},{6,5},{7,6},{9,8},{10,9},{11,10},{12... | collective-permute-start | bytes 1179656 | tf_op jit(solution)/shard_map/ppermute | solution.py:509
  103.6 2.2 %collective-permute-done.4.z_low = f32[2,8,24,256]{3,2,1,0:T(8,128)S(1)} collective-permute-done((f32[2,8,24,256]{3,2,1,0:T(8,128)}, f32[2,8,24,256]{3,2,1,0:T(8,128)S(1)}, u32[]{:S(2)}, u32[]{:S(2)}) %collective-permute-start.4) | collective-permute-done | bytes 393248 | tf_op jit(solution)/shard_map/ppermute | solution.py:509
  105.9 4.0 %collective-permute-done.5.z_high = f32[2,8,24,256]{3,2,1,0:T(8,128)S(1)} collective-permute-done((f32[2,8,24,256]{3,2,1,0:T(8,128)}, f32[2,8,24,256]{3,2,1,0:T(8,128)S(1)}, u32[]{:S(2)}, u32[]{:S(2)}) %collective-permute-start.5) | collective-permute-done | bytes 393248 | tf_op jit(solution)/shard_map/ppermute | solution.py:509
  109.9 1.9 collective-permute-start.8
  111.9 2.4 %collective-permute-start.9 = (f32[4,2,24,256]{3,2,1,0:T(8,128)S(1)}, f32[4,2,24,256]{3,2,1,0:T(8,128)S(1)}, u32[]{:S(2)}, u32[]{:S(2)}) collective-permute-start(f32[4,2,24,256]{3,2,1,0:T(8,128)S(1)} %pad_maximum_fusion.2), channel_id=1, source_target_pairs={{1,0},{2,1},{3,2},{4,3},{5,4},{6,5},{7,6},{9,8},{10,9},{11,10},{12... | collective-permute-start | bytes 589832 | tf_op jit(solution)/shard_map/ppermute | solution.py:509
  114.4 4.4 %collective-permute-done.9.c_high = f32[4,2,24,256]{3,2,1,0:T(8,128)S(1)} collective-permute-done((f32[4,2,24,256]{3,2,1,0:T(8,128)S(1)}, f32[4,2,24,256]{3,2,1,0:T(8,128)S(1)}, u32[]{:S(2)}, u32[]{:S(2)}) %collective-permute-start.9) | collective-permute-done | bytes 196640 | tf_op jit(solution)/shard_map/ppermute | solution.py:509
  119.5 29.9 %operator.1 = (f32[8,192,256]{2,1,0:T(8,128)}, f32[8,192,256]{2,1,0:T(8,128)}, f32[128,1,256]{2,1,0:T(1,128)}) custom-call(f32[2]{0:T(128)} %add_convert_fusion.1.flag_ref, f32[8,8,24,256]{3,2,1,0:T(8,128)} %get-tuple-element.21.field.r_hbm, f32[2,8,24,256]{3,2,1,0:T(8,128)} %copy-done, f32[2,8,24,256]{3,2,1,0:T(8,128)} %copy-done.1, ...), custom_call_target="tpu_custom_call" | custom-call | tf_op jit(solution)/shard_map/operator/pallas_call | solution.py:336
  149.4 39.4 %all_to_all.10.gram_ref = f32[128,1,256]{2,1,0:T(1,128)} all-to-all(f32[128,1,256]{2,1,0:T(1,128)} %get-tuple-element.29), channel_id=1, replica_groups=mesh['gz'=16,'gy'=8] {'gz','gy'}, dimensions={0} | all-to-all | bytes 262144 | tf_op jit(solution)/shard_map/all_to_all | solution.py:515
  188.8 7.0 %final.1 = (f32[24,8,8,256]{3,2,1,0:T(8,128)}, f32[24,8,8,256]{3,2,1,0:T(8,128)}) custom-call(f32[128,1,256]{2,1,0:T(1,128)} %all_to_all.10.gram_ref, f32[8,8,24,256]{3,2,1,0:T(8,128)} %get-tuple-element.21.field.r_hbm, f32[8,192,256]{2,1,0:T(8,128)} %get-tuple-element.30.s_hbm, f32[8,192,256]{2,1,0:T(8,128)} %get-tuple-element.31.q_hbm), custom_call_target="tpu_custom_call" | custom-call | tf_op jit(solution)/shard_map/final/pallas_call | solution.py:493
  (39 shorter events, 1.7 us)
Async XLA Ops:
  6.2 11.9 %copy-start.7 = (s32[8,8,256]{2,1,0:T(8,128)S(1)}, s32[8,8,256]{2,1,0:T(8,128)}, u32[]{:S(2)}) copy-start(s32[8,8,256]{2,1,0:T(8,128)} %param.10) | copy-start | bytes 196612
  6.2 17.3 %copy-start.8 = (f32[24,24]{1,0:T(8,128)S(1)}, f32[24,24]{1,0:T(8,128)}, u32[]{:S(2)}) copy-start(f32[24,24]{1,0:T(8,128)} %param.11) | copy-start | bytes 6916
  6.2 58.9 %all-to-all-start = ((f32[128,56,128]{2,1,0:T(8,128)}), f32[128,56,128]{2,1,0:T(8,128)}, u32[]{:S(2)}, u32[]{:S(2)}) async-start(f32[128,56,128]{2,1,0:T(8,128)} %pack.1), calls=%async_computation | async-start | bytes 7340032 | tf_op jit(solution)/shard_map/all_to_all | solution.py:515
  18.2 7.0 %collective-permute-start.1 = (s32[1,8,256]{2,1,0:T(8,128)S(1)}, s32[1,8,256]{2,1,0:T(8,128)S(1)}, u32[]{:S(2)}, u32[]{:S(2)}) collective-permute-start(s32[1,8,256]{2,1,0:T(8,128)S(1)} %slice.25), channel_id=1, source_target_pairs={{8,0},{16,8},{24,16},{32,24},{40,32},{48,40},{56,48},{64,56},{72,6... | collective-permute-start | bytes 24584 | tf_op jit(solution)/shard_map/ppermute | solution.py:509
  19.5 5.7 %collective-permute-start = (s32[2,8,256]{2,1,0:T(8,128)S(1)}, s32[2,8,256]{2,1,0:T(8,128)S(1)}, u32[]{:S(2)}, u32[]{:S(2)}) collective-permute-start(s32[2,8,256]{2,1,0:T(8,128)S(1)} %slice.24), channel_id=1, source_target_pairs={{0,8},{8,16},{16,24},{24,32},{32,40},{40,48},{48,56},{56,64},{64,7... | collective-permute-start | bytes 49160 | tf_op jit(solution)/shard_map/ppermute | solution.py:509
  24.5 81.4 %copy-start.2 = (bf16[192,192]{1,0:T(8,128)(2,1)}, bf16[192,192]{1,0:T(8,128)(2,1)S(1)}, u32[]{:S(2)}) copy-start(bf16[192,192]{1,0:T(8,128)(2,1)S(1)} %get-tuple-element.28.k_high) | copy-start | bytes 221188
  25.2 34.0 %collective-permute-start.3 = (s32[11,1,256]{2,1,0:T(1,128)S(1)}, s32[11,1,256]{2,1,0:T(1,128)S(1)}, u32[]{:S(2)}, u32[]{:S(2)}) collective-permute-start(s32[11,1,256]{2,1,0:T(1,128)S(1)} %slice.33), channel_id=1, source_target_pairs={{1,0},{2,1},{3,2},{4,3},{5,4},{6,5},{7,6},{9,8},{10,9},{11,10},{12... | collective-permute-start | bytes 33800 | tf_op jit(solution)/shard_map/ppermute | solution.py:509
  43.4 15.9 %collective-permute-start.2 = (s32[11,2,256]{2,1,0:T(2,128)S(1)}, s32[11,2,256]{2,1,0:T(2,128)S(1)}, u32[]{:S(2)}, u32[]{:S(2)}) collective-permute-start(s32[11,2,256]{2,1,0:T(2,128)S(1)} %slice.32), channel_id=1, source_target_pairs={{0,1},{1,2},{2,3},{3,4},{4,5},{5,6},{6,7},{8,9},{9,10},{10,11},{11... | collective-permute-start | bytes 67592 | tf_op jit(solution)/shard_map/ppermute | solution.py:509
  89.4 16.5 %collective-permute-start.4 = (f32[2,8,24,256]{3,2,1,0:T(8,128)}, f32[2,8,24,256]{3,2,1,0:T(8,128)S(1)}, u32[]{:S(2)}, u32[]{:S(2)}) collective-permute-start(f32[2,8,24,256]{3,2,1,0:T(8,128)} %get-tuple-element.22), channel_id=1, source_target_pairs={{0,8},{8,16},{16,24},{24,32},{32,40},{40,48},{48,56},{56,64},{64,7... | collective-permute-start | bytes 1179656 | tf_op jit(solution)/shard_map/ppermute | solution.py:509
  98.0 11.9 %collective-permute-start.5 = (f32[2,8,24,256]{3,2,1,0:T(8,128)}, f32[2,8,24,256]{3,2,1,0:T(8,128)S(1)}, u32[]{:S(2)}, u32[]{:S(2)}) collective-permute-start(f32[2,8,24,256]{3,2,1,0:T(8,128)} %get-tuple-element.23), channel_id=1, source_target_pairs={{8,0},{16,8},{24,16},{32,24},{40,32},{48,40},{56,48},{64,56},{72,6... | collective-permute-start | bytes 1179656 | tf_op jit(solution)/shard_map/ppermute | solution.py:509
  99.3 15.0 %collective-permute-start.6 = (f32[8,2,24,256]{3,2,1,0:T(8,128)}, f32[8,2,24,256]{3,2,1,0:T(8,128)S(1)}, u32[]{:S(2)}, u32[]{:S(2)}) collective-permute-start(f32[8,2,24,256]{3,2,1,0:T(8,128)} %get-tuple-element.24), channel_id=1, source_target_pairs={{0,1},{1,2},{2,3},{3,4},{4,5},{5,6},{6,7},{8,9},{9,10},{10,11},{11... | collective-permute-start | bytes 1179656 | tf_op jit(solution)/shard_map/ppermute | solution.py:509
  101.2 13.1 %collective-permute-start.7 = (f32[8,2,24,256]{3,2,1,0:T(8,128)}, f32[8,2,24,256]{3,2,1,0:T(8,128)S(1)}, u32[]{:S(2)}, u32[]{:S(2)}) collective-permute-start(f32[8,2,24,256]{3,2,1,0:T(8,128)} %get-tuple-element.25), channel_id=1, source_target_pairs={{1,0},{2,1},{3,2},{4,3},{5,4},{6,5},{7,6},{9,8},{10,9},{11,10},{12... | collective-permute-start | bytes 1179656 | tf_op jit(solution)/shard_map/ppermute | solution.py:509
  105.9 13.0 %copy-start = (f32[2,8,24,256]{3,2,1,0:T(8,128)}, f32[2,8,24,256]{3,2,1,0:T(8,128)S(1)}, u32[]{:S(2)}) copy-start(f32[2,8,24,256]{3,2,1,0:T(8,128)S(1)} %collective-permute-done.4.z_low) | copy-start | bytes 1179652
  109.9 9.0 %copy-start.1 = (f32[2,8,24,256]{3,2,1,0:T(8,128)}, f32[2,8,24,256]{3,2,1,0:T(8,128)S(1)}, u32[]{:S(2)}) copy-start(f32[2,8,24,256]{3,2,1,0:T(8,128)S(1)} %collective-permute-done.5.z_high) | copy-start | bytes 1179652
  109.9 4.5 %collective-permute-start.8 = (f32[4,2,24,256]{3,2,1,0:T(8,128)S(1)}, f32[4,2,24,256]{3,2,1,0:T(8,128)S(1)}, u32[]{:S(2)}, u32[]{:S(2)}) collective-permute-start(f32[4,2,24,256]{3,2,1,0:T(8,128)S(1)} %pad_maximum_fusion.1), channel_id=1, source_target_pairs={{0,1},{1,2},{2,3},{3,4},{4,5},{5,6},{6,7},{8,9},{9,10},{10,11},{11... | collective-permute-start | bytes 589832 | tf_op jit(solution)/shard_map/ppermute | solution.py:509
  111.9 7.0 %collective-permute-start.9 = (f32[4,2,24,256]{3,2,1,0:T(8,128)S(1)}, f32[4,2,24,256]{3,2,1,0:T(8,128)S(1)}, u32[]{:S(2)}, u32[]{:S(2)}) collective-permute-start(f32[4,2,24,256]{3,2,1,0:T(8,128)S(1)} %pad_maximum_fusion.2), channel_id=1, source_target_pairs={{1,0},{2,1},{3,2},{4,3},{5,4},{6,5},{7,6},{9,8},{10,9},{11,10},{12... | collective-permute-start | bytes 589832 | tf_op jit(solution)/shard_map/ppermute | solution.py:509
  114.3 4.6 %copy-start.3 = (f32[8,2,24,256]{3,2,1,0:T(8,128)}, f32[8,2,24,256]{3,2,1,0:T(8,128)S(1)}, u32[]{:S(2)}) copy-start(f32[8,2,24,256]{3,2,1,0:T(8,128)S(1)} %collective-permute-done.6.y_low) | copy-start | bytes 1179652
  114.3 4.6 %copy-start.4 = (f32[8,2,24,256]{3,2,1,0:T(8,128)}, f32[8,2,24,256]{3,2,1,0:T(8,128)S(1)}, u32[]{:S(2)}) copy-start(f32[8,2,24,256]{3,2,1,0:T(8,128)S(1)} %collective-permute-done.7.y_high) | copy-start | bytes 1179652
  114.4 4.4 %copy-start.5 = (f32[4,2,24,256]{3,2,1,0:T(8,128)}, f32[4,2,24,256]{3,2,1,0:T(8,128)S(1)}, u32[]{:S(2)}) copy-start(f32[4,2,24,256]{3,2,1,0:T(8,128)S(1)} %collective-permute-done.8.c_low) | copy-start | bytes 589828
  118.9 0.7 copy-start.6

commit v5 on v4

--- a/solution.py
+++ b/solution.py
@@ -40,7 +40,7 @@
     ranks.start()
 
     def clear(i, carry):
-        out_ref[i, 2 * CH : 2 * CH + 8, :] = jnp.full((8, 128), -1.0, F32)
+        out_ref[i, CH] = jnp.full((2, 128), -1.0, F32)
         return carry
 
     lax.fori_loop(0, devices, clear, 0, unroll=8)
@@ -54,9 +54,10 @@
         limit = jnp.sum(jnp.where(lane == p, live, 0.0), axis=1, keepdims=True)
         keep = lane.astype(F32) < limit
         for k in range(0, CH, 8):
-            base = pl.multiple_of(rank * CH + k, 8)
-            out_ref[owner, pl.ds(base, 8), :] = jnp.where(keep, force_ref[p, k : k + 8, :], 0.0)
-        out_ref[owner, pl.ds(2 * CH + rank, 1), :] = voxel_ref[pl.ds(p, 1), :].astype(F32)
+            part = jnp.where(keep, force_ref[p, k : k + 8, :], 0.0)
+            for i in range(4):
+                out_ref[owner, rank * (CH // 2) + k // 2 + i] = part[2 * i : 2 * i + 2, :]
+        out_ref[owner, CH, pl.ds(rank, 1), :] = voxel_ref[pl.ds(p, 1), :].astype(F32)
         return carry
 
     lax.fori_loop(0, blocks, one, 0, unroll=8)
@@ -65,7 +66,7 @@
 def pack(owner, live, voxel, force, devices):
     return pl.pallas_call(
         pack_kernel,
-        out_shape=jax.ShapeDtypeStruct((devices, 2 * CH + 8, 128), F32),
+        out_shape=jax.ShapeDtypeStruct((devices, CH + 1, 2, 128), F32),
         in_specs=[smem(), vmem(), vmem(), vmem(), pl.BlockSpec(memory_space=pl.ANY)],
         out_specs=vmem(),
         scratch_shapes=[
@@ -128,13 +129,19 @@
     recv_ref, field, z_low, z_high, y_low, y_high,
     list_ref, ids_ref, flag_v, flag_s, acc_ref, sem,
 ):
-    rows = 2 * CH + 8
     lane = lax.broadcasted_iota(jnp.int32, (8, 128), 1)
+
+    def voxels(i, carry):
+        pair = recv_ref[i, CH].astype(jnp.int32)
+        for rank in range(2):
+            ids_ref[rank, pl.ds(i, 1), :] = pair[rank : rank + 1, :]
+        return carry
+
+    lax.fori_loop(0, recv_ref.shape[0], voxels, 0, unroll=8)
     for rank in range(2):
         flags = jnp.zeros((8, 128), jnp.int32)
         for t in range(16):
-            ids = recv_ref[pl.ds(t * 8 * rows + 2 * CH + rank, 8, stride=rows), :].astype(jnp.int32)
-            ids_ref[rank, t * 8 : (t + 1) * 8, :] = ids
+            ids = ids_ref[rank, t * 8 : (t + 1) * 8, :]
             flags = jnp.where(lane == t, jnp.where(ids[:, 0:1] >= 0, 1, 0), flags)
         flag_v[rank * 8 : (rank + 1) * 8, :] = flags
     copy = pltpu.make_async_copy(flag_v, flag_s, sem)
@@ -154,7 +161,8 @@
         count = lax.fori_loop(0, 16, collect, count)
 
     def value_of(source, rank):
-        return recv_ref[pl.ds(pl.multiple_of(source * rows + rank * CH, 8), CH), :]
+        half = CH // 2
+        return jnp.concatenate([recv_ref[source, rank * half + i] for i in range(half)], axis=0)
 
     add_blocks(count, list_ref, ids_ref, value_of, acc_ref)
     for z in range(8):
@@ -200,7 +208,7 @@
         ],
         compiler_params=pltpu.CompilerParams(vmem_limit_bytes=VMEM_LIMIT),
         name="scatter",
-    )(recv.reshape(-1, 128))
+    )(recv)
 
 
 def shift_down(v, lane):

time: 195 us -> 192 us (0.985); the launches traced: 196 us -> 191 us
  starting transfers between devices: 55.8 us -> 42.9 us
  local copies, waits for them, and re-layouts: 1.42 us -> 5.33 us
  other arithmetic: 2.26 us -> 4.68 us
    ppermute x10, starting transfers between devices: 43.9 us -> 31.4 us  [moved(): lax.ppermute(value, axis, [(i, i + step) for i in range(count) if 0 <= i...]
    reshape x1, local copies, waits for them, and re-layouts: 0.67 us -> 2.93 us  [body(): jnp.einsum('ij,lm->iljm', element_matrix, jnp.eye(LOADS, dtype=F32))]
  transfers between devices with their start and end apart: 11 -> 11, of which waited for: 6 -> 6; matrix products, arithmetic and copies ran while one was open for 2% -> 4% of each run, Pallas kernels for 0% -> 0%
where the time goes in v5:
time: 192 us; the launch traced here: 191 us
  Pallas kernels  68.3 us (36%)
  starting transfers between devices  42.9 us (22%)
  blocking collectives  39.1 us (20%)
  waiting for transfers between devices  29.3 us (15%)
  local copies, waits for them, and re-layouts  5.33 us (3%)
  other arithmetic  4.68 us (2%)
    all_to_all x1, blocking collectives, exchange(): return lax.all_to_all(value, AXES, split_axis=0, concat_axis=0, tiled=True)  39.1 us
    ppermute x10, starting transfers between devices, moved(): lax.ppermute(value, axis, [(i, i + step) for i in range(count) if 0 <= i...  31.4 us
    pallas_call x1, Pallas kernels, operator(): pl.pallas_call(operator_kernel, out_shape=[node, node, jax.ShapeDtypeStru...  29.9 us
    pallas_call x1, Pallas kernels, scatter(): pl.pallas_call(scatter_kernel, out_shape=[shape(8, 8), shape(2, 8), shape...  26 us
    ppermute x10, waiting for transfers between devices, moved(): lax.ppermute(value, axis, [(i, i + step) for i in range(count) if 0 <= i...  24.1 us
    all_to_all x1, starting transfers between devices, exchange(): return lax.all_to_all(value, AXES, split_axis=0, concat_axis=0, tiled=True)  11.5 us
    pallas_call x1, Pallas kernels, final(): pl.pallas_call(final_kernel, out_shape=[out, out], in_specs=[vmem()] + [f...  7.02 us
    pallas_call x1, Pallas kernels, pack(): pl.pallas_call(pack_kernel, out_shape=jax.ShapeDtypeStruct((devices, CH +...  5.43 us
  transfers between devices with their start and end apart: 11, of which 6 were waited for; matrix products, arithmetic and copies ran while one was open for 4% of the time, Pallas kernels for 0%

profile of v5, /device:TPU:1, one launch (start us, length us, event | category | flops | bytes accessed | tf_op | source)
XLA Modules:
  0.0 190.6 jit_solution(10180969591327911858)
XLA Ops:
  0.6 5.4 %pack.1 = f32[128,25,2,128]{3,2,1,0:T(2,128)} custom-call(s32[128]{0:T(128)} %owner_ref.1, s32[1,128]{1,0:T(1,128)} %bitcast.9, s32[8,128]{1,0:T(8,128)} %bitcast.8, s32[128,128]{1,0:T(8,128)} %voxel_ref.1, f32[128,24,128]{2,1,0:T(8,128)} %force_hbm.1), custom_call_target="tpu_custom_call" | custom-call | tf_op jit(solution)/shard_map/pack/pallas_call | solution.py:67
  6.1 11.5 %all-to-all-start = ((f32[128,25,2,128]{3,2,1,0:T(2,128)}), f32[128,25,2,128]{3,2,1,0:T(2,128)S(1)}, u32[]{:S(2)}, u32[]{:S(2)}) async-start(f32[128,25,2,128]{3,2,1,0:T(2,128)} %pack.1), calls=%async_computation | async-start | bytes 6553600 | tf_op jit(solution)/shard_map/all_to_all | solution.py:523
  17.6 1.3 collective-permute-start.1
  18.9 4.0 %collective-permute-start = (s32[2,8,256]{2,1,0:T(8,128)S(1)}, s32[2,8,256]{2,1,0:T(8,128)S(1)}, u32[]{:S(2)}, u32[]{:S(2)}) collective-permute-start(s32[2,8,256]{2,1,0:T(8,128)S(1)} %slice.24), channel_id=1, source_target_pairs={{0,8},{8,16},{16,24},{24,32},{32,40},{40,48},{48,56},{56,64},{64,7... | collective-permute-start | bytes 49160 | tf_op jit(solution)/shard_map/ppermute | solution.py:517
  23.0 1.6 multiply_bitcast_fusion
  24.6 2.9 %reshape.11 = f32[192,192]{1,0:T(8,128)} reshape(f32[24,8,24,8]{3,2,1,0:T(8,128)} %multiply_bitcast_fusion) | data formatting | bytes 294912 | tf_op jit(solution)/shard_map/reshape | solution.py:537
  29.3 11.3 %collective-permute-start.3 = (s32[11,1,256]{2,1,0:T(1,128)S(1)}, s32[11,1,256]{2,1,0:T(1,128)S(1)}, u32[]{:S(2)}, u32[]{:S(2)}) collective-permute-start(s32[11,1,256]{2,1,0:T(1,128)S(1)} %slice.33), channel_id=1, source_target_pairs={{1,0},{2,1},{3,2},{4,3},{5,4},{6,5},{7,6},{9,8},{10,9},{11,10},{12... | collective-permute-start | bytes 33800 | tf_op jit(solution)/shard_map/ppermute | solution.py:517
  40.6 1.9 %collective-permute-start.2 = (s32[11,2,256]{2,1,0:T(2,128)S(1)}, s32[11,2,256]{2,1,0:T(2,128)S(1)}, u32[]{:S(2)}, u32[]{:S(2)}) collective-permute-start(s32[11,2,256]{2,1,0:T(2,128)S(1)} %slice.32), channel_id=1, source_target_pairs={{0,1},{1,2},{2,3},{3,4},{4,5},{5,6},{6,7},{8,9},{9,10},{10,11},{11... | collective-permute-start | bytes 67592 | tf_op jit(solution)/shard_map/ppermute | solution.py:517
  43.1 11.6 %collective-permute-done.3 = s32[11,1,256]{2,1,0:T(1,128)S(1)} collective-permute-done((s32[11,1,256]{2,1,0:T(1,128)S(1)}, s32[11,1,256]{2,1,0:T(1,128)S(1)}, u32[]{:S(2)}, u32[]{:S(2)}) %collective-permute-start.3) | collective-permute-done | bytes 11296 | tf_op jit(solution)/shard_map/ppermute | solution.py:517
  55.5 5.1 %all-to-all-done.recv_ref = f32[128,25,2,128]{3,2,1,0:T(2,128)S(1)} async-done(((f32[128,25,2,128]{3,2,1,0:T(2,128)}), f32[128,25,2,128]{3,2,1,0:T(2,128)S(1)}, u32[]{:S(2)}, u32[]{:S(2)}) %all-to-all-start) | async-done | bytes 3276832 | tf_op jit(solution)/shard_map/all_to_all | solution.py:523
  60.6 1.7 copy-done
  62.3 26.0 %scatter.1 = (f32[8,8,24,256]{3,2,1,0:T(8,128)}, f32[2,8,24,256]{3,2,1,0:T(8,128)}, f32[2,8,24,256]{3,2,1,0:T(8,128)}, f32[8,2,24,256]{3,2,1,0:T(8,128)}, f32[8,2,24,256]{3,2,1,0:T(8,128)}) custom-call(f32[128,25,2,128]{3,2,1,0:T(2,128)} %copy-done), custom_call_target="tpu_custom_call" | custom-call | tf_op jit(solution)/shard_map/scatter/pallas_call | solution.py:196
  88.3 2.8 %collective-permute-start.4 = (f32[2,8,24,256]{3,2,1,0:T(8,128)}, f32[2,8,24,256]{3,2,1,0:T(8,128)S(1)}, u32[]{:S(2)}, u32[]{:S(2)}) collective-permute-start(f32[2,8,24,256]{3,2,1,0:T(8,128)} %get-tuple-element.22), channel_id=1, source_target_pairs={{0,8},{8,16},{16,24},{24,32},{32,40},{40,48},{48,56},{56,64},{64,7... | collective-permute-start | bytes 1179656 | tf_op jit(solution)/shard_map/ppermute | solution.py:517
  91.1 1.3 collective-permute-start.5
  92.4 2.6 %collective-permute-start.6 = (f32[8,2,24,256]{3,2,1,0:T(8,128)}, f32[8,2,24,256]{3,2,1,0:T(8,128)S(1)}, u32[]{:S(2)}, u32[]{:S(2)}) collective-permute-start(f32[8,2,24,256]{3,2,1,0:T(8,128)} %get-tuple-element.24), channel_id=1, source_target_pairs={{0,1},{1,2},{2,3},{3,4},{4,5},{5,6},{6,7},{8,9},{9,10},{10,11},{11... | collective-permute-start | bytes 1179656 | tf_op jit(solution)/shard_map/ppermute | solution.py:517
  95.0 1.9 %collective-permute-start.7 = (f32[8,2,24,256]{3,2,1,0:T(8,128)}, f32[8,2,24,256]{3,2,1,0:T(8,128)S(1)}, u32[]{:S(2)}, u32[]{:S(2)}) collective-permute-start(f32[8,2,24,256]{3,2,1,0:T(8,128)} %get-tuple-element.25), channel_id=1, source_target_pairs={{1,0},{2,1},{3,2},{4,3},{5,4},{6,5},{7,6},{9,8},{10,9},{11,10},{12... | collective-permute-start | bytes 1179656 | tf_op jit(solution)/shard_map/ppermute | solution.py:517
  96.9 2.8 %collective-permute-done.4.z_low = f32[2,8,24,256]{3,2,1,0:T(8,128)S(1)} collective-permute-done((f32[2,8,24,256]{3,2,1,0:T(8,128)}, f32[2,8,24,256]{3,2,1,0:T(8,128)S(1)}, u32[]{:S(2)}, u32[]{:S(2)}) %collective-permute-start.4) | collective-permute-done | bytes 393248 | tf_op jit(solution)/shard_map/ppermute | solution.py:517
  99.7 5.2 %collective-permute-done.5.z_high = f32[2,8,24,256]{3,2,1,0:T(8,128)S(1)} collective-permute-done((f32[2,8,24,256]{3,2,1,0:T(8,128)}, f32[2,8,24,256]{3,2,1,0:T(8,128)S(1)}, u32[]{:S(2)}, u32[]{:S(2)}) %collective-permute-start.5) | collective-permute-done | bytes 393248 | tf_op jit(solution)/shard_map/ppermute | solution.py:517
  105.0 1.9 %collective-permute-start.8 = (f32[4,2,24,256]{3,2,1,0:T(8,128)S(1)}, f32[4,2,24,256]{3,2,1,0:T(8,128)S(1)}, u32[]{:S(2)}, u32[]{:S(2)}) collective-permute-start(f32[4,2,24,256]{3,2,1,0:T(8,128)S(1)} %pad_maximum_fusion.1), channel_id=1, source_target_pairs={{0,1},{1,2},{2,3},{3,4},{4,5},{5,6},{6,7},{8,9},{9,10},{10,11},{11... | collective-permute-start | bytes 589832 | tf_op jit(solution)/shard_map/ppermute | solution.py:517
  106.9 2.4 %collective-permute-start.9 = (f32[4,2,24,256]{3,2,1,0:T(8,128)S(1)}, f32[4,2,24,256]{3,2,1,0:T(8,128)S(1)}, u32[]{:S(2)}, u32[]{:S(2)}) collective-permute-start(f32[4,2,24,256]{3,2,1,0:T(8,128)S(1)} %pad_maximum_fusion.2), channel_id=1, source_target_pairs={{1,0},{2,1},{3,2},{4,3},{5,4},{6,5},{7,6},{9,8},{10,9},{11,10},{12... | collective-permute-start | bytes 589832 | tf_op jit(solution)/shard_map/ppermute | solution.py:517
  109.5 4.4 %collective-permute-done.9.c_high = f32[4,2,24,256]{3,2,1,0:T(8,128)S(1)} collective-permute-done((f32[4,2,24,256]{3,2,1,0:T(8,128)S(1)}, f32[4,2,24,256]{3,2,1,0:T(8,128)S(1)}, u32[]{:S(2)}, u32[]{:S(2)}) %collective-permute-start.9) | collective-permute-done | bytes 196640 | tf_op jit(solution)/shard_map/ppermute | solution.py:517
  114.6 29.9 %operator.1 = (f32[8,192,256]{2,1,0:T(8,128)}, f32[8,192,256]{2,1,0:T(8,128)}, f32[128,1,256]{2,1,0:T(1,128)}) custom-call(f32[2]{0:T(128)} %add_convert_fusion.1.flag_ref, f32[8,8,24,256]{3,2,1,0:T(8,128)} %get-tuple-element.21.field.r_hbm, f32[2,8,24,256]{3,2,1,0:T(8,128)} %copy-done.1, f32[2,8,24,256]{3,2,1,0:T(8,128)} %copy-done.2, ...), custom_call_target="tpu_custom_call" | custom-call | tf_op jit(solution)/shard_map/operator/pallas_call | solution.py:344
  144.4 39.1 %all_to_all.10.gram_ref = f32[128,1,256]{2,1,0:T(1,128)} all-to-all(f32[128,1,256]{2,1,0:T(1,128)} %get-tuple-element.29), channel_id=1, replica_groups=mesh['gz'=16,'gy'=8] {'gz','gy'}, dimensions={0} | all-to-all | bytes 262144 | tf_op jit(solution)/shard_map/all_to_all | solution.py:523
  183.6 7.0 %final.1 = (f32[24,8,8,256]{3,2,1,0:T(8,128)}, f32[24,8,8,256]{3,2,1,0:T(8,128)}) custom-call(f32[128,1,256]{2,1,0:T(1,128)} %all_to_all.10.gram_ref, f32[8,8,24,256]{3,2,1,0:T(8,128)} %get-tuple-element.21.field.r_hbm, f32[8,192,256]{2,1,0:T(8,128)} %get-tuple-element.30.s_hbm, f32[8,192,256]{2,1,0:T(8,128)} %get-tuple-element.31.q_hbm), custom_call_target="tpu_custom_call" | custom-call | tf_op jit(solution)/shard_map/final/pallas_call | solution.py:501
  (41 shorter events, 3.9 us)
Async XLA Ops:
  6.1 11.5 %copy-start.8 = (s32[8,8,256]{2,1,0:T(8,128)S(1)}, s32[8,8,256]{2,1,0:T(8,128)}, u32[]{:S(2)}) copy-start(s32[8,8,256]{2,1,0:T(8,128)} %param.10) | copy-start | bytes 196612
  6.1 16.9 %copy-start.9 = (f32[24,24]{1,0:T(8,128)S(1)}, f32[24,24]{1,0:T(8,128)}, u32[]{:S(2)}) copy-start(f32[24,24]{1,0:T(8,128)} %param.11) | copy-start | bytes 6916
  6.1 54.5 %all-to-all-start = ((f32[128,25,2,128]{3,2,1,0:T(2,128)}), f32[128,25,2,128]{3,2,1,0:T(2,128)S(1)}, u32[]{:S(2)}, u32[]{:S(2)}) async-start(f32[128,25,2,128]{3,2,1,0:T(2,128)} %pack.1), calls=%async_computation | async-start | bytes 6553600 | tf_op jit(solution)/shard_map/all_to_all | solution.py:523
  17.6 11.6 %collective-permute-start.1 = (s32[1,8,256]{2,1,0:T(8,128)S(1)}, s32[1,8,256]{2,1,0:T(8,128)S(1)}, u32[]{:S(2)}, u32[]{:S(2)}) collective-permute-start(s32[1,8,256]{2,1,0:T(8,128)S(1)} %slice.25), channel_id=1, source_target_pairs={{8,0},{16,8},{24,16},{32,24},{40,32},{48,40},{56,48},{64,56},{72,6... | collective-permute-start | bytes 24584 | tf_op jit(solution)/shard_map/ppermute | solution.py:517
  18.9 10.3 %collective-permute-start = (s32[2,8,256]{2,1,0:T(8,128)S(1)}, s32[2,8,256]{2,1,0:T(8,128)S(1)}, u32[]{:S(2)}, u32[]{:S(2)}) collective-permute-start(s32[2,8,256]{2,1,0:T(8,128)S(1)} %slice.24), channel_id=1, source_target_pairs={{0,8},{8,16},{16,24},{24,32},{32,40},{40,48},{48,56},{56,64},{64,7... | collective-permute-start | bytes 49160 | tf_op jit(solution)/shard_map/ppermute | solution.py:517
  28.5 76.4 %copy-start.3 = (bf16[192,192]{1,0:T(8,128)(2,1)}, bf16[192,192]{1,0:T(8,128)(2,1)S(1)}, u32[]{:S(2)}) copy-start(bf16[192,192]{1,0:T(8,128)(2,1)S(1)} %get-tuple-element.28.k_high) | copy-start | bytes 221188
  29.3 25.5 %collective-permute-start.3 = (s32[11,1,256]{2,1,0:T(1,128)S(1)}, s32[11,1,256]{2,1,0:T(1,128)S(1)}, u32[]{:S(2)}, u32[]{:S(2)}) collective-permute-start(s32[11,1,256]{2,1,0:T(1,128)S(1)} %slice.33), channel_id=1, source_target_pairs={{1,0},{2,1},{3,2},{4,3},{5,4},{6,5},{7,6},{9,8},{10,9},{11,10},{12... | collective-permute-start | bytes 33800 | tf_op jit(solution)/shard_map/ppermute | solution.py:517
  40.6 14.2 %collective-permute-start.2 = (s32[11,2,256]{2,1,0:T(2,128)S(1)}, s32[11,2,256]{2,1,0:T(2,128)S(1)}, u32[]{:S(2)}, u32[]{:S(2)}) collective-permute-start(s32[11,2,256]{2,1,0:T(2,128)S(1)} %slice.32), channel_id=1, source_target_pairs={{0,1},{1,2},{2,3},{3,4},{4,5},{5,6},{6,7},{8,9},{9,10},{10,11},{11... | collective-permute-start | bytes 67592 | tf_op jit(solution)/shard_map/ppermute | solution.py:517
  60.6 1.7 copy-start
  88.3 11.4 %collective-permute-start.4 = (f32[2,8,24,256]{3,2,1,0:T(8,128)}, f32[2,8,24,256]{3,2,1,0:T(8,128)S(1)}, u32[]{:S(2)}, u32[]{:S(2)}) collective-permute-start(f32[2,8,24,256]{3,2,1,0:T(8,128)} %get-tuple-element.22), channel_id=1, source_target_pairs={{0,8},{8,16},{16,24},{24,32},{32,40},{40,48},{48,56},{56,64},{64,7... | collective-permute-start | bytes 1179656 | tf_op jit(solution)/shard_map/ppermute | solution.py:517
  91.1 13.8 %collective-permute-start.5 = (f32[2,8,24,256]{3,2,1,0:T(8,128)}, f32[2,8,24,256]{3,2,1,0:T(8,128)S(1)}, u32[]{:S(2)}, u32[]{:S(2)}) collective-permute-start(f32[2,8,24,256]{3,2,1,0:T(8,128)} %get-tuple-element.23), channel_id=1, source_target_pairs={{8,0},{16,8},{24,16},{32,24},{40,32},{48,40},{56,48},{64,56},{72,6... | collective-permute-start | bytes 1179656 | tf_op jit(solution)/shard_map/ppermute | solution.py:517
  92.4 17.0 %collective-permute-start.6 = (f32[8,2,24,256]{3,2,1,0:T(8,128)}, f32[8,2,24,256]{3,2,1,0:T(8,128)S(1)}, u32[]{:S(2)}, u32[]{:S(2)}) collective-permute-start(f32[8,2,24,256]{3,2,1,0:T(8,128)} %get-tuple-element.24), channel_id=1, source_target_pairs={{0,1},{1,2},{2,3},{3,4},{4,5},{5,6},{6,7},{8,9},{9,10},{10,11},{11... | collective-permute-start | bytes 1179656 | tf_op jit(solution)/shard_map/ppermute | solution.py:517
  95.0 14.4 %collective-permute-start.7 = (f32[8,2,24,256]{3,2,1,0:T(8,128)}, f32[8,2,24,256]{3,2,1,0:T(8,128)S(1)}, u32[]{:S(2)}, u32[]{:S(2)}) collective-permute-start(f32[8,2,24,256]{3,2,1,0:T(8,128)} %get-tuple-element.25), channel_id=1, source_target_pairs={{1,0},{2,1},{3,2},{4,3},{5,4},{6,5},{7,6},{9,8},{10,9},{11,10},{12... | collective-permute-start | bytes 1179656 | tf_op jit(solution)/shard_map/ppermute | solution.py:517
  99.7 14.2 %copy-start.1 = (f32[2,8,24,256]{3,2,1,0:T(8,128)}, f32[2,8,24,256]{3,2,1,0:T(8,128)S(1)}, u32[]{:S(2)}) copy-start(f32[2,8,24,256]{3,2,1,0:T(8,128)S(1)} %collective-permute-done.4.z_low) | copy-start | bytes 1179652
  104.9 9.0 %copy-start.2 = (f32[2,8,24,256]{3,2,1,0:T(8,128)}, f32[2,8,24,256]{3,2,1,0:T(8,128)S(1)}, u32[]{:S(2)}) copy-start(f32[2,8,24,256]{3,2,1,0:T(8,128)S(1)} %collective-permute-done.5.z_high) | copy-start | bytes 1179652
  105.0 4.5 %collective-permute-start.8 = (f32[4,2,24,256]{3,2,1,0:T(8,128)S(1)}, f32[4,2,24,256]{3,2,1,0:T(8,128)S(1)}, u32[]{:S(2)}, u32[]{:S(2)}) collective-permute-start(f32[4,2,24,256]{3,2,1,0:T(8,128)S(1)} %pad_maximum_fusion.1), channel_id=1, source_target_pairs={{0,1},{1,2},{2,3},{3,4},{4,5},{5,6},{6,7},{8,9},{9,10},{10,11},{11... | collective-permute-start | bytes 589832 | tf_op jit(solution)/shard_map/ppermute | solution.py:517
  106.9 7.0 %collective-permute-start.9 = (f32[4,2,24,256]{3,2,1,0:T(8,128)S(1)}, f32[4,2,24,256]{3,2,1,0:T(8,128)S(1)}, u32[]{:S(2)}, u32[]{:S(2)}) collective-permute-start(f32[4,2,24,256]{3,2,1,0:T(8,128)S(1)} %pad_maximum_fusion.2), channel_id=1, source_target_pairs={{1,0},{2,1},{3,2},{4,3},{5,4},{6,5},{7,6},{9,8},{10,9},{11,10},{12... | collective-permute-start | bytes 589832 | tf_op jit(solution)/shard_map/ppermute | solution.py:517
  109.3 4.6 %copy-start.4 = (f32[8,2,24,256]{3,2,1,0:T(8,128)}, f32[8,2,24,256]{3,2,1,0:T(8,128)S(1)}, u32[]{:S(2)}) copy-start(f32[8,2,24,256]{3,2,1,0:T(8,128)S(1)} %collective-permute-done.6.y_low) | copy-start | bytes 1179652
  109.4 4.6 %copy-start.5 = (f32[8,2,24,256]{3,2,1,0:T(8,128)}, f32[8,2,24,256]{3,2,1,0:T(8,128)S(1)}, u32[]{:S(2)}) copy-start(f32[8,2,24,256]{3,2,1,0:T(8,128)S(1)} %collective-permute-done.7.y_high) | copy-start | bytes 1179652
  109.5 4.4 %copy-start.6 = (f32[4,2,24,256]{3,2,1,0:T(8,128)}, f32[4,2,24,256]{3,2,1,0:T(8,128)S(1)}, u32[]{:S(2)}) copy-start(f32[4,2,24,256]{3,2,1,0:T(8,128)S(1)} %collective-permute-done.8.c_low) | copy-start | bytes 589828
  113.9 0.7 copy-start.7
